TPU v7x, 256 devices: a whole 4x4x8 slice. The times are simulated.
256 devices in a mesh: az: 32 (over z, y_hi, core), dr: 8 (over x, y_lo).
Axes of the slice: x: 4, y: 4 (y_hi: 2, y_lo: 2; y = y_hi * 2 + y_lo), z: 8, core: 2. Of those that a mesh axis runs over, the one named last changes fastest.
Arguments:
- stack: bfloat16 [2, 32, 768, 4096], P(None, 'dr', 'az'), may hold values from -6 to 6
- range_filter: float32 [32, 4096], P('dr'), may hold values from 0.2 to 1.5
- scatter_mask: int32 [768, 4096], P('az'), may hold values 0 or 1
Outputs:
- phase_vector: float32 [2, 32, 192, 1024], P(None, None, 'az', 'dr')
All inputs are finite; a program needn't handle non-finite values. No bound on the sum of `scatter_mask` on one device may be relied on, other than what follows from the above.
Results may differ from a plain program's by a relative error of at most 0.0037.
Values may be sent and summed in bfloat16 or wider, within the bound.
No kernel may reach another device: no remote copies, remote signals or barrier semaphores. Data moves between devices by JAX's collectives and lax.ppermute only.
A program may use at most 64 MiB of HBM per device.

v0:
```python
import math

import jax
import jax.numpy as jnp
import numpy as np
from jax import lax
from jax.experimental import pallas as pl
from jax.experimental.pallas import tpu as pltpu
from jax.sharding import PartitionSpec as P

ITERS = 4
BETA_LOAD = 1.0
PROJ_LOAD = 1.0

DATES = 32
LINES = 24
RG = 4096
TILES = 8
HALO = 6
PLANES = 32
HERE = 4
ROWS = HERE * LINES
SLOTS = LINES + 1
TAIL_SLOT = 18
COMBOS = 80
OFFSETS = (0, 32, 56, 72)


def slot_of(line):
    if line < 6:
        return 12 + line
    return line - 6 if line < 18 else line + 1


def split_np(table):
    high = table.astype(jnp.bfloat16)
    low = (table - high.astype(np.float64)).astype(jnp.bfloat16)
    return np.stack([high, low])


def tables():
    turn = 2.0 * np.pi / 128 * (np.outer(np.arange(128), np.arange(128)) % 128)
    cos, sin = np.cos(turn), np.sin(turn)
    forward = split_np(np.block([[cos, -sin], [sin, cos]]))
    inverse = split_np(np.block([[cos, sin], [-sin, cos]]) / RG)
    angle = 2.0 * np.pi / RG * np.outer(np.arange(PLANES), np.arange(128))
    twist = np.stack([np.cos(angle), np.sin(angle)]).astype(np.float32)
    place = np.zeros((640, 512), np.float32)
    for phase in range(4):
        for block in range(128):
            place[122 + 4 * block + phase, phase * 128 + block] = 1.0
    return forward, inverse, twist, place.astype(jnp.bfloat16)


def tail_band():
    band = np.zeros((6, 128, 128), np.float32)
    for row in range(6):
        for line in range(4 * row, 4 * row + 16):
            for block in range(3):
                band[row, line * 3 + block, 125 + block :] = 1.0
    return band.astype(jnp.bfloat16)


def cmul(value, cos, sin):
    re, im = value
    if abs(sin) < 1e-12:
        return (re, im) if cos > 0 else (-re, -im)
    if abs(cos) < 1e-12:
        return (-im, re) if sin > 0 else (im, -re)
    if abs(abs(cos) - abs(sin)) < 1e-12:
        size = abs(cos)
        if cos > 0 and sin > 0:
            return ((re - im) * size, (re + im) * size)
        if cos > 0:
            return ((re + im) * size, (im - re) * size)
        if sin > 0:
            return ((-re - im) * size, (re - im) * size)
        return ((im - re) * size, (-re - im) * size)
    return (re * cos - im * sin, im * cos + re * sin)


def small_dft(values, sign):
    count = len(values)
    if count == 1:
        return values
    even = small_dft(values[0::2], sign)
    odd = small_dft(values[1::2], sign)
    half = count // 2
    low, high = [], []
    for k in range(half):
        angle = sign * 2.0 * math.pi * k / count
        re, im = cmul(odd[k], math.cos(angle), math.sin(angle))
        low.append((even[k][0] + re, even[k][1] + im))
        high.append((even[k][0] - re, even[k][1] - im))
    return low + high


def dft_planes(load, hold, store, sign):
    for m in range(8):
        parts = small_dft([load(8 * i + m) for i in range(4)], sign)
        for s in range(4):
            angle = sign * 2.0 * math.pi * m * s / 32
            re, im = cmul(parts[s], math.cos(angle), math.sin(angle))
            hold[0, s * 8 + m] = re
            hold[1, s * 8 + m] = im
    for s in range(4):
        parts = small_dft([(hold[0, s * 8 + m], hold[1, s * 8 + m]) for m in range(8)], sign)
        for u in range(8):
            store(s + 4 * u, *parts[u])


def split(values):
    high = values.astype(jnp.bfloat16)
    return high, (values - high.astype(jnp.float32)).astype(jnp.bfloat16)


def dot3(values, table):
    high, low = split(values)
    dot = lambda left, right: jnp.dot(left, right, preferred_element_type=jnp.float32)
    return dot(high, table[0]) + (dot(high, table[1]) + dot(low, table[0]))


def filter_kernel(
    stack, gain, mask, forward, inverse, twist, place, out, first, spec, hold, lines_out
):
    for c in range(2):
        for d in range(HERE):
            for n in range(PLANES):
                first[c, n, d * LINES : (d + 1) * LINES] = stack[
                    c, d, :, n * 128 : (n + 1) * 128
                ].astype(jnp.float32)

    def ahead(block, carry):
        rows = pl.ds(pl.multiple_of(block * 8, 8), 8)

        def store(q, re, im):
            spec[0, q, rows] = re
            spec[1, q, rows] = im

        dft_planes(lambda n: (first[0, n, rows], first[1, n, rows]), hold, store, -1)
        return carry

    lax.fori_loop(0, ROWS // 8, ahead, 0)

    def middle(step, carry):
        group = 4
        parts, turns = [], []
        for i in range(group):
            q = step * group + i
            tc = twist[0, pl.ds(q, 1), :]
            ts = twist[1, pl.ds(q, 1), :]
            turns.append((tc, ts))
            re, im = spec[0, q], spec[1, q]
            parts.append(jnp.concatenate([re * tc + im * ts, im * tc - re * ts], axis=1))
        found = dot3(jnp.concatenate(parts, axis=0), forward)
        scaled = []
        for i in range(group):
            q = step * group + i
            for d in range(HERE):
                row = gain[q, pl.ds(d, 1), :]
                begin = i * ROWS + d * LINES
                scaled.append(
                    found[begin : begin + LINES] * jnp.concatenate([row, row], axis=1)
                )
        back = dot3(jnp.concatenate(scaled, axis=0), inverse)
        for i in range(group):
            q = step * group + i
            tc, ts = turns[i]
            re = back[i * ROWS : (i + 1) * ROWS, :128]
            im = back[i * ROWS : (i + 1) * ROWS, 128:]
            spec[0, q] = re * tc - im * ts
            spec[1, q] = im * tc + re * ts
        return carry

    lax.fori_loop(0, PLANES // 4, middle, 0)

    def behind(block, carry):
        rows = pl.ds(pl.multiple_of(block * 8, 8), 8)
        to_re = pl.ds(pl.multiple_of(block * 8, 8), 8)
        to_im = pl.ds(pl.multiple_of(block * 8 + ROWS, 8), 8)
        lines = pl.ds(pl.multiple_of(lax.rem(block, 3) * 8, 8), 8)

        def store(n, re, im):
            weight = mask[lines, n * 128 : (n + 1) * 128].astype(jnp.float32)
            lines_out[n + 1, to_re] = re * weight
            lines_out[n + 1, to_im] = im * weight

        dft_planes(lambda q: (spec[0, q, rows], spec[1, q, rows]), hold, store, 1)
        return carry

    lax.fori_loop(0, ROWS // 8, behind, 0)
    blank = jnp.zeros((2 * ROWS, 128), jnp.float32)
    for n in (0, 33, 34, 35, 36):
        lines_out[n] = blank
    lanes = lax.broadcasted_iota(jnp.int32, (8, 128), 1)

    def tile(t, carry):
        left = jnp.concatenate(
            [
                jnp.concatenate(
                    [lines_out[4 * t + v, pl.ds(line, 8, stride=LINES), :] for line in range(LINES)],
                    axis=0,
                )
                for v in range(5)
            ],
            axis=1,
        ).astype(jnp.bfloat16)
        found = jnp.dot(left, place[...], preferred_element_type=jnp.float32)

        @pl.when(t < TILES)
        def _():
            for line in range(LINES):
                out[t, slot_of(line)] = jnp.concatenate(
                    [found[line * 8 : line * 8 + 8, p * 128 : p * 128 + 128] for p in range(4)],
                    axis=0,
                ).astype(jnp.bfloat16)

        @pl.when(t > 0)
        def _():
            tails = []
            for p in range(4):
                tail = jnp.zeros((8, 128), jnp.float32)
                for line in range(LINES):
                    part = found[line * 8 : line * 8 + 8, p * 128 : p * 128 + 128]
                    if line:
                        part = pltpu.roll(part, 3 * line, 1)
                    keep = (lanes >= 3 * line) & (lanes < 3 * line + 3)
                    tail = jnp.where(keep, part, tail)
                tails.append(tail)
            out[t - 1, TAIL_SLOT] = jnp.concatenate(tails, axis=0).astype(jnp.bfloat16)

        return carry

    lax.fori_loop(0, TILES + 1, tile, 0)


def filter_lines(stack, gains, mask):
    forward, inverse, twist, place = tables()
    gain = jnp.transpose(gains.reshape(HERE, 128, PLANES), (2, 0, 1))
    return pl.pallas_call(
        filter_kernel,
        out_shape=jax.ShapeDtypeStruct((TILES, SLOTS, 32, 128), jnp.bfloat16),
        scratch_shapes=[
            pltpu.VMEM((2, PLANES, ROWS, 128), jnp.float32),
            pltpu.VMEM((2, PLANES, ROWS, 128), jnp.float32),
            pltpu.VMEM((2, PLANES, 8, 128), jnp.float32),
            pltpu.VMEM((37, 2 * ROWS, 128), jnp.float32),
        ],
        name="filter_lines",
    )(stack, gain, mask, forward, inverse, twist, place)


def combo_of(date, group):
    own = date // 8
    return OFFSETS[own] + (date % 8) * (4 - own) + group - own


def fold_rows(parts, low, pair, even):
    half = [
        jnp.where(low, parts[d], parts[d + 4])
        + pltpu.roll(jnp.where(low, parts[d + 4], parts[d]), 4, 0)
        for d in range(4)
    ]
    quarter = [
        jnp.where(
            pair,
            half[d] + pltpu.roll(half[d], 6, 0),
            half[d + 2] + pltpu.roll(half[d + 2], 2, 0),
        )
        for d in range(2)
    ]
    return jnp.where(
        even,
        quarter[0] + pltpu.roll(quarter[0], 7, 0),
        quarter[1] + pltpu.roll(quarter[1], 1, 0),
    )


def link_kernel(own, above, below, band, out, z_re, z_im, z_sum, z_dif, sums, tails, cov, vec):
    rows = lax.broadcasted_iota(jnp.int32, (8, 128), 0)
    lanes = lax.broadcasted_iota(jnp.int32, (8, 128), 1)
    low = rows < 4

    def put(plane, group, first, second):
        re = jnp.where(low, first, pltpu.roll(second, 4, 0))
        im = jnp.where(low, pltpu.roll(first, 4, 0), second)
        z_re[plane, group] = re
        z_im[plane, group] = im
        z_sum[plane, group] = re + im
        z_dif[plane, group] = im - re

    def unpack(ref, slot, line):
        for group in range(4):
            first = ref[2 * group, slot].astype(jnp.float32)
            second = ref[2 * group + 1, slot].astype(jnp.float32)
            for p in range(4):
                put(line * 4 + p, group, first[8 * p : 8 * p + 8], second[8 * p : 8 * p + 8])

    def unpack_run(ref, slot, line, count):
        def step(i, carry):
            unpack(ref, slot + i, line + i)
            return carry

        lax.fori_loop(0, count, step, 0)

    unpack_run(above, 1, 0, 6)
    unpack_run(own, 12, 6, 6)
    unpack_run(own, 0, 12, 12)
    unpack_run(own, 19, 24, 6)
    unpack_run(below, 0, 30, 6)
    for group in range(4):
        pieces = []
        for source in (2 * group, 2 * group + 1):
            mid = own[source, TAIL_SLOT].astype(jnp.float32)
            up = above[source, 0].astype(jnp.float32)
            down = below[source, 6].astype(jnp.float32)
            piece = []
            for p in range(4):
                cut = slice(8 * p, 8 * p + 8)
                value = pltpu.roll(mid[cut], 18, 1)
                value = jnp.where(lanes < 18, pltpu.roll(up[cut], 128 - 54, 1), value)
                value = jnp.where(
                    (lanes >= 90) & (lanes < 108), pltpu.roll(down[cut], 90, 1), value
                )
                piece.append(value)
            pieces.append(piece)
        for p in range(4):
            put(144 + p, group, pieces[0][p], pieces[1][p])

    def gram(base, count, own_group, first_row, groups):
        width = len(groups)
        totals = [[None] * 3 for _ in range(4 * width)]
        for step in range(count):
            plane = base + step
            others = [(z_re[plane, g], z_sum[plane, g], z_dif[plane, g]) for g in groups]
            for i in range(4):
                row = pl.ds(first_row + i, 8, stride=0)
                mine = (
                    z_sum[plane, own_group, row, :],
                    z_re[plane, own_group, row, :],
                    z_im[plane, own_group, row, :],
                )
                for j in range(width):
                    total = totals[i * width + j]
                    for k in range(3):
                        term = others[j][k] * mine[k]
                        total[k] = term if total[k] is None else total[k] + term
        return [(one + three, one - two) for one, two, three in totals]

    for own_group in range(4):
        left = list(range(own_group, 4))
        while left:
            groups, left = left[:2], left[2:]
            width = len(groups)

            def half(h, carry, own_group=own_group, groups=groups, width=width):
                first_row = h * 4

                def one_row(r, carry):
                    found = gram(r * 16, 16, own_group, first_row, groups)
                    for i in range(4 * width):
                        sums[r, i, 0] = found[i][0]
                        sums[r, i, 1] = found[i][1]
                    return carry

                lax.fori_loop(0, 9, one_row, 0)
                found = gram(144, 4, own_group, first_row, groups)
                for i in range(4):
                    for j in range(width):
                        combo = (
                            OFFSETS[own_group]
                            + (first_row + i) * (4 - own_group)
                            + groups[j]
                            - own_group
                        )
                        spot = pl.ds(pl.multiple_of(combo * 8, 8), 8)
                        for c in range(2):
                            tails[c, spot] = found[i * width + j][c]
                            rowsum = [sums[r, i * width + j, c] for r in range(9)]
                            pairs = [rowsum[r] + rowsum[r + 1] for r in range(8)]
                            for a in range(6):
                                value = pairs[a] + pairs[a + 2]
                                value = value + jnp.where(
                                    lanes < 127, pltpu.roll(value, 127, 1), 0.0
                                )
                                value = value + jnp.where(
                                    lanes < 126, pltpu.roll(value, 126, 1), 0.0
                                )
                                cov[a, c, spot] = value
                return carry

            lax.fori_loop(0, 2, half, 0)

    pair = lax.rem(rows, 4) < 2
    even = lax.rem(rows, 2) == 0

    def window_row(a, carry):
        for c in range(2):
            high, lo = split(tails[c])
            cov[a, c] += jnp.dot(
                high, band[a], preferred_element_type=jnp.float32
            ) + jnp.dot(lo, band[a], preferred_element_type=jnp.float32)
        inverse = []
        for g in range(4):
            power = jnp.zeros((8, 128), jnp.float32)
            for i in range(8):
                combo = combo_of(8 * g + i, g)
                power = jnp.where(rows == i, cov[a, 0, combo * 8 : combo * 8 + 8], power)
            inverse.append(1.0 / jnp.sqrt(power + BETA_LOAD))
        for g in range(4):
            vec[0, g] = inverse[g]
            vec[1, g] = jnp.zeros((8, 128), jnp.float32)
            vec[2, g] = inverse[g]

        def iterate(step, carry):
            have_re = [vec[0, g] for g in range(4)]
            have_im = [vec[1, g] for g in range(4)]
            new_re = [jnp.zeros((8, 128), jnp.float32)] * 4
            new_im = [jnp.zeros((8, 128), jnp.float32)] * 4
            for own_group in range(4):
                parts_re, parts_im = [], []
                for i in range(8):
                    row = pl.ds(i, 8, stride=0)
                    mine_re = vec[0, own_group, row, :]
                    mine_im = vec[1, own_group, row, :]
                    part_re = part_im = None
                    for g in range(own_group, 4):
                        combo = combo_of(8 * own_group + i, g)
                        cov_re = cov[a, 0, combo * 8 : combo * 8 + 8]
                        cov_im = cov[a, 1, combo * 8 : combo * 8 + 8]
                        new_re[g] = new_re[g] + (cov_re * mine_re + cov_im * mine_im)
                        new_im[g] = new_im[g] + (cov_re * mine_im - cov_im * mine_re)
                        if g > own_group:
                            term_re = cov_re * have_re[g] - cov_im * have_im[g]
                            term_im = cov_re * have_im[g] + cov_im * have_re[g]
                            part_re = term_re if part_re is None else part_re + term_re
                            part_im = term_im if part_im is None else part_im + term_im
                    parts_re.append(part_re)
                    parts_im.append(part_im)
                if own_group < 3:
                    new_re[own_group] = new_re[own_group] + fold_rows(parts_re, low, pair, even)
                    new_im[own_group] = new_im[own_group] + fold_rows(parts_im, low, pair, even)
            for g in range(4):
                weight = vec[2, g]
                u_re = new_re[g] * weight
                u_im = new_im[g] * weight
                length = 1.0 / jnp.sqrt(u_re * u_re + u_im * u_im + PROJ_LOAD)
                x_re = u_re * length
                x_im = u_im * length
                vec[3, g] = x_re
                vec[4, g] = x_im
                vec[0, g] = x_re * weight
                vec[1, g] = x_im * weight
            return carry

        lax.fori_loop(0, ITERS, iterate, 0)
        for g in range(4):
            for i in range(8):
                for c in range(2):
                    out[c, 8 * g + i, pl.ds(a, 1), :] = vec[3 + c, g, i : i + 1, :]
        return carry

    lax.fori_loop(0, 6, window_row, 0)


def link_windows(own, above, below):
    field = pltpu.VMEM((148, 4, 8, 128), jnp.float32)
    return pl.pallas_call(
        link_kernel,
        out_shape=jax.ShapeDtypeStruct((2, DATES, 6, 128), jnp.float32),
        scratch_shapes=[
            field,
            field,
            field,
            field,
            pltpu.VMEM((9, 8, 2, 8, 128), jnp.float32),
            pltpu.VMEM((2, COMBOS * 8, 128), jnp.float32),
            pltpu.VMEM((6, 2, COMBOS * 8, 128), jnp.float32),
            pltpu.VMEM((5, 4, 8, 128), jnp.float32),
        ],
        name="link_windows",
    )(own, above, below, tail_band())


def on_device(stack, range_filter, scatter_mask):
    tiles = filter_lines(stack, range_filter, scatter_mask)
    own = lax.all_to_all(tiles, "dr", split_axis=0, concat_axis=0, tiled=True)
    count = lax.axis_size("az")
    down = [(i, i + 1) for i in range(count - 1)]
    up = [(i + 1, i) for i in range(count - 1)]
    above = lax.ppermute(own[:, 18:25], "az", down)
    below = lax.ppermute(own[:, 12:19], "az", up)
    return link_windows(own, above, below)


def solution(mesh):
    in_specs = (P(None, "dr", "az", None), P("dr", None), P("az", None))
    out_specs = P(None, None, "az", "dr")
    return jax.shard_map(
        on_device, mesh=mesh, in_specs=in_specs, out_specs=out_specs, check_vma=False
    )
```

profile of v0, /device:TPU:65, one launch (start us, length us, event | category | flops | bytes accessed | tf_op | source)
XLA Modules:
  0.0 97.6 jit_solution(13166884103255455745)
XLA Ops:
  0.0 1.0 reshape.3
  1.0 0.7 copy.10
  1.7 15.7 %filter_lines.1 = bf16[8,25,32,128]{3,2,1,0:T(8,128)(2,1)} custom-call(bf16[2,4,24,4096]{3,2,1,0:T(8,128)(2,1)} %stack.1, f32[32,4,128]{2,1,0:T(4,128)} %bitcast.1, s32[24,4096]{1,0:T(8,128)} %mask.1, bf16[2,256,256]{2,1,0:T(8,128)(2,1)} %constant.10.clone.forward, bf16[2,256,256]{2,1,0:T(8,128)(2,1)} %constant.11.clone.inverse, ...), custom_call_target="tpu_custom_call" | custom-call | tf_op jit(solution)/shard_map/filter_lines/pallas_call | solution.py:240
  17.4 26.1 %all_to_all.5.own = bf16[8,25,32,128]{3,2,1,0:T(8,128)(2,1)S(1)} all-to-all(bf16[8,25,32,128]{3,2,1,0:T(8,128)(2,1)} %filter_lines.1), channel_id=1, replica_groups=mesh['az'=32,'dr'=8] {'dr'}, dimensions={0} | all-to-all | bytes 3276800 | tf_op jit(solution)/shard_map/all_to_all | solution.py:487
  43.6 0.0 copy-start
  43.6 0.1 fusion
  43.7 4.0 %collective-permute-start.1 = (bf16[8,7,32,128]{3,2,1,0:T(8,128)(2,1)S(1)}, bf16[8,7,32,128]{3,2,1,0:T(8,128)(2,1)S(1)}, u32[]{:S(2)}, u32[]{:S(2)}) collective-permute-start(bf16[8,7,32,128]{3,2,1,0:T(8,128)(2,1)S(1)} %get-tuple-element.5), channel_id=1, source_target_pairs={{8,0},{16,8},{24,16},{32,24},{40,32},{48,40},{56,48},{64,56},{72,6... | collective-permute-start | bytes 1376264 | tf_op jit(solution)/shard_map/ppermute | solution.py:492
  47.7 4.4 %collective-permute-start = (bf16[8,7,32,128]{3,2,1,0:T(8,128)(2,1)S(1)}, bf16[8,7,32,128]{3,2,1,0:T(8,128)(2,1)S(1)}, u32[]{:S(2)}, u32[]{:S(2)}) collective-permute-start(bf16[8,7,32,128]{3,2,1,0:T(8,128)(2,1)S(1)} %get-tuple-element.6), channel_id=1, source_target_pairs={{0,8},{8,16},{16,24},{24,32},{32,40},{40,48},{48,56},{56,64},{64,7... | collective-permute-start | bytes 1376264 | tf_op jit(solution)/shard_map/ppermute | solution.py:491
  52.1 9.1 %collective-permute-done.1.below = bf16[8,7,32,128]{3,2,1,0:T(8,128)(2,1)S(1)} collective-permute-done((bf16[8,7,32,128]{3,2,1,0:T(8,128)(2,1)S(1)}, bf16[8,7,32,128]{3,2,1,0:T(8,128)(2,1)S(1)}, u32[]{:S(2)}, u32[]{:S(2)}) %collective-permute-start.1) | collective-permute-done | bytes 458784 | tf_op jit(solution)/shard_map/ppermute | solution.py:492
  61.2 0.0 copy-start.1
  61.2 0.0 collective-permute-done.above
  61.2 0.0 copy-done
  61.2 0.8 copy-done.1
  62.0 0.0 copy-start.2
  62.0 0.8 copy-done.2
  62.8 33.2 %link_windows.1 = f32[2,32,6,128]{3,2,1,0:T(8,128)} custom-call(bf16[8,25,32,128]{3,2,1,0:T(8,128)(2,1)} %copy-done, bf16[8,7,32,128]{3,2,1,0:T(8,128)(2,1)} %copy-done.2, bf16[8,7,32,128]{3,2,1,0:T(8,128)(2,1)} %copy-done.1, bf16[6,128,128]{2,1,0:T(8,128)(2,1)} %constant.14.clone.band), custom_call_target="tpu_custom_call" | custom-call | tf_op jit(solution)/shard_map/link_windows/pallas_call | solution.py:468
  96.0 1.7 %copy.11 = f32[2,32,6,128]{3,1,2,0:T(8,128)} copy(f32[2,32,6,128]{3,2,1,0:T(8,128)} %link_windows.1) | data formatting | bytes 393216 | tf_op jit(solution)/shard_map/link_windows/pallas_call | solution.py:468
Async XLA Ops:
  43.6 17.7 %copy-start = (bf16[8,25,32,128]{3,2,1,0:T(8,128)(2,1)}, bf16[8,25,32,128]{3,2,1,0:T(8,128)(2,1)S(1)}, u32[]{:S(2)}) copy-start(bf16[8,25,32,128]{3,2,1,0:T(8,128)(2,1)S(1)} %all_to_all.5.own) | copy-start | bytes 4915204
  43.7 17.6 %collective-permute-start.1 = (bf16[8,7,32,128]{3,2,1,0:T(8,128)(2,1)S(1)}, bf16[8,7,32,128]{3,2,1,0:T(8,128)(2,1)S(1)}, u32[]{:S(2)}, u32[]{:S(2)}) collective-permute-start(bf16[8,7,32,128]{3,2,1,0:T(8,128)(2,1)S(1)} %get-tuple-element.5), channel_id=1, source_target_pairs={{8,0},{16,8},{24,16},{32,24},{40,32},{48,40},{56,48},{64,56},{72,6... | collective-permute-start | bytes 1376264 | tf_op jit(solution)/shard_map/ppermute | solution.py:492
  47.7 13.6 %collective-permute-start = (bf16[8,7,32,128]{3,2,1,0:T(8,128)(2,1)S(1)}, bf16[8,7,32,128]{3,2,1,0:T(8,128)(2,1)S(1)}, u32[]{:S(2)}, u32[]{:S(2)}) collective-permute-start(bf16[8,7,32,128]{3,2,1,0:T(8,128)(2,1)S(1)} %get-tuple-element.6), channel_id=1, source_target_pairs={{0,8},{8,16},{16,24},{24,32},{32,40},{40,48},{48,56},{56,64},{64,7... | collective-permute-start | bytes 1376264 | tf_op jit(solution)/shard_map/ppermute | solution.py:491
  61.2 0.8 copy-start.1
  62.0 0.8 copy-start.2
where the time goes:
time: 98 us; the launch traced here: 97.6 us
  Pallas kernels  48.9 us (50%)
  blocking collectives  26.1 us (27%)
  waiting for transfers between devices  9.14 us (9%)
  starting transfers between devices  8.41 us (9%)
  local copies, waits for them, and re-layouts  4.98 us (5%)
    pallas_call x1, Pallas kernels, link_windows(): pl.pallas_call(link_kernel, out_shape=jax.ShapeDtypeStruct((2, DATES, 6,...  33.2 us
    all_to_all x1, blocking collectives, on_device(): own = lax.all_to_all(tiles, 'dr', split_axis=0, concat_axis=0, tiled=True)  26.1 us
    pallas_call x1, Pallas kernels, filter_lines(): pl.pallas_call(filter_kernel, out_shape=jax.ShapeDtypeStruct((TILES, SLOT...  15.7 us
    ppermute x1, waiting for transfers between devices, on_device(): below = lax.ppermute(own[:, 12:19], 'az', up)  9.13 us
    ppermute x1, starting transfers between devices, on_device(): above = lax.ppermute(own[:, 18:25], 'az', down)  4.43 us
    ppermute x1, starting transfers between devices, on_device(): below = lax.ppermute(own[:, 12:19], 'az', up)  3.99 us
  transfers between devices with their start and end apart: 2, of which 1 were waited for; matrix products, arithmetic and copies ran while one was open for 0% of the time, Pallas kernels for 0%

commit v1 on v0

v1 whole, which is shorter than its diff:
```python
import math

import jax
import jax.numpy as jnp
import numpy as np
from jax import lax
from jax.experimental import pallas as pl
from jax.experimental.pallas import tpu as pltpu
from jax.sharding import PartitionSpec as P

ITERS = 4
BETA_LOAD = 1.0
PROJ_LOAD = 1.0

DATES = 32
LINES = 24
RG = 4096
TILES = 8
HALO = 6
PLANES = 32
HERE = 4
ROWS = HERE * LINES
SLOTS = LINES + 1
TAIL_SLOT = 18
SHIFTS = 17
PAIRS = SHIFTS * DATES
WRAP = 48


def slot_of(line):
    if line < 6:
        return 12 + line
    return line - 6 if line < 18 else line + 1


def split_np(table):
    high = table.astype(jnp.bfloat16)
    low = (table - high.astype(np.float64)).astype(jnp.bfloat16)
    return np.concatenate([high, high, low], axis=0)


def tables():
    lane = np.arange(128)
    freq = 4 * (lane % 32) + lane // 32
    turn = 2.0 * np.pi / 128 * (np.outer(lane, freq) % 128)
    forward = split_np(np.block([[np.cos(turn), -np.sin(turn)], [np.sin(turn), np.cos(turn)]]))
    turn = 2.0 * np.pi / 128 * (np.outer(freq, lane - HALO) % 128)
    inverse = split_np(
        np.block([[np.cos(turn), np.sin(turn)], [-np.sin(turn), np.cos(turn)]]) / RG
    )
    plane = np.arange(PLANES)
    angle = 2.0 * np.pi / RG * np.outer(plane, lane)
    back = 2.0 * np.pi / RG * np.outer(plane, lane - HALO)
    twist = np.stack([np.cos(angle), np.sin(angle), np.cos(back), np.sin(back)])
    place = np.zeros((512, 512), np.float32)
    for phase in range(4):
        for block in range(128):
            place[4 * block + phase, phase * 128 + block] = 1.0
    return forward, inverse, twist.astype(np.float32), place.astype(jnp.bfloat16)


def tail_band():
    band = np.zeros((6, 128, 128), np.float32)
    for row in range(6):
        for line in range(4 * row, 4 * row + 16):
            for block in range(3):
                band[row, line * 3 + block, 125 + block :] = 1.0
    return band.astype(jnp.bfloat16)


def cmul(value, cos, sin):
    re, im = value
    if abs(sin) < 1e-12:
        return (re, im) if cos > 0 else (-re, -im)
    if abs(cos) < 1e-12:
        return (-im, re) if sin > 0 else (im, -re)
    if abs(abs(cos) - abs(sin)) < 1e-12:
        size = abs(cos)
        if cos > 0 and sin > 0:
            return ((re - im) * size, (re + im) * size)
        if cos > 0:
            return ((re + im) * size, (im - re) * size)
        if sin > 0:
            return ((-re - im) * size, (re - im) * size)
        return ((im - re) * size, (-re - im) * size)
    return (re * cos - im * sin, im * cos + re * sin)


def small_dft(values, sign):
    count = len(values)
    if count == 1:
        return values
    even = small_dft(values[0::2], sign)
    odd = small_dft(values[1::2], sign)
    half = count // 2
    low, high = [], []
    for k in range(half):
        angle = sign * 2.0 * math.pi * k / count
        re, im = cmul(odd[k], math.cos(angle), math.sin(angle))
        low.append((even[k][0] + re, even[k][1] + im))
        high.append((even[k][0] - re, even[k][1] - im))
    return low + high


def dft_planes(load, hold, store, sign):
    for m in range(8):
        parts = small_dft([load(8 * i + m) for i in range(4)], sign)
        for s in range(4):
            angle = sign * 2.0 * math.pi * m * s / 32
            re, im = cmul(parts[s], math.cos(angle), math.sin(angle))
            hold[0, s * 8 + m] = re
            hold[1, s * 8 + m] = im
    for s in range(4):
        parts = small_dft([(hold[0, s * 8 + m], hold[1, s * 8 + m]) for m in range(8)], sign)
        for u in range(8):
            store(s + 4 * u, *parts[u])


def split(values):
    high = values.astype(jnp.bfloat16)
    return high, (values - high.astype(jnp.float32)).astype(jnp.bfloat16)


def dot3(values, table):
    high, low = split(values)
    return jnp.dot(
        jnp.concatenate([high, low, high], axis=1), table, preferred_element_type=jnp.float32
    )


GROUP = 4


def filter_kernel(
    stack, gains, mask, forward, inverse, twist, place, out,
    first, spec, hold, held, gain, weights, lines_out,
):
    lanes = lax.broadcasted_iota(jnp.int32, (8, 128), 1)
    for c in range(2):
        for d in range(HERE):
            for n in range(PLANES):
                first[c, n, d * LINES : (d + 1) * LINES] = stack[
                    c, d, :, n * 128 : (n + 1) * 128
                ].astype(jnp.float32)
    for n in range(PLANES):
        four = gains[:, n * 128 : (n + 1) * 128]
        for d in range(HERE):
            gain[d, n : n + 1] = four[d : d + 1]
    for d in range(HERE):
        turned = jnp.transpose(gain[d])
        gain[d] = jnp.concatenate([turned[32 * w : 32 * w + 32] for w in range(4)], axis=1)
    for block in range(LINES // 8):
        rows = slice(8 * block, 8 * block + 8)
        before = pltpu.roll(mask[rows, RG - 128 :].astype(jnp.float32), HALO, 1)
        for n in range(PLANES):
            now = pltpu.roll(mask[rows, n * 128 : (n + 1) * 128].astype(jnp.float32), HALO, 1)
            joined = jnp.where(lanes < HALO, before, now)
            if n == 0:
                weights[PLANES, rows] = jnp.where(lanes < HALO, joined, 0.0)
                joined = jnp.where(lanes < HALO, 0.0, joined)
            weights[n, rows] = joined
            before = now

    def ahead(block, carry):
        rows = pl.ds(pl.multiple_of(block * 8, 8), 8)

        def store(q, re, im):
            spec[0, q, rows] = re
            spec[1, q, rows] = im

        dft_planes(lambda n: (first[0, n, rows], first[1, n, rows]), hold, store, -1)
        return carry

    lax.fori_loop(0, ROWS // 8, ahead, 0)
    steps = PLANES // GROUP

    def middle(step, carry):
        now = jnp.minimum(step, steps - 1) * GROUP
        past = jnp.maximum(step - 1, 0) * GROUP
        parts = []
        for i in range(GROUP):
            tc = twist[0, pl.ds(now + i, 1), :]
            ts = twist[1, pl.ds(now + i, 1), :]
            re, im = spec[0, now + i], spec[1, now + i]
            parts.append(jnp.concatenate([re * tc + im * ts, im * tc - re * ts], axis=1))
        back = dot3(held[lax.rem(step + 1, 2)], inverse[...])
        found = dot3(jnp.concatenate(parts, axis=0), forward[...])
        for i in range(GROUP):
            for d in range(HERE):
                row = gain[d, pl.ds(now + i, 1), :]
                begin = i * ROWS + d * LINES
                held[lax.rem(step, 2), begin : begin + LINES] = found[
                    begin : begin + LINES
                ] * jnp.concatenate([row, row], axis=1)
        for i in range(GROUP):
            tc = twist[2, pl.ds(past + i, 1), :]
            ts = twist[3, pl.ds(past + i, 1), :]
            re = back[i * ROWS : (i + 1) * ROWS, :128]
            im = back[i * ROWS : (i + 1) * ROWS, 128:]
            first[0, past + i] = re * tc - im * ts
            first[1, past + i] = im * tc + re * ts
        return carry

    lax.fori_loop(0, steps + 1, middle, 0)

    def behind(block, carry):
        rows = pl.ds(pl.multiple_of(block * 8, 8), 8)
        to_im = pl.ds(pl.multiple_of(block * 8 + ROWS, 8), 8)
        lines = pl.ds(pl.multiple_of(lax.rem(block, 3) * 8, 8), 8)

        def store(n, re, im):
            weight = weights[n, lines]
            lines_out[n, rows] = re * weight
            lines_out[n, to_im] = im * weight
            if n == 0:
                weight = weights[PLANES, lines]
                lines_out[PLANES, rows] = re * weight
                lines_out[PLANES, to_im] = im * weight

        dft_planes(lambda q: (first[0, q, rows], first[1, q, rows]), hold, store, 1)
        return carry

    lax.fori_loop(0, ROWS // 8, behind, 0)

    def gather(plane):
        return jnp.concatenate(
            [lines_out[plane, pl.ds(line, 8, stride=LINES), :] for line in range(LINES)], axis=0
        )

    def put_tail(slot, found):
        tails = []
        for p in range(4):
            tail = jnp.zeros((8, 128), jnp.float32)
            for line in range(LINES):
                part = found[line * 8 : line * 8 + 8, p * 128 : p * 128 + 128]
                if line:
                    part = pltpu.roll(part, 3 * line, 1)
                tail = jnp.where(lanes >= 3 * line, part, tail)
            tails.append(jnp.where(lanes < 3 * LINES, tail, 0.0))
        out[slot, TAIL_SLOT] = jnp.concatenate(tails, axis=0).astype(jnp.bfloat16)

    def tile(t, carry):
        left = jnp.concatenate([gather(4 * t + v) for v in range(4)], axis=1).astype(jnp.bfloat16)
        found = jnp.dot(left, place[...], preferred_element_type=jnp.float32)
        for line in range(LINES):
            out[t, slot_of(line)] = jnp.concatenate(
                [found[line * 8 : line * 8 + 8, p * 128 : p * 128 + 128] for p in range(4)],
                axis=0,
            ).astype(jnp.bfloat16)
        put_tail(lax.rem(t + TILES - 1, TILES), found)
        return carry

    lax.fori_loop(0, TILES, tile, 0)
    found = jnp.dot(
        gather(PLANES).astype(jnp.bfloat16), place[:128], preferred_element_type=jnp.float32
    )
    put_tail(TILES - 1, found)


def filter_lines(stack, gains, mask):
    forward, inverse, twist, place = tables()
    return pl.pallas_call(
        filter_kernel,
        out_shape=jax.ShapeDtypeStruct((TILES, SLOTS, 32, 128), jnp.bfloat16),
        scratch_shapes=[
            pltpu.VMEM((2, PLANES, ROWS, 128), jnp.float32),
            pltpu.VMEM((2, PLANES, ROWS, 128), jnp.float32),
            pltpu.VMEM((2, PLANES, 8, 128), jnp.float32),
            pltpu.VMEM((2, GROUP * ROWS, 256), jnp.float32),
            pltpu.VMEM((HERE, PLANES, 128), jnp.float32),
            pltpu.VMEM((PLANES + 1, LINES, 128), jnp.float32),
            pltpu.VMEM((PLANES + 1, 2 * ROWS, 128), jnp.float32),
        ],
        compiler_params=pltpu.CompilerParams(vmem_limit_bytes=24 << 20),
        cost_estimate=pl.CostEstimate(
            flops=4_000_000_000, bytes_accessed=4_000_000, transcendentals=0
        ),
        name="filter_lines",
    )(stack, gains, mask, forward, inverse, twist, place)


def unpacker(fields):
    z_re, z_im, z_sum, z_dif = fields
    rows = lax.broadcasted_iota(jnp.int32, (8, 128), 0)
    low = rows < 4

    def put(plane, group, first, second):
        re = jnp.where(low, first, pltpu.roll(second, 4, 0))
        im = jnp.where(low, pltpu.roll(first, 4, 0), second)
        total, change = re + im, im - re
        z_im[plane, 8 * group : 8 * group + 8] = im
        for begin in [8 * group] + ([32 + 8 * group] if group < 2 else []):
            z_re[plane, begin : begin + 8] = re
            z_sum[plane, begin : begin + 8] = total
            z_dif[plane, begin : begin + 8] = change

    def run(ref, slot, line, count):
        def step(i, carry):
            for group in range(4):
                first = ref[2 * group, slot + i].astype(jnp.float32)
                second = ref[2 * group + 1, slot + i].astype(jnp.float32)
                for p in range(4):
                    cut = slice(8 * p, 8 * p + 8)
                    put((line + i) * 4 + p, group, first[cut], second[cut])
            return carry

        lax.fori_loop(0, count, step, 0)

    return put, run


WIDTH = 8


def gram(fields, base, count, store):
    z_re, z_im, z_sum, z_dif = fields

    def block(index, carry):
        group = index // 2
        own = pl.ds(pl.multiple_of(group * 8, 8), 8)
        begin = pl.multiple_of(group * 8 + lax.rem(index, 2) * 8, 8)
        totals = [[None] * 3 for _ in range(WIDTH)]
        for step in range(count):
            plane = base + step
            mine = (z_sum[plane, own], z_re[plane, own], z_im[plane, own])
            for i in range(WIDTH):
                other = pl.ds(begin + 1 + i, 8)
                others = (z_re[plane, other], z_sum[plane, other], z_dif[plane, other])
                for k in range(3):
                    term = others[k] * mine[k]
                    totals[i][k] = term if step == 0 else totals[i][k] + term
        for i in range(WIDTH):
            one, two, three = totals[i]
            spot = (lax.rem(index, 2) * 8 + 1 + i) * DATES + group * 8
            spot = pl.ds(pl.multiple_of(spot, 8), 8)
            store(0, spot, one + three)
            store(1, spot, one - two)
        return carry

    lax.fori_loop(0, 8, block, 0)
    for group in range(4):
        own = slice(8 * group, 8 * group + 8)
        total = None
        for step in range(count):
            re, im = z_re[base + step, own], z_im[base + step, own]
            term = re * re + im * im
            total = term if total is None else total + term
        store(0, own, total)


def gram_rows(fields, sums, count, first_plane, first_row):
    def one_row(r, carry):
        def store(c, spot, value):
            sums[first_row + r, c, spot] = value

        gram(fields, first_plane + r * 16, 16, store)
        return carry

    lax.fori_loop(0, count, one_row, 0)


def inner_kernel(own, sums, z_re, z_im, z_sum, z_dif):
    fields = (z_re, z_im, z_sum, z_dif)
    put, run = unpacker(fields)
    run(own, 14, 0, 4)
    run(own, 0, 4, 12)
    run(own, 19, 16, 4)
    gram_rows(fields, sums, 5, 0, 0)


def inner_rows(own):
    field = pltpu.VMEM((80, WRAP, 128), jnp.float32)
    return pl.pallas_call(
        inner_kernel,
        out_shape=jax.ShapeDtypeStruct((5, 2, PAIRS, 128), jnp.float32),
        scratch_shapes=[field] * 4,
        compiler_params=pltpu.CompilerParams(vmem_limit_bytes=24 << 20),
        cost_estimate=pl.CostEstimate(
            flops=20_000_000_000, bytes_accessed=4_000_000, transcendentals=0
        ),
        name="inner_rows",
    )(own)


def link_kernel(
    own, above, below, inner, band, out, z_re, z_im, z_sum, z_dif, sums, tails, extra, cov, vec
):
    fields = (z_re, z_im, z_sum, z_dif)
    lanes = lax.broadcasted_iota(jnp.int32, (8, 128), 1)
    put, run = unpacker(fields)
    run(above, 1, 0, 6)
    run(own, 12, 6, 2)
    run(own, 23, 8, 2)
    run(below, 0, 10, 6)
    for group in range(4):
        pieces = []
        for source in (2 * group, 2 * group + 1):
            mid = own[source, TAIL_SLOT].astype(jnp.float32)
            up = above[source, 0].astype(jnp.float32)
            down = below[source, 6].astype(jnp.float32)
            piece = []
            for p in range(4):
                cut = slice(8 * p, 8 * p + 8)
                value = pltpu.roll(mid[cut], 18, 1)
                value = jnp.where(lanes < 18, pltpu.roll(up[cut], 128 - 54, 1), value)
                value = jnp.where(
                    (lanes >= 90) & (lanes < 108), pltpu.roll(down[cut], 90, 1), value
                )
                piece.append(value)
            pieces.append(piece)
        for p in range(4):
            put(64 + p, group, pieces[0][p], pieces[1][p])

    def store_tail(c, spot, value):
        tails[c, spot] = value

    gram(fields, 64, 4, store_tail)
    tails[1, 0:DATES] = jnp.zeros((DATES, 128), jnp.float32)
    gram_rows(fields, sums, 4, 0, 0)

    def add_tail(a, carry):
        for c in range(2):
            high, low = split(tails[c])
            extra[a, c] = jnp.dot(
                jnp.concatenate([high, low], axis=1),
                jnp.concatenate([band[a], band[a]], axis=0),
                preferred_element_type=jnp.float32,
            )
        return carry

    lax.fori_loop(0, 6, add_tail, 0)

    def windows(c, s, group):
        spot = s * DATES + group * 8
        spot = spot if isinstance(spot, int) else pl.multiple_of(spot, 8)
        where = pl.ds(spot, 8)
        rowsum = [sums[r, c, where] for r in (0, 1)]
        rowsum += [inner[r, c, where] for r in range(5)]
        rowsum += [sums[r, c, where] for r in (2, 3)]
        pairs = [rowsum[r] + rowsum[r + 1] for r in range(8)]
        twice = s * 2 * DATES + group * 8
        twice = twice if isinstance(twice, int) else pl.multiple_of(twice, 8)
        for a in range(6):
            value = pairs[a] + pairs[a + 2]
            value = value + jnp.where(lanes < 127, pltpu.roll(value, 127, 1), 0.0)
            value = value + jnp.where(lanes < 126, pltpu.roll(value, 126, 1), 0.0)
            value = value + extra[a, c, where]
            cov[a, c, pl.ds(twice, 8)] = value
            cov[a, c, pl.ds(twice + DATES, 8)] = value

    for group in range(4):
        windows(0, 0, group)

    def shift_windows(s, carry):
        for group in range(4):
            windows(0, s, group)
            windows(1, s, group)
        return carry

    lax.fori_loop(1, SHIFTS, shift_windows, 0)

    def put_vec(c, group, value):
        for copy in range(3):
            vec[c, copy * DATES + group * 8 : copy * DATES + group * 8 + 8] = value

    def window_row(a, carry):
        weights = []
        for group in range(4):
            power = cov[a, 0, 8 * group : 8 * group + 8]
            weights.append(1.0 / jnp.sqrt(power + BETA_LOAD))
            put_vec(0, group, weights[group])

        def iterate(real, last):
            found = []
            for group in range(4):
                row = 8 * group
                re_parts, im_parts = [], []
                for s in range(SHIFTS):
                    terms = [(2 * s * DATES + row, DATES + row + s, 1)]
                    if 0 < s < SHIFTS - 1:
                        terms.append((2 * s * DATES + DATES + row - s, DATES + row - s, -1))
                    for place, other, sign in terms:
                        cov_re = cov[a, 0, place : place + 8]
                        x_re = vec[0, other : other + 8]
                        x_im = None if real else vec[1, other : other + 8]
                        if s == 0:
                            re = cov_re * x_re
                            im = None if real else cov_re * x_im
                        else:
                            cov_im = cov[a, 1, place : place + 8]
                            re = cov_re * x_re
                            im = cov_im * x_re
                            if sign < 0:
                                im = -im if real else cov_re * x_im - im
                                re = re if real else re + cov_im * x_im
                            elif not real:
                                re = re - cov_im * x_im
                                im = im + cov_re * x_im
                        re_parts.append(re)
                        if im is not None:
                            im_parts.append(im)
                found.append((sum_two(re_parts), sum_two(im_parts)))
            for group in range(4):
                u_re = found[group][0] * weights[group]
                u_im = found[group][1] * weights[group]
                length = 1.0 / jnp.sqrt(u_re * u_re + u_im * u_im + PROJ_LOAD)
                x_re, x_im = u_re * length, u_im * length
                if last:
                    out[0, a, 8 * group : 8 * group + 8] = x_re
                    out[1, a, 8 * group : 8 * group + 8] = x_im
                else:
                    put_vec(0, group, x_re * weights[group])
                    put_vec(1, group, x_im * weights[group])

        iterate(True, False)
        lax.fori_loop(0, ITERS - 2, lambda i, carry: (iterate(False, False), carry)[1], 0)
        iterate(False, True)
        return carry

    lax.fori_loop(0, 6, window_row, 0)


def sum_two(parts):
    sums = parts[:2]
    for i, part in enumerate(parts[2:]):
        sums[i % 2] = sums[i % 2] + part
    return sums[0] + sums[1]


def link_windows(own, above, below, inner):
    field = pltpu.VMEM((68, WRAP, 128), jnp.float32)
    found = pl.pallas_call(
        link_kernel,
        out_shape=jax.ShapeDtypeStruct((2, 6, DATES, 128), jnp.float32),
        scratch_shapes=[field] * 4
        + [
            pltpu.VMEM((4, 2, PAIRS, 128), jnp.float32),
            pltpu.VMEM((2, PAIRS, 128), jnp.float32),
            pltpu.VMEM((6, 2, PAIRS, 128), jnp.float32),
            pltpu.VMEM((6, 2, 2 * PAIRS, 128), jnp.float32),
            pltpu.VMEM((2, 3 * DATES, 128), jnp.float32),
        ],
        compiler_params=pltpu.CompilerParams(vmem_limit_bytes=40 << 20),
        cost_estimate=pl.CostEstimate(
            flops=20_000_000_000, bytes_accessed=8_000_000, transcendentals=0
        ),
        name="link_windows",
    )(own, above, below, inner, tail_band())
    return jnp.transpose(found, (0, 2, 1, 3))


def on_device(stack, range_filter, scatter_mask):
    tiles = filter_lines(stack, range_filter, scatter_mask)
    own = lax.all_to_all(tiles, "dr", split_axis=0, concat_axis=0, tiled=True)
    count = lax.axis_size("az")
    down = [(i, i + 1) for i in range(count - 1)]
    up = [(i + 1, i) for i in range(count - 1)]
    above = lax.ppermute(own[:, 18:25], "az", down)
    below = lax.ppermute(own[:, 12:19], "az", up)
    inner = inner_rows(own)
    return link_windows(own, above, below, inner)


def solution(mesh):
    in_specs = (P(None, "dr", "az", None), P("dr", None), P("az", None))
    out_specs = P(None, None, "az", "dr")
    return jax.shard_map(
        on_device, mesh=mesh, in_specs=in_specs, out_specs=out_specs, check_vma=False
    )
```

time: 98 us -> 79.7 us (0.81)
  Pallas kernels: 48.9 us -> 36.3 us
  waiting for transfers between devices: 9.14 us -> 0.82 us
  local copies, waits for them, and re-layouts: 4.98 us -> 7.2 us
    ppermute x1, waiting for transfers between devices: 9.13 us -> 0.82 us  [on_device(): below = lax.ppermute(own[:, 12:19], 'az', up)]
    pallas_call x1 -> x2, Pallas kernels: 33.2 us -> 26.2 us  [the longest x1 18.1 us: link_windows(): pl.pallas_call(link_kernel, out_shape=jax.ShapeDtypeStruct((2, 6, DATES,...]
    pallas_call x1, Pallas kernels: 15.7 us -> 10.1 us  [filter_lines(): pl.pallas_call(filter_kernel, out_shape=jax.ShapeDtypeStruct((TILES, SLOT...]
    unnamed x6 -> x16, local copies, waits for them, and re-layouts: 1.53 us -> 7.12 us
    reshape x2 -> x0, local copies, waits for them, and re-layouts: 1.71 us -> none  [filter_lines(): gain = jnp.transpose(gains.reshape(HERE, 128, PLANES), (2, 0, 1))]
    pallas_call x1 -> x0, local copies, waits for them, and re-layouts: 1.66 us -> none  [link_windows(): pl.pallas_call(link_kernel, out_shape=jax.ShapeDtypeStruct((2, DATES, 6,...]
  transfers between devices with their start and end apart: 2 -> 2, of which waited for: 1 -> 1; matrix products, arithmetic and copies ran while one was open for 0% -> 0% of each run, Pallas kernels for 0% -> 10%
where the time goes in v1:
time: 79.7 us; the launch traced here: 78.8 us
  Pallas kernels  36.3 us (46%)
  blocking collectives  25.9 us (32%)
  starting transfers between devices  8.56 us (11%)
  local copies, waits for them, and re-layouts  7.2 us (9%)
  waiting for transfers between devices  0.82 us (1%)
    all_to_all x1, blocking collectives, on_device(): own = lax.all_to_all(tiles, 'dr', split_axis=0, concat_axis=0, tiled=True)  25.9 us
    pallas_call x1, Pallas kernels, link_windows(): pl.pallas_call(link_kernel, out_shape=jax.ShapeDtypeStruct((2, 6, DATES,...  18.1 us
    pallas_call x1, Pallas kernels, filter_lines(): pl.pallas_call(filter_kernel, out_shape=jax.ShapeDtypeStruct((TILES, SLOT...  10.1 us
    pallas_call x1, Pallas kernels, inner_rows(): pl.pallas_call(inner_kernel, out_shape=jax.ShapeDtypeStruct((5, 2, PAIRS,...  8.17 us
    unnamed x16, local copies, waits for them, and re-layouts  7.12 us
    ppermute x1, starting transfers between devices, on_device(): above = lax.ppermute(own[:, 18:25], 'az', down)  4.57 us
    ppermute x1, starting transfers between devices, on_device(): below = lax.ppermute(own[:, 12:19], 'az', up)  3.99 us
  transfers between devices with their start and end apart: 2, of which 1 were waited for; matrix products, arithmetic and copies ran while one was open for 0% of the time, Pallas kernels for 10%

profile of v1, /device:TPU:65, one launch (start us, length us, event | category | flops | bytes accessed | tf_op | source)
XLA Modules:
  0.0 78.8 jit_solution(4873850738542524325)
XLA Ops:
  0.0 0.0 copy-start
  0.0 1.4 %copy-done = bf16[2,4,24,4096]{3,2,1,0:T(8,128)(2,1)S(1)} copy-done((bf16[2,4,24,4096]{3,2,1,0:T(8,128)(2,1)S(1)}, bf16[2,4,24,4096]{3,2,1,0:T(8,128)(2,1)}, u32[]{:S(2)}) %copy-start) | copy-done | bytes 1572888
  1.4 0.0 copy-start.1
  1.4 1.0 %copy-done.1 = s32[24,4096]{1,0:T(8,128)S(1)} copy-done((s32[24,4096]{1,0:T(8,128)S(1)}, s32[24,4096]{1,0:T(8,128)}, u32[]{:S(2)}) %copy-start.1) | copy-done | bytes 393240
  2.4 0.0 copy-start.2
  2.4 0.8 %copy-done.2 = f32[4,4096]{1,0:T(4,128)S(1)} copy-done((f32[4,4096]{1,0:T(4,128)S(1)}, f32[4,4096]{1,0:T(4,128)}, u32[]{:S(2)}) %copy-start.2) | copy-done | bytes 65560
  3.2 0.0 copy-start.3
  3.2 1.0 %copy-done.3 = bf16[512,512]{1,0:T(8,128)(2,1)S(1)} copy-done((bf16[512,512]{1,0:T(8,128)(2,1)S(1)}, bf16[512,512]{1,0:T(8,128)(2,1)}, u32[]{:S(2)}) %copy-start.3) | copy-done | bytes 524312
  4.3 0.0 copy-start.4
  4.3 1.0 %copy-done.4 = bf16[768,256]{1,0:T(8,128)(2,1)S(1)} copy-done((bf16[768,256]{1,0:T(8,128)(2,1)S(1)}, bf16[768,256]{1,0:T(8,128)(2,1)}, u32[]{:S(2)}) %copy-start.4) | copy-done | bytes 393240
  5.3 0.0 copy-start.5
  5.3 1.0 %copy-done.5 = bf16[768,256]{1,0:T(8,128)(2,1)S(1)} copy-done((bf16[768,256]{1,0:T(8,128)(2,1)S(1)}, bf16[768,256]{1,0:T(8,128)(2,1)}, u32[]{:S(2)}) %copy-start.5) | copy-done | bytes 393240
  6.3 0.0 copy-start.7
  6.3 0.8 %copy-done.7 = f32[4,32,128]{2,1,0:T(8,128)S(1)} copy-done((f32[4,32,128]{2,1,0:T(8,128)S(1)}, f32[4,32,128]{2,1,0:T(8,128)}, u32[]{:S(2)}) %copy-start.7) | copy-done | bytes 65560
  7.1 10.1 %filter_lines.1 = bf16[8,25,32,128]{3,2,1,0:T(8,128)(2,1)S(1)} custom-call(bf16[2,4,24,4096]{3,2,1,0:T(8,128)(2,1)S(1)} %copy-done, f32[4,4096]{1,0:T(4,128)S(1)} %copy-done.2, s32[24,4096]{1,0:T(8,128)S(1)} %copy-done.1, bf16[768,256]{1,0:T(8,128)(2,1)S(1)} %copy-done.5, bf16[768,256]{1,0:T(8,128)(2,1)S(1)} %copy-done.4, f32[4,32,128]{2,1,0:T(8,128)S(1)} %copy-done.7, ...), custom_call_target="tpu_custom_call" | custom-call | flops 4000000000 | bytes 4000000 | tf_op jit(solution)/shard_map/filter_lines/pallas_call | solution.py:262
  17.2 25.9 %all_to_all.5.own = bf16[8,25,32,128]{3,2,1,0:T(8,128)(2,1)S(1)} all-to-all(bf16[8,25,32,128]{3,2,1,0:T(8,128)(2,1)S(1)} %filter_lines.1), channel_id=1, replica_groups=mesh['az'=32,'dr'=8] {'dr'}, dimensions={0} | all-to-all | bytes 3276800 | tf_op jit(solution)/shard_map/all_to_all | solution.py:554
  43.1 0.1 fusion
  43.2 4.0 %collective-permute-start.1 = (bf16[8,7,32,128]{3,2,1,0:T(8,128)(2,1)S(1)}, bf16[8,7,32,128]{3,2,1,0:T(8,128)(2,1)S(1)}, u32[]{:S(2)}, u32[]{:S(2)}) collective-permute-start(bf16[8,7,32,128]{3,2,1,0:T(8,128)(2,1)S(1)} %get-tuple-element.5), channel_id=1, source_target_pairs={{8,0},{16,8},{24,16},{32,24},{40,32},{48,40},{56,48},{64,56},{72,6... | collective-permute-start | bytes 1376264 | tf_op jit(solution)/shard_map/ppermute | solution.py:559
  47.2 0.0 copy-start.6
  47.2 4.6 %collective-permute-start = (bf16[8,7,32,128]{3,2,1,0:T(8,128)(2,1)S(1)}, bf16[8,7,32,128]{3,2,1,0:T(8,128)(2,1)S(1)}, u32[]{:S(2)}, u32[]{:S(2)}) collective-permute-start(bf16[8,7,32,128]{3,2,1,0:T(8,128)(2,1)S(1)} %get-tuple-element.6), channel_id=1, source_target_pairs={{0,8},{8,16},{16,24},{24,32},{32,40},{40,48},{48,56},{56,64},{64,7... | collective-permute-start | bytes 1376264 | tf_op jit(solution)/shard_map/ppermute | solution.py:558
  51.8 8.2 %inner_rows.1.inner = f32[5,2,544,128]{3,2,1,0:T(8,128)S(1)} custom-call(bf16[8,25,32,128]{3,2,1,0:T(8,128)(2,1)S(1)} %all_to_all.5.own), custom_call_target="tpu_custom_call" | custom-call | flops 20000000000 | bytes 4000000 | tf_op jit(solution)/shard_map/inner_rows/pallas_call | solution.py:373
  59.9 0.8 %collective-permute-done.1.below = bf16[8,7,32,128]{3,2,1,0:T(8,128)(2,1)S(1)} collective-permute-done((bf16[8,7,32,128]{3,2,1,0:T(8,128)(2,1)S(1)}, bf16[8,7,32,128]{3,2,1,0:T(8,128)(2,1)S(1)}, u32[]{:S(2)}, u32[]{:S(2)}) %collective-permute-start.1) | collective-permute-done | bytes 458784 | tf_op jit(solution)/shard_map/ppermute | solution.py:559
  60.8 0.0 collective-permute-done.above
  60.8 0.0 copy-done.6
  60.8 18.1 %link_windows.1 = f32[2,6,32,128]{3,2,1,0:T(8,128)} custom-call(bf16[8,25,32,128]{3,2,1,0:T(8,128)(2,1)S(1)} %all_to_all.5.own, bf16[8,7,32,128]{3,2,1,0:T(8,128)(2,1)S(1)} %collective-permute-done.above, bf16[8,7,32,128]{3,2,1,0:T(8,128)(2,1)S(1)} %collective-permute-done.1.below, f32[5,2,544,128]{3,2,1,0:T(8,128)S(1)} %inner_rows.1.inner, ...), custom_call_target="tpu_custom_call" | custom-call | flops 20000000000 | bytes 8000000 | tf_op jit(solution)/shard_map/link_windows/pallas_call | solution.py:532
Async XLA Ops:
  0.0 1.4 %copy-start = (bf16[2,4,24,4096]{3,2,1,0:T(8,128)(2,1)S(1)}, bf16[2,4,24,4096]{3,2,1,0:T(8,128)(2,1)}, u32[]{:S(2)}) copy-start(bf16[2,4,24,4096]{3,2,1,0:T(8,128)(2,1)} %stack.1) | copy-start | bytes 4718596
  1.4 1.0 %copy-start.1 = (s32[24,4096]{1,0:T(8,128)S(1)}, s32[24,4096]{1,0:T(8,128)}, u32[]{:S(2)}) copy-start(s32[24,4096]{1,0:T(8,128)} %mask.1) | copy-start | bytes 1179652
  2.4 0.8 %copy-start.2 = (f32[4,4096]{1,0:T(4,128)S(1)}, f32[4,4096]{1,0:T(4,128)}, u32[]{:S(2)}) copy-start(f32[4,4096]{1,0:T(4,128)} %gains.1) | copy-start | bytes 196612
  3.2 1.0 %copy-start.3 = (bf16[512,512]{1,0:T(8,128)(2,1)S(1)}, bf16[512,512]{1,0:T(8,128)(2,1)}, u32[]{:S(2)}) copy-start(bf16[512,512]{1,0:T(8,128)(2,1)} %constant.13.clone.place) | copy-start | bytes 1572868
  4.3 1.0 %copy-start.4 = (bf16[768,256]{1,0:T(8,128)(2,1)S(1)}, bf16[768,256]{1,0:T(8,128)(2,1)}, u32[]{:S(2)}) copy-start(bf16[768,256]{1,0:T(8,128)(2,1)} %constant.11.clone.inverse) | copy-start | bytes 1179652
  5.3 1.0 %copy-start.5 = (bf16[768,256]{1,0:T(8,128)(2,1)S(1)}, bf16[768,256]{1,0:T(8,128)(2,1)}, u32[]{:S(2)}) copy-start(bf16[768,256]{1,0:T(8,128)(2,1)} %constant.10.clone.forward) | copy-start | bytes 1179652
  6.3 0.8 %copy-start.7 = (f32[4,32,128]{2,1,0:T(8,128)S(1)}, f32[4,32,128]{2,1,0:T(8,128)}, u32[]{:S(2)}) copy-start(f32[4,32,128]{2,1,0:T(8,128)} %constant.12.clone.twist) | copy-start | bytes 196612
  43.2 17.6 %collective-permute-start.1 = (bf16[8,7,32,128]{3,2,1,0:T(8,128)(2,1)S(1)}, bf16[8,7,32,128]{3,2,1,0:T(8,128)(2,1)S(1)}, u32[]{:S(2)}, u32[]{:S(2)}) collective-permute-start(bf16[8,7,32,128]{3,2,1,0:T(8,128)(2,1)S(1)} %get-tuple-element.5), channel_id=1, source_target_pairs={{8,0},{16,8},{24,16},{32,24},{40,32},{48,40},{56,48},{64,56},{72,6... | collective-permute-start | bytes 1376264 | tf_op jit(solution)/shard_map/ppermute | solution.py:559
  47.2 13.6 %copy-start.6 = (bf16[6,128,128]{2,1,0:T(8,128)(2,1)S(1)}, bf16[6,128,128]{2,1,0:T(8,128)(2,1)}, u32[]{:S(2)}) copy-start(bf16[6,128,128]{2,1,0:T(8,128)(2,1)} %constant.14.clone.band) | copy-start | bytes 589828
  47.2 13.6 %collective-permute-start = (bf16[8,7,32,128]{3,2,1,0:T(8,128)(2,1)S(1)}, bf16[8,7,32,128]{3,2,1,0:T(8,128)(2,1)S(1)}, u32[]{:S(2)}, u32[]{:S(2)}) collective-permute-start(bf16[8,7,32,128]{3,2,1,0:T(8,128)(2,1)S(1)} %get-tuple-element.6), channel_id=1, source_target_pairs={{0,8},{8,16},{16,24},{24,32},{32,40},{40,48},{48,56},{56,64},{64,7... | collective-permute-start | bytes 1376264 | tf_op jit(solution)/shard_map/ppermute | solution.py:558

commit v2 on v1

--- a/solution.py
+++ b/solution.py
@@ -1,3 +1,4 @@
+import functools
 import math
 
 import jax
@@ -8,29 +9,30 @@
 from jax.experimental.pallas import tpu as pltpu
 from jax.sharding import PartitionSpec as P
 
+
 ITERS = 4
 BETA_LOAD = 1.0
 PROJ_LOAD = 1.0
 
 DATES = 32
-LINES = 24
 RG = 4096
 TILES = 8
 HALO = 6
 PLANES = 32
 HERE = 4
-ROWS = HERE * LINES
-SLOTS = LINES + 1
-TAIL_SLOT = 18
+FIRST, SECOND = (0, 16), (8,)
 SHIFTS = 17
-PAIRS = SHIFTS * DATES
+PAIRS = (SHIFTS + 1) * DATES
 WRAP = 48
 
 
-def slot_of(line):
-    if line < 6:
-        return 12 + line
-    return line - 6 if line < 18 else line + 1
+def slots_of(blocks):
+    if blocks == FIRST:
+        order = [6, 7, 16, 17, 0, 1, 2, 3, 4, 5, None, 18, 19, 20, 21, 22, 23]
+    else:
+        order = list(range(8, 16)) + [None]
+    lines = [block + i for block in blocks for i in range(8)]
+    return [order.index(line) for line in lines], order.index(None)
 
 
 def split_np(table):
@@ -60,12 +62,17 @@
 
 
 def tail_band():
+    near = np.zeros((128, 128), np.float32)
+    for block in range(128):
+        near[block, max(block - 3, 0) : block + 1] = 1.0
     band = np.zeros((6, 128, 128), np.float32)
     for row in range(6):
         for line in range(4 * row, 4 * row + 16):
             for block in range(3):
                 band[row, line * 3 + block, 125 + block :] = 1.0
-    return band.astype(jnp.bfloat16)
+    both = np.concatenate(list(band), axis=1)
+    both = np.concatenate([both, both], axis=0).astype(jnp.bfloat16)
+    return np.concatenate([near, near], axis=0).astype(jnp.bfloat16), both
 
 
 def cmul(value, cos, sin):
@@ -128,32 +135,52 @@
     )
 
 
-GROUP = 4
-
-
 def filter_kernel(
-    stack, gains, mask, forward, inverse, twist, place, out,
+    blocks, group, stack, gains, mask, forward, inverse, twist, place, out,
+    raw, gains_in, mask_in, forward_in, inverse_in, twist_in, place_in, sem,
     first, spec, hold, held, gain, weights, lines_out,
 ):
+    count = len(blocks)
+    lines_here = 8 * count
+    rows_here = HERE * lines_here
+    line_slots, tail_slot = slots_of(blocks)
+    copies = {}
+    for i, block in enumerate(blocks):
+        for c in range(2):
+            for d in range(HERE):
+                index = (c * HERE + d) * count + i
+                copies[c, d, i] = pltpu.make_async_copy(
+                    stack.at[c, d, pl.ds(block, 8)], raw.at[c, d * count + i], sem.at[index]
+                )
+        copies["mask", i] = pltpu.make_async_copy(
+            mask.at[pl.ds(block, 8)], mask_in.at[pl.ds(8 * i, 8)], sem.at[8 * count + i]
+        )
+    others = (
+        ("gains", gains, gains_in),
+        ("twist", twist, twist_in),
+        ("forward", forward, forward_in),
+        ("inverse", inverse, inverse_in),
+        ("place", place, place_in),
+    )
+    for i, (name, source, target) in enumerate(others):
+        copies[name] = pltpu.make_async_copy(source, target, sem.at[9 * count + i])
+    for copy in copies.values():
+        copy.start()
     lanes = lax.broadcasted_iota(jnp.int32, (8, 128), 1)
-    for c in range(2):
-        for d in range(HERE):
-            for n in range(PLANES):
-                first[c, n, d * LINES : (d + 1) * LINES] = stack[
-                    c, d, :, n * 128 : (n + 1) * 128
-                ].astype(jnp.float32)
+    copies["gains"].wait()
     for n in range(PLANES):
-        four = gains[:, n * 128 : (n + 1) * 128]
+        four = gains_in[:, n * 128 : (n + 1) * 128]
         for d in range(HERE):
             gain[d, n : n + 1] = four[d : d + 1]
     for d in range(HERE):
         turned = jnp.transpose(gain[d])
         gain[d] = jnp.concatenate([turned[32 * w : 32 * w + 32] for w in range(4)], axis=1)
-    for block in range(LINES // 8):
-        rows = slice(8 * block, 8 * block + 8)
-        before = pltpu.roll(mask[rows, RG - 128 :].astype(jnp.float32), HALO, 1)
+    for i in range(count):
+        copies["mask", i].wait()
+        rows = slice(8 * i, 8 * i + 8)
+        before = pltpu.roll(mask_in[rows, RG - 128 :].astype(jnp.float32), HALO, 1)
         for n in range(PLANES):
-            now = pltpu.roll(mask[rows, n * 128 : (n + 1) * 128].astype(jnp.float32), HALO, 1)
+            now = pltpu.roll(mask_in[rows, n * 128 : (n + 1) * 128].astype(jnp.float32), HALO, 1)
             joined = jnp.where(lanes < HALO, before, now)
             if n == 0:
                 weights[PLANES, rows] = jnp.where(lanes < HALO, joined, 0.0)
@@ -168,35 +195,49 @@
             spec[0, q, rows] = re
             spec[1, q, rows] = im
 
-        dft_planes(lambda n: (first[0, n, rows], first[1, n, rows]), hold, store, -1)
-        return carry
-
-    lax.fori_loop(0, ROWS // 8, ahead, 0)
-    steps = PLANES // GROUP
+        for c in range(2):
+            pltpu.make_async_copy(
+                stack.at[0, 0, pl.ds(0, 8)], raw.at[c, block], sem.at[c * HERE * count + block]
+            ).wait()
+
+        def load(n):
+            lanes = slice(n * 128, (n + 1) * 128)
+            return (
+                raw[0, block, :, lanes].astype(jnp.float32),
+                raw[1, block, :, lanes].astype(jnp.float32),
+            )
+
+        dft_planes(load, hold, store, -1)
+        return carry
+
+    lax.fori_loop(0, rows_here // 8, ahead, 0)
+    steps = PLANES // group
+    for name in ("twist", "forward", "inverse"):
+        copies[name].wait()
 
     def middle(step, carry):
-        now = jnp.minimum(step, steps - 1) * GROUP
-        past = jnp.maximum(step - 1, 0) * GROUP
+        now = jnp.minimum(step, steps - 1) * group
+        past = jnp.maximum(step - 1, 0) * group
         parts = []
-        for i in range(GROUP):
-            tc = twist[0, pl.ds(now + i, 1), :]
-            ts = twist[1, pl.ds(now + i, 1), :]
+        for i in range(group):
+            tc = twist_in[0, pl.ds(now + i, 1), :]
+            ts = twist_in[1, pl.ds(now + i, 1), :]
             re, im = spec[0, now + i], spec[1, now + i]
             parts.append(jnp.concatenate([re * tc + im * ts, im * tc - re * ts], axis=1))
-        back = dot3(held[lax.rem(step + 1, 2)], inverse[...])
-        found = dot3(jnp.concatenate(parts, axis=0), forward[...])
-        for i in range(GROUP):
+        back = dot3(held[lax.rem(step + 1, 2)], inverse_in[...])
+        found = dot3(jnp.concatenate(parts, axis=0), forward_in[...])
+        for i in range(group):
             for d in range(HERE):
                 row = gain[d, pl.ds(now + i, 1), :]
-                begin = i * ROWS + d * LINES
-                held[lax.rem(step, 2), begin : begin + LINES] = found[
-                    begin : begin + LINES
+                begin = i * rows_here + d * lines_here
+                held[lax.rem(step, 2), begin : begin + lines_here] = found[
+                    begin : begin + lines_here
                 ] * jnp.concatenate([row, row], axis=1)
-        for i in range(GROUP):
-            tc = twist[2, pl.ds(past + i, 1), :]
-            ts = twist[3, pl.ds(past + i, 1), :]
-            re = back[i * ROWS : (i + 1) * ROWS, :128]
-            im = back[i * ROWS : (i + 1) * ROWS, 128:]
+        for i in range(group):
+            tc = twist_in[2, pl.ds(past + i, 1), :]
+            ts = twist_in[3, pl.ds(past + i, 1), :]
+            re = back[i * rows_here : (i + 1) * rows_here, :128]
+            im = back[i * rows_here : (i + 1) * rows_here, 128:]
             first[0, past + i] = re * tc - im * ts
             first[1, past + i] = im * tc + re * ts
         return carry
@@ -205,8 +246,8 @@
 
     def behind(block, carry):
         rows = pl.ds(pl.multiple_of(block * 8, 8), 8)
-        to_im = pl.ds(pl.multiple_of(block * 8 + ROWS, 8), 8)
-        lines = pl.ds(pl.multiple_of(lax.rem(block, 3) * 8, 8), 8)
+        to_im = pl.ds(pl.multiple_of(block * 8 + rows_here, 8), 8)
+        lines = pl.ds(pl.multiple_of(lax.rem(block, count) * 8, 8), 8)
 
         def store(n, re, im):
             weight = weights[n, lines]
@@ -220,30 +261,32 @@
         dft_planes(lambda q: (first[0, q, rows], first[1, q, rows]), hold, store, 1)
         return carry
 
-    lax.fori_loop(0, ROWS // 8, behind, 0)
+    lax.fori_loop(0, rows_here // 8, behind, 0)
+    copies["place"].wait()
 
     def gather(plane):
         return jnp.concatenate(
-            [lines_out[plane, pl.ds(line, 8, stride=LINES), :] for line in range(LINES)], axis=0
+            [lines_out[plane, pl.ds(line, 8, stride=lines_here), :] for line in range(lines_here)],
+            axis=0,
         )
 
     def put_tail(slot, found):
         tails = []
         for p in range(4):
             tail = jnp.zeros((8, 128), jnp.float32)
-            for line in range(LINES):
+            for line in range(lines_here):
                 part = found[line * 8 : line * 8 + 8, p * 128 : p * 128 + 128]
                 if line:
                     part = pltpu.roll(part, 3 * line, 1)
                 tail = jnp.where(lanes >= 3 * line, part, tail)
-            tails.append(jnp.where(lanes < 3 * LINES, tail, 0.0))
-        out[slot, TAIL_SLOT] = jnp.concatenate(tails, axis=0).astype(jnp.bfloat16)
+            tails.append(jnp.where(lanes < 3 * lines_here, tail, 0.0))
+        out[slot, tail_slot] = jnp.concatenate(tails, axis=0).astype(jnp.bfloat16)
 
     def tile(t, carry):
         left = jnp.concatenate([gather(4 * t + v) for v in range(4)], axis=1).astype(jnp.bfloat16)
-        found = jnp.dot(left, place[...], preferred_element_type=jnp.float32)
-        for line in range(LINES):
-            out[t, slot_of(line)] = jnp.concatenate(
+        found = jnp.dot(left, place_in[...], preferred_element_type=jnp.float32)
+        for line in range(lines_here):
+            out[t, line_slots[line]] = jnp.concatenate(
                 [found[line * 8 : line * 8 + 8, p * 128 : p * 128 + 128] for p in range(4)],
                 axis=0,
             ).astype(jnp.bfloat16)
@@ -252,30 +295,42 @@
 
     lax.fori_loop(0, TILES, tile, 0)
     found = jnp.dot(
-        gather(PLANES).astype(jnp.bfloat16), place[:128], preferred_element_type=jnp.float32
+        gather(PLANES).astype(jnp.bfloat16), place_in[:128], preferred_element_type=jnp.float32
     )
     put_tail(TILES - 1, found)
 
 
-def filter_lines(stack, gains, mask):
+def filter_lines(stack, gains, mask, blocks, group):
     forward, inverse, twist, place = tables()
+    count = len(blocks)
+    rows = HERE * 8 * count
     return pl.pallas_call(
-        filter_kernel,
-        out_shape=jax.ShapeDtypeStruct((TILES, SLOTS, 32, 128), jnp.bfloat16),
+        functools.partial(filter_kernel, blocks, group),
+        out_shape=jax.ShapeDtypeStruct((TILES, 8 * count + 1, 32, 128), jnp.bfloat16),
+        in_specs=[pl.BlockSpec(memory_space=pltpu.MemorySpace.HBM)] * 7,
         scratch_shapes=[
-            pltpu.VMEM((2, PLANES, ROWS, 128), jnp.float32),
-            pltpu.VMEM((2, PLANES, ROWS, 128), jnp.float32),
+            pltpu.VMEM((2, HERE * count, 8, RG), jnp.bfloat16),
+            pltpu.VMEM((HERE, RG), jnp.float32),
+            pltpu.VMEM((8 * count, RG), jnp.int32),
+            pltpu.VMEM((768, 256), jnp.bfloat16),
+            pltpu.VMEM((768, 256), jnp.bfloat16),
+            pltpu.VMEM((4, PLANES, 128), jnp.float32),
+            pltpu.VMEM((512, 512), jnp.bfloat16),
+            pltpu.SemaphoreType.DMA((9 * count + 5,)),
+            pltpu.VMEM((2, PLANES, rows, 128), jnp.float32),
+            pltpu.VMEM((2, PLANES, rows, 128), jnp.float32),
             pltpu.VMEM((2, PLANES, 8, 128), jnp.float32),
-            pltpu.VMEM((2, GROUP * ROWS, 256), jnp.float32),
+            pltpu.VMEM((2, group * rows, 256), jnp.float32),
             pltpu.VMEM((HERE, PLANES, 128), jnp.float32),
-            pltpu.VMEM((PLANES + 1, LINES, 128), jnp.float32),
-            pltpu.VMEM((PLANES + 1, 2 * ROWS, 128), jnp.float32),
+            pltpu.VMEM((PLANES + 1, 8 * count, 128), jnp.float32),
+            pltpu.VMEM((PLANES + 1, 2 * rows, 128), jnp.float32),
         ],
-        compiler_params=pltpu.CompilerParams(vmem_limit_bytes=24 << 20),
+        compiler_params=pltpu.CompilerParams(
+            vmem_limit_bytes=(60 if blocks == FIRST else 24) << 20
+        ),
         cost_estimate=pl.CostEstimate(
-            flops=4_000_000_000, bytes_accessed=4_000_000, transcendentals=0
+            flops=2_000_000_000 * count, bytes_accessed=2_000_000, transcendentals=0
         ),
-        name="filter_lines",
     )(stack, gains, mask, forward, inverse, twist, place)
 
 
@@ -319,16 +374,23 @@
         group = index // 2
         own = pl.ds(pl.multiple_of(group * 8, 8), 8)
         begin = pl.multiple_of(group * 8 + lax.rem(index, 2) * 8, 8)
-        totals = [[None] * 3 for _ in range(WIDTH)]
-        for step in range(count):
-            plane = base + step
-            mine = (z_sum[plane, own], z_re[plane, own], z_im[plane, own])
-            for i in range(WIDTH):
-                other = pl.ds(begin + 1 + i, 8)
-                others = (z_re[plane, other], z_sum[plane, other], z_dif[plane, other])
-                for k in range(3):
-                    term = others[k] * mine[k]
-                    totals[i][k] = term if step == 0 else totals[i][k] + term
+        unit = min(8, count)
+
+        def some(chunk, totals):
+            totals = [list(totals[3 * i : 3 * i + 3]) for i in range(WIDTH)]
+            for step in range(unit):
+                plane = base + chunk * unit + step
+                mine = (z_sum[plane, own], z_re[plane, own], z_im[plane, own])
+                for i in range(WIDTH):
+                    other = pl.ds(begin + 1 + i, 8)
+                    others = (z_re[plane, other], z_sum[plane, other], z_dif[plane, other])
+                    for k in range(3):
+                        totals[i][k] = totals[i][k] + others[k] * mine[k]
+            return tuple(t for total in totals for t in total)
+
+        zero = jnp.zeros((8, 128), jnp.float32)
+        totals = lax.fori_loop(0, count // unit, some, (zero,) * (3 * WIDTH))
+        totals = [totals[3 * i : 3 * i + 3] for i in range(WIDTH)]
         for i in range(WIDTH):
             one, two, three = totals[i]
             spot = (lax.rem(index, 2) * 8 + 1 + i) * DATES + group * 8
@@ -359,54 +421,65 @@
     lax.fori_loop(0, count, one_row, 0)
 
 
-def inner_kernel(own, sums, z_re, z_im, z_sum, z_dif):
-    fields = (z_re, z_im, z_sum, z_dif)
-    put, run = unpacker(fields)
-    run(own, 14, 0, 4)
-    run(own, 0, 4, 12)
-    run(own, 19, 16, 4)
-    gram_rows(fields, sums, 5, 0, 0)
-
-
-def inner_rows(own):
-    field = pltpu.VMEM((80, WRAP, 128), jnp.float32)
+def early_kernel(own, sums, *fields):
+    _, run = unpacker(fields)
+    run(own, 6, 0, 4)
+    run(own, 11, 4, 4)
+    gram_rows(fields, sums, 2, 0, 0)
+
+
+def inner_kernel(own, rest, sums, *fields):
+    _, run = unpacker(fields)
+    run(own, 0, 0, 2)
+    run(rest, 0, 2, 8)
+    run(own, 2, 10, 2)
+    gram_rows(fields, sums, 3, 0, 0)
+
+
+def own_rows(kernel, count, *chunks):
+    field = pltpu.VMEM((count * 16, WRAP, 128), jnp.float32)
     return pl.pallas_call(
-        inner_kernel,
-        out_shape=jax.ShapeDtypeStruct((5, 2, PAIRS, 128), jnp.float32),
+        kernel,
+        out_shape=jax.ShapeDtypeStruct((count, 2, PAIRS, 128), jnp.float32),
         scratch_shapes=[field] * 4,
-        compiler_params=pltpu.CompilerParams(vmem_limit_bytes=24 << 20),
+        compiler_params=pltpu.CompilerParams(vmem_limit_bytes=16 << 20),
         cost_estimate=pl.CostEstimate(
-            flops=20_000_000_000, bytes_accessed=4_000_000, transcendentals=0
+            flops=3_000_000_000 * count, bytes_accessed=2_000_000, transcendentals=0
         ),
-        name="inner_rows",
-    )(own)
+    )(*chunks)
 
 
 def link_kernel(
-    own, above, below, inner, band, out, z_re, z_im, z_sum, z_dif, sums, tails, extra, cov, vec
+    own, rest, above, below, early, inner, near, band, out,
+    z_re, z_im, z_sum, z_dif, sums, tails, extra, cov, vec,
 ):
     fields = (z_re, z_im, z_sum, z_dif)
     lanes = lax.broadcasted_iota(jnp.int32, (8, 128), 1)
     put, run = unpacker(fields)
     run(above, 1, 0, 6)
-    run(own, 12, 6, 2)
-    run(own, 23, 8, 2)
+    run(own, 4, 6, 2)
+    run(own, 15, 8, 2)
     run(below, 0, 10, 6)
     for group in range(4):
         pieces = []
         for source in (2 * group, 2 * group + 1):
-            mid = own[source, TAIL_SLOT].astype(jnp.float32)
+            mine = own[source, 10].astype(jnp.float32)
+            others = rest[source, 8].astype(jnp.float32)
             up = above[source, 0].astype(jnp.float32)
             down = below[source, 6].astype(jnp.float32)
             piece = []
             for p in range(4):
                 cut = slice(8 * p, 8 * p + 8)
-                value = pltpu.roll(mid[cut], 18, 1)
-                value = jnp.where(lanes < 18, pltpu.roll(up[cut], 128 - 54, 1), value)
-                value = jnp.where(
-                    (lanes >= 90) & (lanes < 108), pltpu.roll(down[cut], 90, 1), value
-                )
-                piece.append(value)
+                value = jnp.zeros((8, 128), jnp.float32)
+                for part, turn, begin in (
+                    (up, 128 - 30, 0),
+                    (mine, 18, 18),
+                    (others, 42, 42),
+                    (mine, 42, 66),
+                    (down, 90, 90),
+                ):
+                    value = jnp.where(lanes >= begin, pltpu.roll(part[cut], turn, 1), value)
+                piece.append(jnp.where(lanes < 108, value, 0.0))
             pieces.append(piece)
         for p in range(4):
             put(64 + p, group, pieces[0][p], pieces[1][p])
@@ -417,47 +490,37 @@
     gram(fields, 64, 4, store_tail)
     tails[1, 0:DATES] = jnp.zeros((DATES, 128), jnp.float32)
     gram_rows(fields, sums, 4, 0, 0)
-
-    def add_tail(a, carry):
+    for c in range(2):
+        high, low = split(tails[c])
+        extra[c] = jnp.dot(
+            jnp.concatenate([high, low], axis=1), band[...], preferred_element_type=jnp.float32
+        )
+
+    def windows(step, carry):
+        size = 2 * DATES
+        begin = pl.multiple_of(step * size, size)
+        spot = pl.ds(begin, size)
+        twice = pl.multiple_of(step * 2 * size, 2 * size)
         for c in range(2):
-            high, low = split(tails[c])
-            extra[a, c] = jnp.dot(
-                jnp.concatenate([high, low], axis=1),
-                jnp.concatenate([band[a], band[a]], axis=0),
-                preferred_element_type=jnp.float32,
+            rowsum = [sums[r, c, spot] for r in (0, 1)]
+            rowsum += [early[0, c, spot]] + [inner[r, c, spot] for r in range(3)]
+            rowsum += [early[1, c, spot]]
+            rowsum += [sums[r, c, spot] for r in (2, 3)]
+            pairs = [rowsum[r] + rowsum[r + 1] for r in range(8)]
+            value = jnp.concatenate([pairs[a] + pairs[a + 2] for a in range(6)], axis=0)
+            high, low = split(value)
+            found = jnp.dot(
+                jnp.concatenate([high, low], axis=1), near[...], preferred_element_type=jnp.float32
             )
-        return carry
-
-    lax.fori_loop(0, 6, add_tail, 0)
-
-    def windows(c, s, group):
-        spot = s * DATES + group * 8
-        spot = spot if isinstance(spot, int) else pl.multiple_of(spot, 8)
-        where = pl.ds(spot, 8)
-        rowsum = [sums[r, c, where] for r in (0, 1)]
-        rowsum += [inner[r, c, where] for r in range(5)]
-        rowsum += [sums[r, c, where] for r in (2, 3)]
-        pairs = [rowsum[r] + rowsum[r + 1] for r in range(8)]
-        twice = s * 2 * DATES + group * 8
-        twice = twice if isinstance(twice, int) else pl.multiple_of(twice, 8)
-        for a in range(6):
-            value = pairs[a] + pairs[a + 2]
-            value = value + jnp.where(lanes < 127, pltpu.roll(value, 127, 1), 0.0)
-            value = value + jnp.where(lanes < 126, pltpu.roll(value, 126, 1), 0.0)
-            value = value + extra[a, c, where]
-            cov[a, c, pl.ds(twice, 8)] = value
-            cov[a, c, pl.ds(twice + DATES, 8)] = value
-
-    for group in range(4):
-        windows(0, 0, group)
-
-    def shift_windows(s, carry):
-        for group in range(4):
-            windows(0, s, group)
-            windows(1, s, group)
-        return carry
-
-    lax.fori_loop(1, SHIFTS, shift_windows, 0)
+            for a in range(6):
+                full = found[a * size : (a + 1) * size] + extra[c, spot, a * 128 : a * 128 + 128]
+                for i in range(2):
+                    half = full[i * DATES : (i + 1) * DATES]
+                    cov[a, c, pl.ds(twice + 2 * i * DATES, DATES)] = half
+                    cov[a, c, pl.ds(twice + (2 * i + 1) * DATES, DATES)] = half
+        return carry
+
+    lax.fori_loop(0, (SHIFTS + 1) // 2, windows, 0)
 
     def put_vec(c, group, value):
         for copy in range(3):
@@ -527,7 +590,7 @@
     return sums[0] + sums[1]
 
 
-def link_windows(own, above, below, inner):
+def link_windows(own, rest, above, below, early, inner):
     field = pltpu.VMEM((68, WRAP, 128), jnp.float32)
     found = pl.pallas_call(
         link_kernel,
@@ -536,7 +599,7 @@
         + [
             pltpu.VMEM((4, 2, PAIRS, 128), jnp.float32),
             pltpu.VMEM((2, PAIRS, 128), jnp.float32),
-            pltpu.VMEM((6, 2, PAIRS, 128), jnp.float32),
+            pltpu.VMEM((2, PAIRS, 6 * 128), jnp.float32),
             pltpu.VMEM((6, 2, 2 * PAIRS, 128), jnp.float32),
             pltpu.VMEM((2, 3 * DATES, 128), jnp.float32),
         ],
@@ -545,20 +608,25 @@
             flops=20_000_000_000, bytes_accessed=8_000_000, transcendentals=0
         ),
         name="link_windows",
-    )(own, above, below, inner, tail_band())
+    )(own, rest, above, below, early, inner, *tail_band())
     return jnp.transpose(found, (0, 2, 1, 3))
 
 
 def on_device(stack, range_filter, scatter_mask):
-    tiles = filter_lines(stack, range_filter, scatter_mask)
-    own = lax.all_to_all(tiles, "dr", split_axis=0, concat_axis=0, tiled=True)
+    def move(tiles):
+        return lax.all_to_all(tiles, "dr", split_axis=0, concat_axis=0, tiled=True)
+
+    own = move(filter_lines(stack, range_filter, scatter_mask, FIRST, 4))
+    tiles = filter_lines(stack, range_filter, scatter_mask, SECOND, 8)
+    rest = move(tiles)
     count = lax.axis_size("az")
     down = [(i, i + 1) for i in range(count - 1)]
     up = [(i + 1, i) for i in range(count - 1)]
-    above = lax.ppermute(own[:, 18:25], "az", down)
-    below = lax.ppermute(own[:, 12:19], "az", up)
-    inner = inner_rows(own)
-    return link_windows(own, above, below, inner)
+    above = lax.ppermute(own[:, 10:17], "az", down)
+    below = lax.ppermute(own[:, 4:11], "az", up)
+    early = own_rows(early_kernel, 2, own)
+    inner = own_rows(inner_kernel, 3, own, rest)
+    return link_windows(own, rest, above, below, early, inner)
 
 
 def solution(mesh):

time: 79.7 us -> 73.6 us (0.923)
  the two profiles are of different devices: /device:TPU:65 before, /device:TPU:32 now
where the time goes in v2:
time: 73.6 us; the launch traced here: 73.2 us
  Pallas kernels  40.6 us (55%)
  waiting for transfers between devices  15.7 us (21%)
  starting transfers between devices  13.8 us (19%)
  local copies, waits for them, and re-layouts  2.99 us (4%)
    pallas_call x2, Pallas kernels, filter_lines(): pl.pallas_call(functools.partial(filter_kernel, blocks, group), out_shape...  18.5 us
    all_to_all x2, waiting for transfers between devices, move(): return lax.all_to_all(tiles, 'dr', split_axis=0, concat_axis=0, tiled=True)  15.7 us
    pallas_call x1, Pallas kernels, link_windows(): pl.pallas_call(link_kernel, out_shape=jax.ShapeDtypeStruct((2, 6, DATES,...  14.9 us
    all_to_all x2, starting transfers between devices, move(): return lax.all_to_all(tiles, 'dr', split_axis=0, concat_axis=0, tiled=True)  8.99 us
    pallas_call x2, Pallas kernels, own_rows(): pl.pallas_call(kernel, out_shape=jax.ShapeDtypeStruct((count, 2, PAIRS, 1...  7.16 us
    unnamed x18, local copies, waits for them, and re-layouts  2.91 us
    ppermute x1, starting transfers between devices, on_device(): below = lax.ppermute(own[:, 4:11], 'az', up)  2.88 us
    ppermute x1, starting transfers between devices, on_device(): above = lax.ppermute(own[:, 10:17], 'az', down)  1.92 us
  transfers between devices with their start and end apart: 4, of which 2 were waited for; matrix products, arithmetic and copies ran while one was open for 0% of the time, Pallas kernels for 20%

profile of v2, /device:TPU:32, one launch (start us, length us, event | category | flops | bytes accessed | tf_op | source)
XLA Modules:
  0.0 73.2 jit_solution(5883469324781553826)
XLA Ops:
  0.0 0.0 copy-start.5
  0.0 10.7 %shard_map.127 = bf16[8,17,32,128]{3,2,1,0:T(8,128)(2,1)} custom-call(bf16[2,4,24,4096]{3,2,1,0:T(8,128)(2,1)} %stack.3, f32[4,4096]{1,0:T(4,128)} %gains.3, s32[24,4096]{1,0:T(8,128)} %mask.3, bf16[768,256]{1,0:T(8,128)(2,1)} %constant.12.clone.forward, bf16[768,256]{1,0:T(8,128)(2,1)} %constant.13.clone.inverse, f32[4,32,128]{2,1,0:T(8,128)} %constant.14.clone.twist, ...), custom_call_target="tpu_custom_call" | custom-call | flops 4000000000 | bytes 2000000 | tf_op jit(solution)/shard_map/pallas_call | solution.py:307
  10.7 0.0 copy-start
  10.7 0.0 copy-start.1
  10.7 0.0 copy-start.2
  10.7 5.5 %all-to-all-start = ((bf16[8,17,32,128]{3,2,1,0:T(8,128)(2,1)}), bf16[8,17,32,128]{3,2,1,0:T(8,128)(2,1)S(1)}, u32[]{:S(2)}, u32[]{:S(2)}) async-start(bf16[8,17,32,128]{3,2,1,0:T(8,128)(2,1)} %shard_map.127), calls=%async_computation | async-start | bytes 2228224 | tf_op jit(solution)/shard_map/all_to_all | solution.py:617
  16.2 0.0 copy-done.5
  16.2 0.0 copy-done
  16.2 0.0 copy-done.1
  16.2 0.0 copy-done.2
  16.2 0.0 copy-start.3
  16.2 1.0 %copy-done.3 = bf16[512,512]{1,0:T(8,128)(2,1)S(1)} copy-done((bf16[512,512]{1,0:T(8,128)(2,1)S(1)}, bf16[512,512]{1,0:T(8,128)(2,1)}, u32[]{:S(2)}) %copy-start.3) | copy-done | bytes 524312
  17.2 0.0 copy-start.6
  17.2 1.0 %copy-done.6 = bf16[768,256]{1,0:T(8,128)(2,1)S(1)} copy-done((bf16[768,256]{1,0:T(8,128)(2,1)S(1)}, bf16[768,256]{1,0:T(8,128)(2,1)}, u32[]{:S(2)}) %copy-start.6) | copy-done | bytes 393240
  18.2 0.0 copy-start.8
  18.2 0.8 %copy-done.8 = f32[4,32,128]{2,1,0:T(8,128)S(1)} copy-done((f32[4,32,128]{2,1,0:T(8,128)S(1)}, f32[4,32,128]{2,1,0:T(8,128)}, u32[]{:S(2)}) %copy-start.8) | copy-done | bytes 65560
  19.1 7.8 %shard_map.128 = bf16[8,9,32,128]{3,2,1,0:T(8,128)(2,1)} custom-call(bf16[2,4,24,4096]{3,2,1,0:T(8,128)(2,1)S(1)} %copy-done, f32[4,4096]{1,0:T(4,128)S(1)} %copy-done.2, s32[24,4096]{1,0:T(8,128)S(1)} %copy-done.1, bf16[768,256]{1,0:T(8,128)(2,1)S(1)} %copy-done.6, bf16[768,256]{1,0:T(8,128)(2,1)S(1)} %copy-done.5, f32[4,32,128]{2,1,0:T(8,128)S(1)} %copy-done.8, ...), custom_call_target="tpu_custom_call" | custom-call | flops 2000000000 | bytes 2000000 | tf_op jit(solution)/shard_map/pallas_call | solution.py:307
  26.9 6.2 %all-to-all-done.own = bf16[8,17,32,128]{3,2,1,0:T(8,128)(2,1)S(1)} async-done(((bf16[8,17,32,128]{3,2,1,0:T(8,128)(2,1)}), bf16[8,17,32,128]{3,2,1,0:T(8,128)(2,1)S(1)}, u32[]{:S(2)}, u32[]{:S(2)}) %all-to-all-start) | async-done | bytes 1114144 | tf_op jit(solution)/shard_map/all_to_all | solution.py:617
  33.1 3.5 %all-to-all-start.1 = ((bf16[8,9,32,128]{3,2,1,0:T(8,128)(2,1)}), bf16[8,9,32,128]{3,2,1,0:T(8,128)(2,1)S(1)}, u32[]{:S(2)}, u32[]{:S(2)}) async-start(bf16[8,9,32,128]{3,2,1,0:T(8,128)(2,1)} %shard_map.128), calls=%async_computation.1 | async-start | bytes 1179648 | tf_op jit(solution)/shard_map/all_to_all | solution.py:617
  36.6 0.1 fusion
  36.7 2.9 %collective-permute-start.1 = (bf16[8,7,32,128]{3,2,1,0:T(8,128)(2,1)S(1)}, bf16[8,7,32,128]{3,2,1,0:T(8,128)(2,1)S(1)}, u32[]{:S(2)}, u32[]{:S(2)}) collective-permute-start(bf16[8,7,32,128]{3,2,1,0:T(8,128)(2,1)S(1)} %get-tuple-element.5), channel_id=1, source_target_pairs={{8,0},{16,8},{24,16},{32,24},{40,32},{48,40},{56,48},{64,56},{72,6... | collective-permute-start | bytes 1376264 | tf_op jit(solution)/shard_map/ppermute | solution.py:626
  39.6 1.9 %collective-permute-start = (bf16[8,7,32,128]{3,2,1,0:T(8,128)(2,1)S(1)}, bf16[8,7,32,128]{3,2,1,0:T(8,128)(2,1)S(1)}, u32[]{:S(2)}, u32[]{:S(2)}) collective-permute-start(bf16[8,7,32,128]{3,2,1,0:T(8,128)(2,1)S(1)} %get-tuple-element.6), channel_id=1, source_target_pairs={{0,8},{8,16},{16,24},{24,32},{32,40},{40,48},{48,56},{56,64},{64,7... | collective-permute-start | bytes 1376264 | tf_op jit(solution)/shard_map/ppermute | solution.py:625
  41.6 9.5 %all-to-all-done.1.rest = bf16[8,9,32,128]{3,2,1,0:T(8,128)(2,1)S(1)} async-done(((bf16[8,9,32,128]{3,2,1,0:T(8,128)(2,1)}), bf16[8,9,32,128]{3,2,1,0:T(8,128)(2,1)S(1)}, u32[]{:S(2)}, u32[]{:S(2)}) %all-to-all-start.1) | async-done | bytes 589856 | tf_op jit(solution)/shard_map/all_to_all | solution.py:617
  51.0 4.3 %shard_map.130.inner = f32[3,2,576,128]{3,2,1,0:T(8,128)S(1)} custom-call(bf16[8,17,32,128]{3,2,1,0:T(8,128)(2,1)S(1)} %all-to-all-done.own, bf16[8,9,32,128]{3,2,1,0:T(8,128)(2,1)S(1)} %all-to-all-done.1.rest), custom_call_target="tpu_custom_call" | custom-call | flops 8999999488 | bytes 2000000 | tf_op jit(solution)/shard_map/pallas_call | solution.py:441
  55.3 0.0 copy-start.4
  55.3 0.0 copy-start.7
  55.4 2.9 %shard_map.129.early = f32[2,2,576,128]{3,2,1,0:T(8,128)S(1)} custom-call(bf16[8,17,32,128]{3,2,1,0:T(8,128)(2,1)S(1)} %all-to-all-done.own), custom_call_target="tpu_custom_call" | custom-call | flops 6000000000 | bytes 2000000 | tf_op jit(solution)/shard_map/pallas_call | solution.py:441
  58.2 0.0 collective-permute-done.1.below
  58.2 0.0 collective-permute-done.above
  58.2 0.0 copy-done.4
  58.3 0.0 copy-done.7
  58.3 14.9 %link_windows.1 = f32[2,6,32,128]{3,2,1,0:T(8,128)} custom-call(bf16[8,17,32,128]{3,2,1,0:T(8,128)(2,1)S(1)} %all-to-all-done.own, bf16[8,9,32,128]{3,2,1,0:T(8,128)(2,1)S(1)} %all-to-all-done.1.rest, bf16[8,7,32,128]{3,2,1,0:T(8,128)(2,1)S(1)} %collective-permute-done.above, bf16[8,7,32,128]{3,2,1,0:T(8,128)(2,1)S(1)} %collective-permute-done.1.below, ...), custom_call_target="tpu_custom_call" | custom-call | flops 20000000000 | bytes 8000000 | tf_op jit(solution)/shard_map/link_windows/pallas_call | solution.py:595
Async XLA Ops:
  0.0 16.2 %copy-start.5 = (bf16[768,256]{1,0:T(8,128)(2,1)S(1)}, bf16[768,256]{1,0:T(8,128)(2,1)}, u32[]{:S(2)}) copy-start(bf16[768,256]{1,0:T(8,128)(2,1)} %constant.13.clone.inverse) | copy-start | bytes 1179652
  10.7 5.5 %copy-start = (bf16[2,4,24,4096]{3,2,1,0:T(8,128)(2,1)S(1)}, bf16[2,4,24,4096]{3,2,1,0:T(8,128)(2,1)}, u32[]{:S(2)}) copy-start(bf16[2,4,24,4096]{3,2,1,0:T(8,128)(2,1)} %stack.3) | copy-start | bytes 4718596
  10.7 5.5 %copy-start.1 = (s32[24,4096]{1,0:T(8,128)S(1)}, s32[24,4096]{1,0:T(8,128)}, u32[]{:S(2)}) copy-start(s32[24,4096]{1,0:T(8,128)} %mask.3) | copy-start | bytes 1179652
  10.7 5.5 %copy-start.2 = (f32[4,4096]{1,0:T(4,128)S(1)}, f32[4,4096]{1,0:T(4,128)}, u32[]{:S(2)}) copy-start(f32[4,4096]{1,0:T(4,128)} %gains.3) | copy-start | bytes 196612
  10.7 22.4 %all-to-all-start = ((bf16[8,17,32,128]{3,2,1,0:T(8,128)(2,1)}), bf16[8,17,32,128]{3,2,1,0:T(8,128)(2,1)S(1)}, u32[]{:S(2)}, u32[]{:S(2)}) async-start(bf16[8,17,32,128]{3,2,1,0:T(8,128)(2,1)} %shard_map.127), calls=%async_computation | async-start | bytes 2228224 | tf_op jit(solution)/shard_map/all_to_all | solution.py:617
  16.2 1.0 %copy-start.3 = (bf16[512,512]{1,0:T(8,128)(2,1)S(1)}, bf16[512,512]{1,0:T(8,128)(2,1)}, u32[]{:S(2)}) copy-start(bf16[512,512]{1,0:T(8,128)(2,1)} %constant.15.clone.place) | copy-start | bytes 1572868
  17.2 1.0 %copy-start.6 = (bf16[768,256]{1,0:T(8,128)(2,1)S(1)}, bf16[768,256]{1,0:T(8,128)(2,1)}, u32[]{:S(2)}) copy-start(bf16[768,256]{1,0:T(8,128)(2,1)} %constant.12.clone.forward) | copy-start | bytes 1179652
  18.2 0.8 %copy-start.8 = (f32[4,32,128]{2,1,0:T(8,128)S(1)}, f32[4,32,128]{2,1,0:T(8,128)}, u32[]{:S(2)}) copy-start(f32[4,32,128]{2,1,0:T(8,128)} %constant.14.clone.twist) | copy-start | bytes 196612
  33.1 17.9 %all-to-all-start.1 = ((bf16[8,9,32,128]{3,2,1,0:T(8,128)(2,1)}), bf16[8,9,32,128]{3,2,1,0:T(8,128)(2,1)S(1)}, u32[]{:S(2)}, u32[]{:S(2)}) async-start(bf16[8,9,32,128]{3,2,1,0:T(8,128)(2,1)} %shard_map.128), calls=%async_computation.1 | async-start | bytes 1179648 | tf_op jit(solution)/shard_map/all_to_all | solution.py:617
  36.7 21.5 %collective-permute-start.1 = (bf16[8,7,32,128]{3,2,1,0:T(8,128)(2,1)S(1)}, bf16[8,7,32,128]{3,2,1,0:T(8,128)(2,1)S(1)}, u32[]{:S(2)}, u32[]{:S(2)}) collective-permute-start(bf16[8,7,32,128]{3,2,1,0:T(8,128)(2,1)S(1)} %get-tuple-element.5), channel_id=1, source_target_pairs={{8,0},{16,8},{24,16},{32,24},{40,32},{48,40},{56,48},{64,56},{72,6... | collective-permute-start | bytes 1376264 | tf_op jit(solution)/shard_map/ppermute | solution.py:626
  39.6 18.6 %collective-permute-start = (bf16[8,7,32,128]{3,2,1,0:T(8,128)(2,1)S(1)}, bf16[8,7,32,128]{3,2,1,0:T(8,128)(2,1)S(1)}, u32[]{:S(2)}, u32[]{:S(2)}) collective-permute-start(bf16[8,7,32,128]{3,2,1,0:T(8,128)(2,1)S(1)} %get-tuple-element.6), channel_id=1, source_target_pairs={{0,8},{8,16},{16,24},{24,32},{32,40},{40,48},{48,56},{56,64},{64,7... | collective-permute-start | bytes 1376264 | tf_op jit(solution)/shard_map/ppermute | solution.py:625
  55.3 2.9 %copy-start.4 = (bf16[256,768]{1,0:T(8,128)(2,1)S(1)}, bf16[256,768]{1,0:T(8,128)(2,1)}, u32[]{:S(2)}) copy-start(bf16[256,768]{1,0:T(8,128)(2,1)} %constant.17.clone.band) | copy-start | bytes 1179652
  55.3 2.9 %copy-start.7 = (bf16[256,128]{1,0:T(8,128)(2,1)S(1)}, bf16[256,128]{1,0:T(8,128)(2,1)}, u32[]{:S(2)}) copy-start(bf16[256,128]{1,0:T(8,128)(2,1)} %constant.16.clone.near) | copy-start | bytes 196612

commit v3 on v2

--- a/solution.py
+++ b/solution.py
@@ -35,44 +35,19 @@
     return [order.index(line) for line in lines], order.index(None)
 
 
-def split_np(table):
-    high = table.astype(jnp.bfloat16)
-    low = (table - high.astype(np.float64)).astype(jnp.bfloat16)
-    return np.concatenate([high, high, low], axis=0)
-
-
 def tables():
     lane = np.arange(128)
     freq = 4 * (lane % 32) + lane // 32
     turn = 2.0 * np.pi / 128 * (np.outer(lane, freq) % 128)
-    forward = split_np(np.block([[np.cos(turn), -np.sin(turn)], [np.sin(turn), np.cos(turn)]]))
+    forward = np.block([[np.cos(turn), -np.sin(turn)], [np.sin(turn), np.cos(turn)]])
     turn = 2.0 * np.pi / 128 * (np.outer(freq, lane - HALO) % 128)
-    inverse = split_np(
-        np.block([[np.cos(turn), np.sin(turn)], [-np.sin(turn), np.cos(turn)]]) / RG
-    )
+    inverse = np.block([[np.cos(turn), np.sin(turn)], [-np.sin(turn), np.cos(turn)]]) / RG
     plane = np.arange(PLANES)
     angle = 2.0 * np.pi / RG * np.outer(plane, lane)
     back = 2.0 * np.pi / RG * np.outer(plane, lane - HALO)
-    twist = np.stack([np.cos(angle), np.sin(angle), np.cos(back), np.sin(back)])
-    place = np.zeros((512, 512), np.float32)
-    for phase in range(4):
-        for block in range(128):
-            place[4 * block + phase, phase * 128 + block] = 1.0
-    return forward, inverse, twist.astype(np.float32), place.astype(jnp.bfloat16)
-
-
-def tail_band():
-    near = np.zeros((128, 128), np.float32)
-    for block in range(128):
-        near[block, max(block - 3, 0) : block + 1] = 1.0
-    band = np.zeros((6, 128, 128), np.float32)
-    for row in range(6):
-        for line in range(4 * row, 4 * row + 16):
-            for block in range(3):
-                band[row, line * 3 + block, 125 + block :] = 1.0
-    both = np.concatenate(list(band), axis=1)
-    both = np.concatenate([both, both], axis=0).astype(jnp.bfloat16)
-    return np.concatenate([near, near], axis=0).astype(jnp.bfloat16), both
+    parts = [forward[:, :128], forward[:, 128:], inverse[:, :128], inverse[:, 128:]]
+    parts += [np.cos(angle), np.sin(angle), np.cos(back), np.sin(back)]
+    return np.concatenate(parts, axis=0).astype(np.float32)
 
 
 def cmul(value, cos, sin):
@@ -136,37 +111,61 @@
 
 
 def filter_kernel(
-    blocks, group, stack, gains, mask, forward, inverse, twist, place, out,
-    raw, gains_in, mask_in, forward_in, inverse_in, twist_in, place_in, sem,
-    first, spec, hold, held, gain, weights, lines_out,
+    blocks, group, stack, gains, mask, table, out,
+    raw, gains_in, mask_in, table_in, sem,
+    spec, first, hold, held, gain, weights, lines_out, forward, inverse, place,
 ):
     count = len(blocks)
     lines_here = 8 * count
     rows_here = HERE * lines_here
     line_slots, tail_slot = slots_of(blocks)
+    stack_copies = []
+    for d in range(HERE):
+        for i, block in enumerate(blocks):
+            for c in range(2):
+                stack_copies.append(
+                    pltpu.make_async_copy(
+                        stack.at[c, d, pl.ds(block, 8)],
+                        raw.at[c, d * count + i],
+                        sem.at[c * HERE * count + d * count + i],
+                    )
+                )
     copies = {}
+    for i, (name, source, target) in enumerate(
+        (("table", table, table_in), ("gains", gains, gains_in))
+    ):
+        copies[name] = pltpu.make_async_copy(source, target, sem.at[9 * count + i])
     for i, block in enumerate(blocks):
-        for c in range(2):
-            for d in range(HERE):
-                index = (c * HERE + d) * count + i
-                copies[c, d, i] = pltpu.make_async_copy(
-                    stack.at[c, d, pl.ds(block, 8)], raw.at[c, d * count + i], sem.at[index]
-                )
         copies["mask", i] = pltpu.make_async_copy(
             mask.at[pl.ds(block, 8)], mask_in.at[pl.ds(8 * i, 8)], sem.at[8 * count + i]
         )
-    others = (
-        ("gains", gains, gains_in),
-        ("twist", twist, twist_in),
-        ("forward", forward, forward_in),
-        ("inverse", inverse, inverse_in),
-        ("place", place, place_in),
-    )
-    for i, (name, source, target) in enumerate(others):
-        copies[name] = pltpu.make_async_copy(source, target, sem.at[9 * count + i])
-    for copy in copies.values():
+    for copy in stack_copies + list(copies.values()):
         copy.start()
     lanes = lax.broadcasted_iota(jnp.int32, (8, 128), 1)
+
+    def ahead(block, carry):
+        rows = pl.ds(pl.multiple_of(block * 8, 8), 8)
+
+        def store(q, re, im):
+            spec[0, q, rows] = re
+            spec[1, q, rows] = im
+
+        for c in range(2):
+            pltpu.make_async_copy(
+                stack.at[0, 0, pl.ds(0, 8)], raw.at[c, block], sem.at[c * HERE * count + block]
+            ).wait()
+
+        def load(n):
+            lanes = slice(n * 128, (n + 1) * 128)
+            return (
+                raw[0, block, :, lanes].astype(jnp.float32),
+                raw[1, block, :, lanes].astype(jnp.float32),
+            )
+
+        dft_planes(load, hold, store, -1)
+        return carry
+
+    lax.fori_loop(0, rows_here // 8, ahead, 0)
     copies["gains"].wait()
     for n in range(PLANES):
         four = gains_in[:, n * 128 : (n + 1) * 128]
@@ -175,6 +174,50 @@
     for d in range(HERE):
         turned = jnp.transpose(gain[d])
         gain[d] = jnp.concatenate([turned[32 * w : 32 * w + 32] for w in range(4)], axis=1)
+    steps = PLANES // group
+    copies["table"].wait()
+    for i, target in enumerate((forward, inverse)):
+        for half in range(2):
+            begin = 256 * (2 * i + half)
+            high, low = split(table_in[begin : begin + 256])
+            for j, part in enumerate((high, high, low)):
+                target[256 * j : 256 * j + 256, 128 * half : 128 * half + 128] = part
+    row = lax.broadcasted_iota(jnp.int32, (512, 128), 0)
+    column = lax.broadcasted_iota(jnp.int32, (512, 128), 1)
+    for p in range(4):
+        place[:, 128 * p : 128 * p + 128] = jnp.where(row == 4 * column + p, 1.0, 0.0).astype(
+            jnp.bfloat16
+        )
+
+    def middle(step, carry):
+        now = jnp.minimum(step, steps - 1) * group
+        past = jnp.maximum(step - 1, 0) * group
+        parts = []
+        for i in range(group):
+            tc = table_in[pl.ds(1024 + now + i, 1), :]
+            ts = table_in[pl.ds(1056 + now + i, 1), :]
+            re, im = spec[0, now + i], spec[1, now + i]
+            parts.append(jnp.concatenate([re * tc + im * ts, im * tc - re * ts], axis=1))
+        back = dot3(held[lax.rem(step + 1, 2)], inverse[...])
+        found = dot3(jnp.concatenate(parts, axis=0), forward[...])
+        for i in range(group):
+            for d in range(HERE):
+                row = gain[d, pl.ds(now + i, 1), :]
+                begin = i * rows_here + d * lines_here
+                held[lax.rem(step, 2), begin : begin + lines_here] = found[
+                    begin : begin + lines_here
+                ] * jnp.concatenate([row, row], axis=1)
+        for i in range(group):
+            tc = table_in[pl.ds(1088 + past + i, 1), :]
+            ts = table_in[pl.ds(1120 + past + i, 1), :]
+            re = back[i * rows_here : (i + 1) * rows_here, :128]
+            im = back[i * rows_here : (i + 1) * rows_here, 128:]
+            first[0, past + i] = re * tc - im * ts
+            first[1, past + i] = im * tc + re * ts
+        return carry
+
+    lax.fori_loop(0, steps + 1, middle, 0)
+
     for i in range(count):
         copies["mask", i].wait()
         rows = slice(8 * i, 8 * i + 8)
@@ -188,62 +231,6 @@
             weights[n, rows] = joined
             before = now
 
-    def ahead(block, carry):
-        rows = pl.ds(pl.multiple_of(block * 8, 8), 8)
-
-        def store(q, re, im):
-            spec[0, q, rows] = re
-            spec[1, q, rows] = im
-
-        for c in range(2):
-            pltpu.make_async_copy(
-                stack.at[0, 0, pl.ds(0, 8)], raw.at[c, block], sem.at[c * HERE * count + block]
-            ).wait()
-
-        def load(n):
-            lanes = slice(n * 128, (n + 1) * 128)
-            return (
-                raw[0, block, :, lanes].astype(jnp.float32),
-                raw[1, block, :, lanes].astype(jnp.float32),
-            )
-
-        dft_planes(load, hold, store, -1)
-        return carry
-
-    lax.fori_loop(0, rows_here // 8, ahead, 0)
-    steps = PLANES // group
-    for name in ("twist", "forward", "inverse"):
-        copies[name].wait()
-
-    def middle(step, carry):
-        now = jnp.minimum(step, steps - 1) * group
-        past = jnp.maximum(step - 1, 0) * group
-        parts = []
-        for i in range(group):
-            tc = twist_in[0, pl.ds(now + i, 1), :]
-            ts = twist_in[1, pl.ds(now + i, 1), :]
-            re, im = spec[0, now + i], spec[1, now + i]
-            parts.append(jnp.concatenate([re * tc + im * ts, im * tc - re * ts], axis=1))
-        back = dot3(held[lax.rem(step + 1, 2)], inverse_in[...])
-        found = dot3(jnp.concatenate(parts, axis=0), forward_in[...])
-        for i in range(group):
-            for d in range(HERE):
-                row = gain[d, pl.ds(now + i, 1), :]
-                begin = i * rows_here + d * lines_here
-                held[lax.rem(step, 2), begin : begin + lines_here] = found[
-                    begin : begin + lines_here
-                ] * jnp.concatenate([row, row], axis=1)
-        for i in range(group):
-            tc = twist_in[2, pl.ds(past + i, 1), :]
-            ts = twist_in[3, pl.ds(past + i, 1), :]
-            re = back[i * rows_here : (i + 1) * rows_here, :128]
-            im = back[i * rows_here : (i + 1) * rows_here, 128:]
-            first[0, past + i] = re * tc - im * ts
-            first[1, past + i] = im * tc + re * ts
-        return carry
-
-    lax.fori_loop(0, steps + 1, middle, 0)
-
     def behind(block, carry):
         rows = pl.ds(pl.multiple_of(block * 8, 8), 8)
         to_im = pl.ds(pl.multiple_of(block * 8 + rows_here, 8), 8)
@@ -262,7 +249,6 @@
         return carry
 
     lax.fori_loop(0, rows_here // 8, behind, 0)
-    copies["place"].wait()
 
     def gather(plane):
         return jnp.concatenate(
@@ -282,41 +268,41 @@
             tails.append(jnp.where(lanes < 3 * lines_here, tail, 0.0))
         out[slot, tail_slot] = jnp.concatenate(tails, axis=0).astype(jnp.bfloat16)
 
-    def tile(t, carry):
+    def one_tile(t):
         left = jnp.concatenate([gather(4 * t + v) for v in range(4)], axis=1).astype(jnp.bfloat16)
-        found = jnp.dot(left, place_in[...], preferred_element_type=jnp.float32)
+        found = jnp.dot(left, place[...], preferred_element_type=jnp.float32)
         for line in range(lines_here):
             out[t, line_slots[line]] = jnp.concatenate(
                 [found[line * 8 : line * 8 + 8, p * 128 : p * 128 + 128] for p in range(4)],
                 axis=0,
             ).astype(jnp.bfloat16)
         put_tail(lax.rem(t + TILES - 1, TILES), found)
-        return carry
-
-    lax.fori_loop(0, TILES, tile, 0)
+
+    def tile(step, carry):
+        one_tile(2 * step)
+        one_tile(2 * step + 1)
+        return carry
+
+    lax.fori_loop(0, TILES // 2, tile, 0)
     found = jnp.dot(
-        gather(PLANES).astype(jnp.bfloat16), place_in[:128], preferred_element_type=jnp.float32
+        gather(PLANES).astype(jnp.bfloat16), place[:128], preferred_element_type=jnp.float32
     )
     put_tail(TILES - 1, found)
 
 
 def filter_lines(stack, gains, mask, blocks, group):
-    forward, inverse, twist, place = tables()
     count = len(blocks)
     rows = HERE * 8 * count
     return pl.pallas_call(
         functools.partial(filter_kernel, blocks, group),
         out_shape=jax.ShapeDtypeStruct((TILES, 8 * count + 1, 32, 128), jnp.bfloat16),
-        in_specs=[pl.BlockSpec(memory_space=pltpu.MemorySpace.HBM)] * 7,
+        in_specs=[pl.BlockSpec(memory_space=pltpu.MemorySpace.HBM)] * 4,
         scratch_shapes=[
             pltpu.VMEM((2, HERE * count, 8, RG), jnp.bfloat16),
             pltpu.VMEM((HERE, RG), jnp.float32),
             pltpu.VMEM((8 * count, RG), jnp.int32),
-            pltpu.VMEM((768, 256), jnp.bfloat16),
-            pltpu.VMEM((768, 256), jnp.bfloat16),
-            pltpu.VMEM((4, PLANES, 128), jnp.float32),
-            pltpu.VMEM((512, 512), jnp.bfloat16),
-            pltpu.SemaphoreType.DMA((9 * count + 5,)),
+            pltpu.VMEM((1152, 128), jnp.float32),
+            pltpu.SemaphoreType.DMA((9 * count + 2,)),
             pltpu.VMEM((2, PLANES, rows, 128), jnp.float32),
             pltpu.VMEM((2, PLANES, rows, 128), jnp.float32),
             pltpu.VMEM((2, PLANES, 8, 128), jnp.float32),
@@ -324,14 +310,15 @@
             pltpu.VMEM((HERE, PLANES, 128), jnp.float32),
             pltpu.VMEM((PLANES + 1, 8 * count, 128), jnp.float32),
             pltpu.VMEM((PLANES + 1, 2 * rows, 128), jnp.float32),
+            pltpu.VMEM((768, 256), jnp.bfloat16),
+            pltpu.VMEM((768, 256), jnp.bfloat16),
+            pltpu.VMEM((512, 512), jnp.bfloat16),
         ],
-        compiler_params=pltpu.CompilerParams(
-            vmem_limit_bytes=(60 if blocks == FIRST else 24) << 20
-        ),
+        compiler_params=pltpu.CompilerParams(vmem_limit_bytes=65_700_000),
         cost_estimate=pl.CostEstimate(
             flops=2_000_000_000 * count, bytes_accessed=2_000_000, transcendentals=0
         ),
-    )(stack, gains, mask, forward, inverse, twist, place)
+    )(stack, gains, mask, tables())
 
 
 def unpacker(fields):
@@ -442,7 +429,7 @@
         kernel,
         out_shape=jax.ShapeDtypeStruct((count, 2, PAIRS, 128), jnp.float32),
         scratch_shapes=[field] * 4,
-        compiler_params=pltpu.CompilerParams(vmem_limit_bytes=16 << 20),
+        compiler_params=pltpu.CompilerParams(vmem_limit_bytes=(4 + 3 * count) << 20),
         cost_estimate=pl.CostEstimate(
             flops=3_000_000_000 * count, bytes_accessed=2_000_000, transcendentals=0
         ),
@@ -590,6 +577,20 @@
     return sums[0] + sums[1]
 
 
+def tail_band():
+    near = np.zeros((128, 128), np.float32)
+    for block in range(128):
+        near[block, max(block - 3, 0) : block + 1] = 1.0
+    band = np.zeros((6, 128, 128), np.float32)
+    for row in range(6):
+        for line in range(4 * row, 4 * row + 16):
+            for block in range(3):
+                band[row, line * 3 + block, 125 + block :] = 1.0
+    both = np.concatenate(list(band), axis=1)
+    both = np.concatenate([both, both], axis=0).astype(jnp.bfloat16)
+    return np.concatenate([near, near], axis=0).astype(jnp.bfloat16), both
+
+
 def link_windows(own, rest, above, below, early, inner):
     field = pltpu.VMEM((68, WRAP, 128), jnp.float32)
     found = pl.pallas_call(
@@ -603,7 +604,7 @@
             pltpu.VMEM((6, 2, 2 * PAIRS, 128), jnp.float32),
             pltpu.VMEM((2, 3 * DATES, 128), jnp.float32),
         ],
-        compiler_params=pltpu.CompilerParams(vmem_limit_bytes=40 << 20),
+        compiler_params=pltpu.CompilerParams(vmem_limit_bytes=28 << 20),
         cost_estimate=pl.CostEstimate(
             flops=20_000_000_000, bytes_accessed=8_000_000, transcendentals=0
         ),
@@ -616,7 +617,8 @@
     def move(tiles):
         return lax.all_to_all(tiles, "dr", split_axis=0, concat_axis=0, tiled=True)
 
-    own = move(filter_lines(stack, range_filter, scatter_mask, FIRST, 4))
+    tiles = filter_lines(stack, range_filter, scatter_mask, FIRST, 4)
+    own = move(tiles)
     tiles = filter_lines(stack, range_filter, scatter_mask, SECOND, 8)
     rest = move(tiles)
     count = lax.axis_size("az")

time: 73.6 us -> 72.1 us (0.980)
  the two profiles are of different devices: /device:TPU:32 before, /device:TPU:160 now
where the time goes in v3:
time: 72.1 us; the launch traced here: 71.8 us
  Pallas kernels  38.3 us (53%)
  waiting for transfers between devices  18.8 us (26%)
  starting transfers between devices  14.6 us (20%)
    all_to_all x2, waiting for transfers between devices, move(): return lax.all_to_all(tiles, 'dr', split_axis=0, concat_axis=0, tiled=True)  18.8 us
    pallas_call x2, Pallas kernels, filter_lines(): pl.pallas_call(functools.partial(filter_kernel, blocks, group), out_shape...  16.2 us
    pallas_call x1, Pallas kernels, link_windows(): pl.pallas_call(link_kernel, out_shape=jax.ShapeDtypeStruct((2, 6, DATES,...  14.9 us
    all_to_all x2, starting transfers between devices, move(): return lax.all_to_all(tiles, 'dr', split_axis=0, concat_axis=0, tiled=True)  8.86 us
    pallas_call x2, Pallas kernels, own_rows(): pl.pallas_call(kernel, out_shape=jax.ShapeDtypeStruct((count, 2, PAIRS, 1...  7.16 us
    ppermute x1, starting transfers between devices, on_device(): below = lax.ppermute(own[:, 4:11], 'az', up)  3.77 us
    ppermute x1, starting transfers between devices, on_device(): above = lax.ppermute(own[:, 10:17], 'az', down)  1.92 us
  transfers between devices with their start and end apart: 4, of which 2 were waited for; matrix products, arithmetic and copies ran while one was open for 0% of the time, Pallas kernels for 19%

profile of v3, /device:TPU:160, one launch (start us, length us, event | category | flops | bytes accessed | tf_op | source)
XLA Modules:
  0.0 71.8 jit_solution(15589802139940241358)
XLA Ops:
  0.0 9.4 %shard_map.73 = bf16[8,17,32,128]{3,2,1,0:T(8,128)(2,1)} custom-call(bf16[2,4,24,4096]{3,2,1,0:T(8,128)(2,1)} %stack.3, f32[4,4096]{1,0:T(4,128)} %gains.3, s32[24,4096]{1,0:T(8,128)} %mask.3, f32[1152,128]{1,0:T(8,128)} %constant.6.clone.table), custom_call_target="tpu_custom_call" | custom-call | flops 4000000000 | bytes 2000000 | tf_op jit(solution)/shard_map/pallas_call | solution.py:296
  9.4 5.3 %all-to-all-start = ((bf16[8,17,32,128]{3,2,1,0:T(8,128)(2,1)}), bf16[8,17,32,128]{3,2,1,0:T(8,128)(2,1)S(1)}, u32[]{:S(2)}, u32[]{:S(2)}) async-start(bf16[8,17,32,128]{3,2,1,0:T(8,128)(2,1)} %shard_map.73), calls=%async_computation | async-start | bytes 2228224 | tf_op jit(solution)/shard_map/all_to_all | solution.py:618
  14.8 6.8 %shard_map.74 = bf16[8,9,32,128]{3,2,1,0:T(8,128)(2,1)} custom-call(bf16[2,4,24,4096]{3,2,1,0:T(8,128)(2,1)} %stack.3, f32[4,4096]{1,0:T(4,128)} %gains.3, s32[24,4096]{1,0:T(8,128)} %mask.3, f32[1152,128]{1,0:T(8,128)} %constant.6.clone.table), custom_call_target="tpu_custom_call" | custom-call | flops 2000000000 | bytes 2000000 | tf_op jit(solution)/shard_map/pallas_call | solution.py:296
  21.5 10.2 %all-to-all-done.own = bf16[8,17,32,128]{3,2,1,0:T(8,128)(2,1)S(1)} async-done(((bf16[8,17,32,128]{3,2,1,0:T(8,128)(2,1)}), bf16[8,17,32,128]{3,2,1,0:T(8,128)(2,1)S(1)}, u32[]{:S(2)}, u32[]{:S(2)}) %all-to-all-start) | async-done | bytes 1114144 | tf_op jit(solution)/shard_map/all_to_all | solution.py:618
  31.7 3.5 %all-to-all-start.1 = ((bf16[8,9,32,128]{3,2,1,0:T(8,128)(2,1)}), bf16[8,9,32,128]{3,2,1,0:T(8,128)(2,1)S(1)}, u32[]{:S(2)}, u32[]{:S(2)}) async-start(bf16[8,9,32,128]{3,2,1,0:T(8,128)(2,1)} %shard_map.74), calls=%async_computation.1 | async-start | bytes 1179648 | tf_op jit(solution)/shard_map/all_to_all | solution.py:618
  35.3 0.1 fusion
  35.3 3.8 %collective-permute-start.1 = (bf16[8,7,32,128]{3,2,1,0:T(8,128)(2,1)S(1)}, bf16[8,7,32,128]{3,2,1,0:T(8,128)(2,1)S(1)}, u32[]{:S(2)}, u32[]{:S(2)}) collective-permute-start(bf16[8,7,32,128]{3,2,1,0:T(8,128)(2,1)S(1)} %get-tuple-element.5), channel_id=1, source_target_pairs={{8,0},{16,8},{24,16},{32,24},{40,32},{48,40},{56,48},{64,56},{72,6... | collective-permute-start | bytes 1376264 | tf_op jit(solution)/shard_map/ppermute | solution.py:628
  39.1 1.9 %collective-permute-start = (bf16[8,7,32,128]{3,2,1,0:T(8,128)(2,1)S(1)}, bf16[8,7,32,128]{3,2,1,0:T(8,128)(2,1)S(1)}, u32[]{:S(2)}, u32[]{:S(2)}) collective-permute-start(bf16[8,7,32,128]{3,2,1,0:T(8,128)(2,1)S(1)} %get-tuple-element.6), channel_id=1, source_target_pairs={{0,8},{8,16},{16,24},{24,32},{32,40},{40,48},{48,56},{56,64},{64,7... | collective-permute-start | bytes 1376264 | tf_op jit(solution)/shard_map/ppermute | solution.py:627
  41.1 8.6 %all-to-all-done.1.rest = bf16[8,9,32,128]{3,2,1,0:T(8,128)(2,1)S(1)} async-done(((bf16[8,9,32,128]{3,2,1,0:T(8,128)(2,1)}), bf16[8,9,32,128]{3,2,1,0:T(8,128)(2,1)S(1)}, u32[]{:S(2)}, u32[]{:S(2)}) %all-to-all-start.1) | async-done | bytes 589856 | tf_op jit(solution)/shard_map/all_to_all | solution.py:618
  49.6 4.3 %shard_map.76.inner = f32[3,2,576,128]{3,2,1,0:T(8,128)S(1)} custom-call(bf16[8,17,32,128]{3,2,1,0:T(8,128)(2,1)S(1)} %all-to-all-done.own, bf16[8,9,32,128]{3,2,1,0:T(8,128)(2,1)S(1)} %all-to-all-done.1.rest), custom_call_target="tpu_custom_call" | custom-call | flops 8999999488 | bytes 2000000 | tf_op jit(solution)/shard_map/pallas_call | solution.py:428
  53.9 0.0 copy-start
  54.0 0.0 copy-start.1
  54.0 2.9 %shard_map.75.early = f32[2,2,576,128]{3,2,1,0:T(8,128)S(1)} custom-call(bf16[8,17,32,128]{3,2,1,0:T(8,128)(2,1)S(1)} %all-to-all-done.own), custom_call_target="tpu_custom_call" | custom-call | flops 6000000000 | bytes 2000000 | tf_op jit(solution)/shard_map/pallas_call | solution.py:428
  56.8 0.0 collective-permute-done.1.below
  56.8 0.0 collective-permute-done.above
  56.9 0.0 copy-done
  56.9 0.0 copy-done.1
  56.9 14.9 %link_windows.1 = f32[2,6,32,128]{3,2,1,0:T(8,128)} custom-call(bf16[8,17,32,128]{3,2,1,0:T(8,128)(2,1)S(1)} %all-to-all-done.own, bf16[8,9,32,128]{3,2,1,0:T(8,128)(2,1)S(1)} %all-to-all-done.1.rest, bf16[8,7,32,128]{3,2,1,0:T(8,128)(2,1)S(1)} %collective-permute-done.above, bf16[8,7,32,128]{3,2,1,0:T(8,128)(2,1)S(1)} %collective-permute-done.1.below, ...), custom_call_target="tpu_custom_call" | custom-call | flops 20000000000 | bytes 8000000 | tf_op jit(solution)/shard_map/link_windows/pallas_call | solution.py:596
Async XLA Ops:
  9.4 22.3 %all-to-all-start = ((bf16[8,17,32,128]{3,2,1,0:T(8,128)(2,1)}), bf16[8,17,32,128]{3,2,1,0:T(8,128)(2,1)S(1)}, u32[]{:S(2)}, u32[]{:S(2)}) async-start(bf16[8,17,32,128]{3,2,1,0:T(8,128)(2,1)} %shard_map.73), calls=%async_computation | async-start | bytes 2228224 | tf_op jit(solution)/shard_map/all_to_all | solution.py:618
  31.7 17.9 %all-to-all-start.1 = ((bf16[8,9,32,128]{3,2,1,0:T(8,128)(2,1)}), bf16[8,9,32,128]{3,2,1,0:T(8,128)(2,1)S(1)}, u32[]{:S(2)}, u32[]{:S(2)}) async-start(bf16[8,9,32,128]{3,2,1,0:T(8,128)(2,1)} %shard_map.74), calls=%async_computation.1 | async-start | bytes 1179648 | tf_op jit(solution)/shard_map/all_to_all | solution.py:618
  35.3 21.5 %collective-permute-start.1 = (bf16[8,7,32,128]{3,2,1,0:T(8,128)(2,1)S(1)}, bf16[8,7,32,128]{3,2,1,0:T(8,128)(2,1)S(1)}, u32[]{:S(2)}, u32[]{:S(2)}) collective-permute-start(bf16[8,7,32,128]{3,2,1,0:T(8,128)(2,1)S(1)} %get-tuple-element.5), channel_id=1, source_target_pairs={{8,0},{16,8},{24,16},{32,24},{40,32},{48,40},{56,48},{64,56},{72,6... | collective-permute-start | bytes 1376264 | tf_op jit(solution)/shard_map/ppermute | solution.py:628
  39.1 17.7 %collective-permute-start = (bf16[8,7,32,128]{3,2,1,0:T(8,128)(2,1)S(1)}, bf16[8,7,32,128]{3,2,1,0:T(8,128)(2,1)S(1)}, u32[]{:S(2)}, u32[]{:S(2)}) collective-permute-start(bf16[8,7,32,128]{3,2,1,0:T(8,128)(2,1)S(1)} %get-tuple-element.6), channel_id=1, source_target_pairs={{0,8},{8,16},{16,24},{24,32},{32,40},{40,48},{48,56},{56,64},{64,7... | collective-permute-start | bytes 1376264 | tf_op jit(solution)/shard_map/ppermute | solution.py:627
  53.9 2.9 %copy-start = (bf16[256,768]{1,0:T(8,128)(2,1)S(1)}, bf16[256,768]{1,0:T(8,128)(2,1)}, u32[]{:S(2)}) copy-start(bf16[256,768]{1,0:T(8,128)(2,1)} %constant.8.clone.band) | copy-start | bytes 1179652
  54.0 2.9 %copy-start.1 = (bf16[256,128]{1,0:T(8,128)(2,1)S(1)}, bf16[256,128]{1,0:T(8,128)(2,1)}, u32[]{:S(2)}) copy-start(bf16[256,128]{1,0:T(8,128)(2,1)} %constant.7.clone.near) | copy-start | bytes 196612

commit v4 on v3

--- a/solution.py
+++ b/solution.py
@@ -1,4 +1,3 @@
-import functools
 import math
 
 import jax
@@ -21,18 +20,19 @@
 PLANES = 32
 HERE = 4
 FIRST, SECOND = (0, 16), (8,)
+KEPT = (6, 7, 16, 17)
 SHIFTS = 17
 PAIRS = (SHIFTS + 1) * DATES
 WRAP = 48
 
 
-def slots_of(blocks):
-    if blocks == FIRST:
-        order = [6, 7, 16, 17, 0, 1, 2, 3, 4, 5, None, 18, 19, 20, 21, 22, 23]
-    else:
-        order = list(range(8, 16)) + [None]
-    lines = [block + i for block in blocks for i in range(8)]
-    return [order.index(line) for line in lines], order.index(None)
+def slot_of(line):
+    if 6 <= line < 18:
+        return line - 6
+    return line if line < 6 else line - 11
+
+
+EARLY_TAIL, LATE_TAIL, SLOTS = 6, 12, 13
 
 
 def tables():
@@ -111,14 +111,15 @@
 
 
 def filter_kernel(
-    blocks, group, stack, gains, mask, table, out,
+    blocks, group, stack, gains, mask, table, kept, out,
     raw, gains_in, mask_in, table_in, sem,
     spec, first, hold, held, gain, weights, lines_out, forward, inverse, place,
 ):
     count = len(blocks)
     lines_here = 8 * count
     rows_here = HERE * lines_here
-    line_slots, tail_slot = slots_of(blocks)
+    pitch = lines_here + 1
+    early = blocks == FIRST
     stack_copies = []
     for d in range(HERE):
         for i, block in enumerate(blocks):
@@ -233,16 +234,18 @@
 
     def behind(block, carry):
         rows = pl.ds(pl.multiple_of(block * 8, 8), 8)
-        to_im = pl.ds(pl.multiple_of(block * 8 + rows_here, 8), 8)
+        begin = (block // count) * pitch + lax.rem(block, count) * 8
+        to_re = pl.ds(begin, 8)
+        to_im = pl.ds(begin + HERE * pitch, 8)
         lines = pl.ds(pl.multiple_of(lax.rem(block, count) * 8, 8), 8)
 
         def store(n, re, im):
             weight = weights[n, lines]
-            lines_out[n, rows] = re * weight
+            lines_out[n, to_re] = re * weight
             lines_out[n, to_im] = im * weight
             if n == 0:
                 weight = weights[PLANES, lines]
-                lines_out[PLANES, rows] = re * weight
+                lines_out[PLANES, to_re] = re * weight
                 lines_out[PLANES, to_im] = im * weight
 
         dft_planes(lambda q: (first[0, q, rows], first[1, q, rows]), hold, store, 1)
@@ -252,7 +255,7 @@
 
     def gather(plane):
         return jnp.concatenate(
-            [lines_out[plane, pl.ds(line, 8, stride=lines_here), :] for line in range(lines_here)],
+            [lines_out[plane, pl.ds(line, 8, stride=pitch), :] for line in range(lines_here)],
             axis=0,
         )
 
@@ -266,16 +269,26 @@
                     part = pltpu.roll(part, 3 * line, 1)
                 tail = jnp.where(lanes >= 3 * line, part, tail)
             tails.append(jnp.where(lanes < 3 * lines_here, tail, 0.0))
-        out[slot, tail_slot] = jnp.concatenate(tails, axis=0).astype(jnp.bfloat16)
+        out[slot, EARLY_TAIL if early else LATE_TAIL] = jnp.concatenate(tails, axis=0).astype(
+            jnp.bfloat16
+        )
 
     def one_tile(t):
         left = jnp.concatenate([gather(4 * t + v) for v in range(4)], axis=1).astype(jnp.bfloat16)
         found = jnp.dot(left, place[...], preferred_element_type=jnp.float32)
-        for line in range(lines_here):
-            out[t, line_slots[line]] = jnp.concatenate(
-                [found[line * 8 : line * 8 + 8, p * 128 : p * 128 + 128] for p in range(4)],
+        for index in range(lines_here):
+            line = blocks[index // 8] + index % 8
+            value = jnp.concatenate(
+                [found[index * 8 : index * 8 + 8, p * 128 : p * 128 + 128] for p in range(4)],
                 axis=0,
             ).astype(jnp.bfloat16)
+            if early and line in KEPT:
+                kept[t, KEPT.index(line)] = value
+            else:
+                out[t, slot_of(line)] = value
+        if not early:
+            for index, line in enumerate(KEPT):
+                out[t, slot_of(line)] = kept[t, index]
         put_tail(lax.rem(t + TILES - 1, TILES), found)
 
     def tile(step, carry):
@@ -290,13 +303,23 @@
     put_tail(TILES - 1, found)
 
 
-def filter_lines(stack, gains, mask, blocks, group):
+def filter_lines(stack, gains, mask, blocks, group, kept=None):
     count = len(blocks)
+    tiles = jax.ShapeDtypeStruct((TILES, SLOTS, 32, 128), jnp.bfloat16)
+    rest = jax.ShapeDtypeStruct((TILES, len(KEPT), 32, 128), jnp.bfloat16)
+    hbm = pl.BlockSpec(memory_space=pltpu.MemorySpace.HBM)
+    vmem = pl.BlockSpec(memory_space=pltpu.MemorySpace.VMEM)
+
+    def kernel(*refs):
+        if blocks == FIRST:
+            refs = refs[:4] + (refs[5], refs[4]) + refs[6:]
+        filter_kernel(blocks, group, *refs)
+
     rows = HERE * 8 * count
     return pl.pallas_call(
-        functools.partial(filter_kernel, blocks, group),
-        out_shape=jax.ShapeDtypeStruct((TILES, 8 * count + 1, 32, 128), jnp.bfloat16),
-        in_specs=[pl.BlockSpec(memory_space=pltpu.MemorySpace.HBM)] * 4,
+        kernel,
+        out_shape=(tiles, rest) if blocks == FIRST else tiles,
+        in_specs=[hbm] * 4 + ([] if blocks == FIRST else [vmem]),
         scratch_shapes=[
             pltpu.VMEM((2, HERE * count, 8, RG), jnp.bfloat16),
             pltpu.VMEM((HERE, RG), jnp.float32),
@@ -309,7 +332,7 @@
             pltpu.VMEM((2, group * rows, 256), jnp.float32),
             pltpu.VMEM((HERE, PLANES, 128), jnp.float32),
             pltpu.VMEM((PLANES + 1, 8 * count, 128), jnp.float32),
-            pltpu.VMEM((PLANES + 1, 2 * rows, 128), jnp.float32),
+            pltpu.VMEM((PLANES + 1, 2 * rows + 2 * HERE, 128), jnp.float32),
             pltpu.VMEM((768, 256), jnp.bfloat16),
             pltpu.VMEM((768, 256), jnp.bfloat16),
             pltpu.VMEM((512, 512), jnp.bfloat16),
@@ -318,7 +341,7 @@
         cost_estimate=pl.CostEstimate(
             flops=2_000_000_000 * count, bytes_accessed=2_000_000, transcendentals=0
         ),
-    )(stack, gains, mask, tables())
+    )(stack, gains, mask, tables(), *(() if kept is None else (kept,)))
 
 
 def unpacker(fields):
@@ -410,16 +433,14 @@
 
 def early_kernel(own, sums, *fields):
     _, run = unpacker(fields)
-    run(own, 6, 0, 4)
-    run(own, 11, 4, 4)
+    run(own, 2, 0, 4)
+    run(own, 7, 4, 4)
     gram_rows(fields, sums, 2, 0, 0)
 
 
-def inner_kernel(own, rest, sums, *fields):
+def inner_kernel(rest, sums, *fields):
     _, run = unpacker(fields)
-    run(own, 0, 0, 2)
-    run(rest, 0, 2, 8)
-    run(own, 2, 10, 2)
+    run(rest, 0, 0, 12)
     gram_rows(fields, sums, 3, 0, 0)
 
 
@@ -444,14 +465,14 @@
     lanes = lax.broadcasted_iota(jnp.int32, (8, 128), 1)
     put, run = unpacker(fields)
     run(above, 1, 0, 6)
-    run(own, 4, 6, 2)
-    run(own, 15, 8, 2)
+    run(own, 0, 6, 2)
+    run(own, 11, 8, 2)
     run(below, 0, 10, 6)
     for group in range(4):
         pieces = []
         for source in (2 * group, 2 * group + 1):
-            mine = own[source, 10].astype(jnp.float32)
-            others = rest[source, 8].astype(jnp.float32)
+            mine = own[source, EARLY_TAIL].astype(jnp.float32)
+            others = rest[source, LATE_TAIL].astype(jnp.float32)
             up = above[source, 0].astype(jnp.float32)
             down = below[source, 6].astype(jnp.float32)
             piece = []
@@ -617,17 +638,17 @@
     def move(tiles):
         return lax.all_to_all(tiles, "dr", split_axis=0, concat_axis=0, tiled=True)
 
-    tiles = filter_lines(stack, range_filter, scatter_mask, FIRST, 4)
+    tiles, kept = filter_lines(stack, range_filter, scatter_mask, FIRST, 4)
     own = move(tiles)
-    tiles = filter_lines(stack, range_filter, scatter_mask, SECOND, 8)
+    tiles = filter_lines(stack, range_filter, scatter_mask, SECOND, 8, kept)
     rest = move(tiles)
     count = lax.axis_size("az")
     down = [(i, i + 1) for i in range(count - 1)]
     up = [(i + 1, i) for i in range(count - 1)]
-    above = lax.ppermute(own[:, 10:17], "az", down)
-    below = lax.ppermute(own[:, 4:11], "az", up)
+    above = lax.ppermute(own[:, 6:13], "az", down)
+    below = lax.ppermute(own[:, 0:7], "az", up)
     early = own_rows(early_kernel, 2, own)
-    inner = own_rows(inner_kernel, 3, own, rest)
+    inner = own_rows(inner_kernel, 3, rest)
     return link_windows(own, rest, above, below, early, inner)
 
 

time: 72.1 us -> 71 us (0.985)
  the two profiles are of different devices: /device:TPU:160 before, /device:TPU:66 now
where the time goes in v4:
time: 71 us; the launch traced here: 70.6 us
  Pallas kernels  39.2 us (55%)
  waiting for transfers between devices  16 us (23%)
  starting transfers between devices  15.2 us (21%)
    pallas_call x2, Pallas kernels, filter_lines(): pl.pallas_call(kernel, out_shape=(tiles, rest) if blocks == FIRST else ti...  17.1 us
    all_to_all x2, waiting for transfers between devices, move(): return lax.all_to_all(tiles, 'dr', split_axis=0, concat_axis=0, tiled=True)  16 us
    pallas_call x1, Pallas kernels, link_windows(): pl.pallas_call(link_kernel, out_shape=jax.ShapeDtypeStruct((2, 6, DATES,...  14.9 us
    all_to_all x2, starting transfers between devices, move(): return lax.all_to_all(tiles, 'dr', split_axis=0, concat_axis=0, tiled=True)  10.8 us
    pallas_call x2, Pallas kernels, own_rows(): pl.pallas_call(kernel, out_shape=jax.ShapeDtypeStruct((count, 2, PAIRS, 1...  7.16 us
    ppermute x1, starting transfers between devices, on_device(): below = lax.ppermute(own[:, 0:7], 'az', up)  2.57 us
    ppermute x1, starting transfers between devices, on_device(): above = lax.ppermute(own[:, 6:13], 'az', down)  1.92 us
  transfers between devices with their start and end apart: 4, of which 2 were waited for; matrix products, arithmetic and copies ran while one was open for 0% of the time, Pallas kernels for 21%

profile of v4, /device:TPU:66, one launch (start us, length us, event | category | flops | bytes accessed | tf_op | source)
XLA Modules:
  0.0 70.6 jit_solution(2886892262676251574)
XLA Ops:
  0.0 9.3 %shard_map.73 = (bf16[8,13,32,128]{3,2,1,0:T(8,128)(2,1)}, bf16[8,4,32,128]{3,2,1,0:T(8,128)(2,1)}) custom-call(bf16[2,4,24,4096]{3,2,1,0:T(8,128)(2,1)} %refs_0_.3, f32[4,4096]{1,0:T(4,128)} %refs_1_.3, s32[24,4096]{1,0:T(8,128)} %refs_2_.3, f32[1152,128]{1,0:T(8,128)} %constant.6.clone.refs_3_), custom_call_target="tpu_custom_call" | custom-call | flops 4000000000 | bytes 2000000 | tf_op jit(solution)/shard_map/pallas_call | solution.py:319
  9.3 5.9 %all-to-all-start = ((bf16[8,13,32,128]{3,2,1,0:T(8,128)(2,1)}), bf16[8,13,32,128]{3,2,1,0:T(8,128)(2,1)S(1)}, u32[]{:S(2)}, u32[]{:S(2)}) async-start(bf16[8,13,32,128]{3,2,1,0:T(8,128)(2,1)} %get-tuple-element.7), calls=%async_computation | async-start | bytes 1703936 | tf_op jit(solution)/shard_map/all_to_all | solution.py:639
  15.2 7.8 %shard_map.74 = bf16[8,13,32,128]{3,2,1,0:T(8,128)(2,1)} custom-call(bf16[2,4,24,4096]{3,2,1,0:T(8,128)(2,1)} %refs_0_.3, f32[4,4096]{1,0:T(4,128)} %refs_1_.3, s32[24,4096]{1,0:T(8,128)} %refs_2_.3, f32[1152,128]{1,0:T(8,128)} %constant.6.clone.refs_3_, bf16[8,4,32,128]{3,2,1,0:T(8,128)(2,1)} %get-tuple-element.8.refs_4_), custom_call_target="tpu_custom_call" | custom-call | flops 2000000000 | bytes 2000000 | tf_op jit(solution)/shard_map/pallas_call | solution.py:319
  23.0 3.9 %all-to-all-done.own = bf16[8,13,32,128]{3,2,1,0:T(8,128)(2,1)S(1)} async-done(((bf16[8,13,32,128]{3,2,1,0:T(8,128)(2,1)}), bf16[8,13,32,128]{3,2,1,0:T(8,128)(2,1)S(1)}, u32[]{:S(2)}, u32[]{:S(2)}) %all-to-all-start) | async-done | bytes 852000 | tf_op jit(solution)/shard_map/all_to_all | solution.py:639
  26.9 4.9 %all-to-all-start.1 = ((bf16[8,13,32,128]{3,2,1,0:T(8,128)(2,1)}), bf16[8,13,32,128]{3,2,1,0:T(8,128)(2,1)S(1)}, u32[]{:S(2)}, u32[]{:S(2)}) async-start(bf16[8,13,32,128]{3,2,1,0:T(8,128)(2,1)} %shard_map.74), calls=%async_computation.1 | async-start | bytes 1703936 | tf_op jit(solution)/shard_map/all_to_all | solution.py:639
  31.8 0.1 fusion
  31.9 2.6 %collective-permute-start.1 = (bf16[8,7,32,128]{3,2,1,0:T(8,128)(2,1)S(1)}, bf16[8,7,32,128]{3,2,1,0:T(8,128)(2,1)S(1)}, u32[]{:S(2)}, u32[]{:S(2)}) collective-permute-start(bf16[8,7,32,128]{3,2,1,0:T(8,128)(2,1)S(1)} %get-tuple-element.9), channel_id=1, source_target_pairs={{8,0},{16,8},{24,16},{32,24},{40,32},{48,40},{56,48},{64,56},{72,6... | collective-permute-start | bytes 1376264 | tf_op jit(solution)/shard_map/ppermute | solution.py:649
  34.5 1.9 %collective-permute-start = (bf16[8,7,32,128]{3,2,1,0:T(8,128)(2,1)S(1)}, bf16[8,7,32,128]{3,2,1,0:T(8,128)(2,1)S(1)}, u32[]{:S(2)}, u32[]{:S(2)}) collective-permute-start(bf16[8,7,32,128]{3,2,1,0:T(8,128)(2,1)S(1)} %get-tuple-element.10), channel_id=1, source_target_pairs={{0,8},{8,16},{16,24},{24,32},{32,40},{40,48},{48,56},{56,64},{64,7... | collective-permute-start | bytes 1376264 | tf_op jit(solution)/shard_map/ppermute | solution.py:648
  36.4 12.0 %all-to-all-done.1.rest = bf16[8,13,32,128]{3,2,1,0:T(8,128)(2,1)S(1)} async-done(((bf16[8,13,32,128]{3,2,1,0:T(8,128)(2,1)}), bf16[8,13,32,128]{3,2,1,0:T(8,128)(2,1)S(1)}, u32[]{:S(2)}, u32[]{:S(2)}) %all-to-all-start.1) | async-done | bytes 852000 | tf_op jit(solution)/shard_map/all_to_all | solution.py:639
  48.5 4.3 %shard_map.76.inner = f32[3,2,576,128]{3,2,1,0:T(8,128)S(1)} custom-call(bf16[8,13,32,128]{3,2,1,0:T(8,128)(2,1)S(1)} %all-to-all-done.1.rest), custom_call_target="tpu_custom_call" | custom-call | flops 8999999488 | bytes 2000000 | tf_op jit(solution)/shard_map/pallas_call | solution.py:449
  52.8 0.0 copy-start
  52.8 0.0 copy-start.1
  52.8 2.9 %shard_map.75.early = f32[2,2,576,128]{3,2,1,0:T(8,128)S(1)} custom-call(bf16[8,13,32,128]{3,2,1,0:T(8,128)(2,1)S(1)} %all-to-all-done.own), custom_call_target="tpu_custom_call" | custom-call | flops 6000000000 | bytes 2000000 | tf_op jit(solution)/shard_map/pallas_call | solution.py:449
  55.7 0.0 collective-permute-done.1.below
  55.7 0.0 collective-permute-done.above
  55.7 0.0 copy-done
  55.7 0.0 copy-done.1
  55.7 14.9 %link_windows.1 = f32[2,6,32,128]{3,2,1,0:T(8,128)} custom-call(bf16[8,13,32,128]{3,2,1,0:T(8,128)(2,1)S(1)} %all-to-all-done.own, bf16[8,13,32,128]{3,2,1,0:T(8,128)(2,1)S(1)} %all-to-all-done.1.rest, bf16[8,7,32,128]{3,2,1,0:T(8,128)(2,1)S(1)} %collective-permute-done.above, bf16[8,7,32,128]{3,2,1,0:T(8,128)(2,1)S(1)} %collective-permute-done.1.below, ...), custom_call_target="tpu_custom_call" | custom-call | flops 20000000000 | bytes 8000000 | tf_op jit(solution)/shard_map/link_windows/pallas_call | solution.py:617
Async XLA Ops:
  9.3 17.6 %all-to-all-start = ((bf16[8,13,32,128]{3,2,1,0:T(8,128)(2,1)}), bf16[8,13,32,128]{3,2,1,0:T(8,128)(2,1)S(1)}, u32[]{:S(2)}, u32[]{:S(2)}) async-start(bf16[8,13,32,128]{3,2,1,0:T(8,128)(2,1)} %get-tuple-element.7), calls=%async_computation | async-start | bytes 1703936 | tf_op jit(solution)/shard_map/all_to_all | solution.py:639
  26.9 21.5 %all-to-all-start.1 = ((bf16[8,13,32,128]{3,2,1,0:T(8,128)(2,1)}), bf16[8,13,32,128]{3,2,1,0:T(8,128)(2,1)S(1)}, u32[]{:S(2)}, u32[]{:S(2)}) async-start(bf16[8,13,32,128]{3,2,1,0:T(8,128)(2,1)} %shard_map.74), calls=%async_computation.1 | async-start | bytes 1703936 | tf_op jit(solution)/shard_map/all_to_all | solution.py:639
  31.9 23.7 %collective-permute-start.1 = (bf16[8,7,32,128]{3,2,1,0:T(8,128)(2,1)S(1)}, bf16[8,7,32,128]{3,2,1,0:T(8,128)(2,1)S(1)}, u32[]{:S(2)}, u32[]{:S(2)}) collective-permute-start(bf16[8,7,32,128]{3,2,1,0:T(8,128)(2,1)S(1)} %get-tuple-element.9), channel_id=1, source_target_pairs={{8,0},{16,8},{24,16},{32,24},{40,32},{48,40},{56,48},{64,56},{72,6... | collective-permute-start | bytes 1376264 | tf_op jit(solution)/shard_map/ppermute | solution.py:649
  34.5 21.2 %collective-permute-start = (bf16[8,7,32,128]{3,2,1,0:T(8,128)(2,1)S(1)}, bf16[8,7,32,128]{3,2,1,0:T(8,128)(2,1)S(1)}, u32[]{:S(2)}, u32[]{:S(2)}) collective-permute-start(bf16[8,7,32,128]{3,2,1,0:T(8,128)(2,1)S(1)} %get-tuple-element.10), channel_id=1, source_target_pairs={{0,8},{8,16},{16,24},{24,32},{32,40},{40,48},{48,56},{56,64},{64,7... | collective-permute-start | bytes 1376264 | tf_op jit(solution)/shard_map/ppermute | solution.py:648
  52.8 2.9 %copy-start = (bf16[256,768]{1,0:T(8,128)(2,1)S(1)}, bf16[256,768]{1,0:T(8,128)(2,1)}, u32[]{:S(2)}) copy-start(bf16[256,768]{1,0:T(8,128)(2,1)} %constant.8.clone.band) | copy-start | bytes 1179652
  52.8 2.9 %copy-start.1 = (bf16[256,128]{1,0:T(8,128)(2,1)S(1)}, bf16[256,128]{1,0:T(8,128)(2,1)}, u32[]{:S(2)}) copy-start(bf16[256,128]{1,0:T(8,128)(2,1)} %constant.7.clone.near) | copy-start | bytes 196612

commit v5 on v4

--- a/solution.py
+++ b/solution.py
@@ -431,26 +431,56 @@
     lax.fori_loop(0, count, one_row, 0)
 
 
-def early_kernel(own, sums, *fields):
+def send_rows(fields, held, target, sem, count):
+    def copy(r):
+        return pltpu.make_async_copy(held.at[r], target.at[r], sem.at[r])
+
+    def one_row(r, carry):
+        def store(c, spot, value):
+            held[r, c, spot] = value
+
+        gram(fields, r * 16, 16, store)
+
+        @pl.when(r > 0)
+        def _():
+            copy(r - 1).start()
+
+        return carry
+
+    lax.fori_loop(0, count, one_row, 0)
+    copy(count - 1).start()
+    for r in range(count):
+        copy(r).wait()
+
+
+def early_kernel(own, target, held, sem, *fields):
     _, run = unpacker(fields)
     run(own, 2, 0, 4)
     run(own, 7, 4, 4)
-    gram_rows(fields, sums, 2, 0, 0)
-
-
-def inner_kernel(rest, sums, *fields):
+    send_rows(fields, held, target, sem, 2)
+
+
+def halo_kernel(own, above, below, target, held, sem, *fields):
     _, run = unpacker(fields)
-    run(rest, 0, 0, 12)
-    gram_rows(fields, sums, 3, 0, 0)
-
-
-def own_rows(kernel, count, *chunks):
+    run(above, 1, 0, 6)
+    run(own, 0, 6, 2)
+    run(own, 11, 8, 2)
+    run(below, 0, 10, 6)
+    send_rows(fields, held, target, sem, 4)
+
+
+def some_rows(kernel, count, *chunks):
     field = pltpu.VMEM((count * 16, WRAP, 128), jnp.float32)
     return pl.pallas_call(
         kernel,
         out_shape=jax.ShapeDtypeStruct((count, 2, PAIRS, 128), jnp.float32),
-        scratch_shapes=[field] * 4,
-        compiler_params=pltpu.CompilerParams(vmem_limit_bytes=(4 + 3 * count) << 20),
+        out_specs=pl.BlockSpec(memory_space=pltpu.MemorySpace.HBM),
+        scratch_shapes=[
+            pltpu.VMEM((count, 2, PAIRS, 128), jnp.float32),
+            pltpu.SemaphoreType.DMA((count,)),
+        ]
+        + [field] * 4,
+        compiler_params=pltpu.CompilerParams(vmem_limit_bytes=64_200_000),
         cost_estimate=pl.CostEstimate(
             flops=3_000_000_000 * count, bytes_accessed=2_000_000, transcendentals=0
         ),
@@ -458,16 +488,19 @@
 
 
 def link_kernel(
-    own, rest, above, below, early, inner, near, band, out,
-    z_re, z_im, z_sum, z_dif, sums, tails, extra, cov, vec,
+    own, rest, above, below, early_sums, halo_sums, near, band, out,
+    z_re, z_im, z_sum, z_dif, sums, early, edges, sem, tails, extra, cov, vec,
 ):
+    copies = [
+        pltpu.make_async_copy(early_sums, early, sem.at[0]),
+        pltpu.make_async_copy(halo_sums, edges, sem.at[1]),
+    ]
+    for copy in copies:
+        copy.start()
     fields = (z_re, z_im, z_sum, z_dif)
     lanes = lax.broadcasted_iota(jnp.int32, (8, 128), 1)
     put, run = unpacker(fields)
-    run(above, 1, 0, 6)
-    run(own, 0, 6, 2)
-    run(own, 11, 8, 2)
-    run(below, 0, 10, 6)
+    run(rest, 0, 0, 12)
     for group in range(4):
         pieces = []
         for source in (2 * group, 2 * group + 1):
@@ -490,19 +523,22 @@
                 piece.append(jnp.where(lanes < 108, value, 0.0))
             pieces.append(piece)
         for p in range(4):
-            put(64 + p, group, pieces[0][p], pieces[1][p])
+            put(48 + p, group, pieces[0][p], pieces[1][p])
 
     def store_tail(c, spot, value):
         tails[c, spot] = value
 
-    gram(fields, 64, 4, store_tail)
+    gram(fields, 48, 4, store_tail)
     tails[1, 0:DATES] = jnp.zeros((DATES, 128), jnp.float32)
-    gram_rows(fields, sums, 4, 0, 0)
+    gram_rows(fields, sums, 3, 0, 0)
     for c in range(2):
         high, low = split(tails[c])
         extra[c] = jnp.dot(
             jnp.concatenate([high, low], axis=1), band[...], preferred_element_type=jnp.float32
         )
+
+    for copy in copies:
+        copy.wait()
 
     def windows(step, carry):
         size = 2 * DATES
@@ -510,10 +546,10 @@
         spot = pl.ds(begin, size)
         twice = pl.multiple_of(step * 2 * size, 2 * size)
         for c in range(2):
-            rowsum = [sums[r, c, spot] for r in (0, 1)]
-            rowsum += [early[0, c, spot]] + [inner[r, c, spot] for r in range(3)]
+            rowsum = [edges[r, c, spot] for r in (0, 1)]
+            rowsum += [early[0, c, spot]] + [sums[r, c, spot] for r in range(3)]
             rowsum += [early[1, c, spot]]
-            rowsum += [sums[r, c, spot] for r in (2, 3)]
+            rowsum += [edges[r, c, spot] for r in (2, 3)]
             pairs = [rowsum[r] + rowsum[r + 1] for r in range(8)]
             value = jnp.concatenate([pairs[a] + pairs[a + 2] for a in range(6)], axis=0)
             high, low = split(value)
@@ -612,25 +648,31 @@
     return np.concatenate([near, near], axis=0).astype(jnp.bfloat16), both
 
 
-def link_windows(own, rest, above, below, early, inner):
-    field = pltpu.VMEM((68, WRAP, 128), jnp.float32)
+def link_windows(own, rest, above, below, early, edges):
+    field = pltpu.VMEM((52, WRAP, 128), jnp.float32)
+    vmem = pl.BlockSpec(memory_space=pltpu.MemorySpace.VMEM)
+    hbm = pl.BlockSpec(memory_space=pltpu.MemorySpace.HBM)
     found = pl.pallas_call(
         link_kernel,
         out_shape=jax.ShapeDtypeStruct((2, 6, DATES, 128), jnp.float32),
+        in_specs=[vmem] * 4 + [hbm] * 2 + [vmem] * 2,
         scratch_shapes=[field] * 4
         + [
+            pltpu.VMEM((3, 2, PAIRS, 128), jnp.float32),
+            pltpu.VMEM((2, 2, PAIRS, 128), jnp.float32),
             pltpu.VMEM((4, 2, PAIRS, 128), jnp.float32),
+            pltpu.SemaphoreType.DMA((2,)),
             pltpu.VMEM((2, PAIRS, 128), jnp.float32),
             pltpu.VMEM((2, PAIRS, 6 * 128), jnp.float32),
             pltpu.VMEM((6, 2, 2 * PAIRS, 128), jnp.float32),
             pltpu.VMEM((2, 3 * DATES, 128), jnp.float32),
         ],
-        compiler_params=pltpu.CompilerParams(vmem_limit_bytes=28 << 20),
+        compiler_params=pltpu.CompilerParams(vmem_limit_bytes=64_200_000),
         cost_estimate=pl.CostEstimate(
             flops=20_000_000_000, bytes_accessed=8_000_000, transcendentals=0
         ),
         name="link_windows",
-    )(own, rest, above, below, early, inner, *tail_band())
+    )(own, rest, above, below, early, edges, *tail_band())
     return jnp.transpose(found, (0, 2, 1, 3))
 
 
@@ -647,9 +689,9 @@
     up = [(i + 1, i) for i in range(count - 1)]
     above = lax.ppermute(own[:, 6:13], "az", down)
     below = lax.ppermute(own[:, 0:7], "az", up)
-    early = own_rows(early_kernel, 2, own)
-    inner = own_rows(inner_kernel, 3, rest)
-    return link_windows(own, rest, above, below, early, inner)
+    early = some_rows(early_kernel, 2, own)
+    edges = some_rows(halo_kernel, 4, own, above, below)
+    return link_windows(own, rest, above, below, early, edges)
 
 
 def solution(mesh):

time: 71 us -> 80 us (1.13)
  the two profiles are of different devices: /device:TPU:66 before, /device:TPU:65 now
where the time goes in v5:
time: 80 us; the launch traced here: 79.2 us
  Pallas kernels  45.7 us (57%)
  starting transfers between devices  16.5 us (21%)
  waiting for transfers between devices  14.3 us (18%)
  local copies, waits for them, and re-layouts  2.53 us (3%)
    pallas_call x2, Pallas kernels, filter_lines(): pl.pallas_call(kernel, out_shape=(tiles, rest) if blocks == FIRST else ti...  17.1 us
    pallas_call x1, Pallas kernels, link_windows(): pl.pallas_call(link_kernel, out_shape=jax.ShapeDtypeStruct((2, 6, DATES,...  15.3 us
    pallas_call x2, Pallas kernels, some_rows(): pl.pallas_call(kernel, out_shape=jax.ShapeDtypeStruct((count, 2, PAIRS, 1...  13.3 us
    ppermute x1, waiting for transfers between devices, on_device(): below = lax.ppermute(own[:, 0:7], 'az', up)  9.59 us
    all_to_all x2, starting transfers between devices, move(): return lax.all_to_all(tiles, 'dr', split_axis=0, concat_axis=0, tiled=True)  8.61 us
    all_to_all x2, waiting for transfers between devices, move(): return lax.all_to_all(tiles, 'dr', split_axis=0, concat_axis=0, tiled=True)  4.73 us
    ppermute x1, starting transfers between devices, on_device(): above = lax.ppermute(own[:, 6:13], 'az', down)  4.42 us
    ppermute x1, starting transfers between devices, on_device(): below = lax.ppermute(own[:, 0:7], 'az', up)  3.52 us
  transfers between devices with their start and end apart: 4, of which 2 were waited for; matrix products, arithmetic and copies ran while one was open for 0% of the time, Pallas kernels for 27%

profile of v5, /device:TPU:65, one launch (start us, length us, event | category | flops | bytes accessed | tf_op | source)
XLA Modules:
  0.0 79.2 jit_solution(14313426466201995320)
XLA Ops:
  0.0 9.3 %shard_map.73 = (bf16[8,13,32,128]{3,2,1,0:T(8,128)(2,1)}, bf16[8,4,32,128]{3,2,1,0:T(8,128)(2,1)}) custom-call(bf16[2,4,24,4096]{3,2,1,0:T(8,128)(2,1)} %refs_0_.3, f32[4,4096]{1,0:T(4,128)} %refs_1_.3, s32[24,4096]{1,0:T(8,128)} %refs_2_.3, f32[1152,128]{1,0:T(8,128)} %constant.6.clone.refs_3_), custom_call_target="tpu_custom_call" | custom-call | flops 4000000000 | bytes 2000000 | tf_op jit(solution)/shard_map/pallas_call | solution.py:319
  9.3 5.1 %all-to-all-start = ((bf16[8,13,32,128]{3,2,1,0:T(8,128)(2,1)}), bf16[8,13,32,128]{3,2,1,0:T(8,128)(2,1)S(1)}, u32[]{:S(2)}, u32[]{:S(2)}) async-start(bf16[8,13,32,128]{3,2,1,0:T(8,128)(2,1)} %get-tuple-element.7), calls=%async_computation | async-start | bytes 1703936 | tf_op jit(solution)/shard_map/all_to_all | solution.py:681
  14.4 7.8 %shard_map.74 = bf16[8,13,32,128]{3,2,1,0:T(8,128)(2,1)} custom-call(bf16[2,4,24,4096]{3,2,1,0:T(8,128)(2,1)} %refs_0_.3, f32[4,4096]{1,0:T(4,128)} %refs_1_.3, s32[24,4096]{1,0:T(8,128)} %refs_2_.3, f32[1152,128]{1,0:T(8,128)} %constant.6.clone.refs_3_, bf16[8,4,32,128]{3,2,1,0:T(8,128)(2,1)} %get-tuple-element.8.refs_4_), custom_call_target="tpu_custom_call" | custom-call | flops 2000000000 | bytes 2000000 | tf_op jit(solution)/shard_map/pallas_call | solution.py:319
  22.2 4.7 %all-to-all-done.own = bf16[8,13,32,128]{3,2,1,0:T(8,128)(2,1)S(1)} async-done(((bf16[8,13,32,128]{3,2,1,0:T(8,128)(2,1)}), bf16[8,13,32,128]{3,2,1,0:T(8,128)(2,1)S(1)}, u32[]{:S(2)}, u32[]{:S(2)}) %all-to-all-start) | async-done | bytes 852000 | tf_op jit(solution)/shard_map/all_to_all | solution.py:681
  26.9 0.0 copy-start
  26.9 3.5 %all-to-all-start.1 = ((bf16[8,13,32,128]{3,2,1,0:T(8,128)(2,1)}), bf16[8,13,32,128]{3,2,1,0:T(8,128)(2,1)S(1)}, u32[]{:S(2)}, u32[]{:S(2)}) async-start(bf16[8,13,32,128]{3,2,1,0:T(8,128)(2,1)} %shard_map.74), calls=%async_computation.1 | async-start | bytes 1703936 | tf_op jit(solution)/shard_map/all_to_all | solution.py:681
  30.5 0.1 fusion
  30.6 0.0 copy-done
  30.6 3.5 %collective-permute-start.1 = (bf16[8,7,32,128]{3,2,1,0:T(8,128)(2,1)S(1)}, bf16[8,7,32,128]{3,2,1,0:T(8,128)(2,1)S(1)}, u32[]{:S(2)}, u32[]{:S(2)}) collective-permute-start(bf16[8,7,32,128]{3,2,1,0:T(8,128)(2,1)S(1)} %get-tuple-element.9), channel_id=1, source_target_pairs={{8,0},{16,8},{24,16},{32,24},{40,32},{48,40},{56,48},{64,56},{72,6... | collective-permute-start | bytes 1376264 | tf_op jit(solution)/shard_map/ppermute | solution.py:691
  34.1 4.4 %collective-permute-start = (bf16[8,7,32,128]{3,2,1,0:T(8,128)(2,1)S(1)}, bf16[8,7,32,128]{3,2,1,0:T(8,128)(2,1)S(1)}, u32[]{:S(2)}, u32[]{:S(2)}) collective-permute-start(bf16[8,7,32,128]{3,2,1,0:T(8,128)(2,1)S(1)} %get-tuple-element.10), channel_id=1, source_target_pairs={{0,8},{8,16},{16,24},{24,32},{32,40},{40,48},{48,56},{56,64},{64,7... | collective-permute-start | bytes 1376264 | tf_op jit(solution)/shard_map/ppermute | solution.py:690
  38.5 5.1 %shard_map.75.early_sums = f32[2,2,576,128]{3,2,1,0:T(8,128)} custom-call(bf16[8,13,32,128]{3,2,1,0:T(8,128)(2,1)} %copy-done), custom_call_target="tpu_custom_call" | custom-call | flops 6000000000 | bytes 2000000 | tf_op jit(solution)/shard_map/pallas_call | solution.py:474
  43.6 9.6 %collective-permute-done.1.below = bf16[8,7,32,128]{3,2,1,0:T(8,128)(2,1)S(1)} collective-permute-done((bf16[8,7,32,128]{3,2,1,0:T(8,128)(2,1)S(1)}, bf16[8,7,32,128]{3,2,1,0:T(8,128)(2,1)S(1)}, u32[]{:S(2)}, u32[]{:S(2)}) %collective-permute-start.1) | collective-permute-done | bytes 458784 | tf_op jit(solution)/shard_map/ppermute | solution.py:691
  53.2 0.0 copy-start.2
  53.2 0.0 collective-permute-done.above
  53.2 0.8 copy-done.2
  54.0 0.0 copy-start.3
  54.0 0.8 copy-done.3
  54.8 8.2 %shard_map.76.halo_sums = f32[4,2,576,128]{3,2,1,0:T(8,128)} custom-call(bf16[8,13,32,128]{3,2,1,0:T(8,128)(2,1)} %copy-done, bf16[8,7,32,128]{3,2,1,0:T(8,128)(2,1)} %copy-done.3, bf16[8,7,32,128]{3,2,1,0:T(8,128)(2,1)} %copy-done.2), custom_call_target="tpu_custom_call" | custom-call | flops 12000000000 | bytes 2000000 | tf_op jit(solution)/shard_map/pallas_call | solution.py:474
  63.0 0.0 all-to-all-done.1.rest
  63.0 0.0 copy-start.1
  63.0 0.9 %copy-done.1 = bf16[8,13,32,128]{3,2,1,0:T(8,128)(2,1)} copy-done((bf16[8,13,32,128]{3,2,1,0:T(8,128)(2,1)}, bf16[8,13,32,128]{3,2,1,0:T(8,128)(2,1)S(1)}, u32[]{:S(2)}) %copy-start.1) | copy-done | bytes 851992
  63.9 15.3 %link_windows.1 = f32[2,6,32,128]{3,2,1,0:T(8,128)} custom-call(bf16[8,13,32,128]{3,2,1,0:T(8,128)(2,1)} %copy-done, bf16[8,13,32,128]{3,2,1,0:T(8,128)(2,1)} %copy-done.1, bf16[8,7,32,128]{3,2,1,0:T(8,128)(2,1)} %copy-done.3, bf16[8,7,32,128]{3,2,1,0:T(8,128)(2,1)} %copy-done.2, f32[2,2,576,128]{3,2,1,0:T(8,128)} %shard_map.75.early_sums, ...), custom_call_target="tpu_custom_call" | custom-call | flops 20000000000 | bytes 8000000 | tf_op jit(solution)/shard_map/link_windows/pallas_call | solution.py:655
Async XLA Ops:
  9.3 17.6 %all-to-all-start = ((bf16[8,13,32,128]{3,2,1,0:T(8,128)(2,1)}), bf16[8,13,32,128]{3,2,1,0:T(8,128)(2,1)S(1)}, u32[]{:S(2)}, u32[]{:S(2)}) async-start(bf16[8,13,32,128]{3,2,1,0:T(8,128)(2,1)} %get-tuple-element.7), calls=%async_computation | async-start | bytes 1703936 | tf_op jit(solution)/shard_map/all_to_all | solution.py:681
  26.9 3.6 %copy-start = (bf16[8,13,32,128]{3,2,1,0:T(8,128)(2,1)}, bf16[8,13,32,128]{3,2,1,0:T(8,128)(2,1)S(1)}, u32[]{:S(2)}) copy-start(bf16[8,13,32,128]{3,2,1,0:T(8,128)(2,1)S(1)} %all-to-all-done.own) | copy-start | bytes 2555908
  26.9 36.0 %all-to-all-start.1 = ((bf16[8,13,32,128]{3,2,1,0:T(8,128)(2,1)}), bf16[8,13,32,128]{3,2,1,0:T(8,128)(2,1)S(1)}, u32[]{:S(2)}, u32[]{:S(2)}) async-start(bf16[8,13,32,128]{3,2,1,0:T(8,128)(2,1)} %shard_map.74), calls=%async_computation.1 | async-start | bytes 1703936 | tf_op jit(solution)/shard_map/all_to_all | solution.py:681
  30.6 22.6 %collective-permute-start.1 = (bf16[8,7,32,128]{3,2,1,0:T(8,128)(2,1)S(1)}, bf16[8,7,32,128]{3,2,1,0:T(8,128)(2,1)S(1)}, u32[]{:S(2)}, u32[]{:S(2)}) collective-permute-start(bf16[8,7,32,128]{3,2,1,0:T(8,128)(2,1)S(1)} %get-tuple-element.9), channel_id=1, source_target_pairs={{8,0},{16,8},{24,16},{32,24},{40,32},{48,40},{56,48},{64,56},{72,6... | collective-permute-start | bytes 1376264 | tf_op jit(solution)/shard_map/ppermute | solution.py:691
  34.1 19.1 %collective-permute-start = (bf16[8,7,32,128]{3,2,1,0:T(8,128)(2,1)S(1)}, bf16[8,7,32,128]{3,2,1,0:T(8,128)(2,1)S(1)}, u32[]{:S(2)}, u32[]{:S(2)}) collective-permute-start(bf16[8,7,32,128]{3,2,1,0:T(8,128)(2,1)S(1)} %get-tuple-element.10), channel_id=1, source_target_pairs={{0,8},{8,16},{16,24},{24,32},{32,40},{40,48},{48,56},{56,64},{64,7... | collective-permute-start | bytes 1376264 | tf_op jit(solution)/shard_map/ppermute | solution.py:690
  53.2 0.8 copy-start.2
  54.0 0.8 %copy-start.3 = (bf16[8,7,32,128]{3,2,1,0:T(8,128)(2,1)}, bf16[8,7,32,128]{3,2,1,0:T(8,128)(2,1)S(1)}, u32[]{:S(2)}) copy-start(bf16[8,7,32,128]{3,2,1,0:T(8,128)(2,1)S(1)} %collective-permute-done.above) | copy-start | bytes 1376260
  63.0 0.9 %copy-start.1 = (bf16[8,13,32,128]{3,2,1,0:T(8,128)(2,1)}, bf16[8,13,32,128]{3,2,1,0:T(8,128)(2,1)S(1)}, u32[]{:S(2)}) copy-start(bf16[8,13,32,128]{3,2,1,0:T(8,128)(2,1)S(1)} %all-to-all-done.1.rest) | copy-start | bytes 2555908

commit v6 on v4

--- a/solution.py
+++ b/solution.py
@@ -21,6 +21,7 @@
 HERE = 4
 FIRST, SECOND = (0, 16), (8,)
 KEPT = (6, 7, 16, 17)
+GROUP_FIRST, GROUP_SECOND = 8, 16
 SHIFTS = 17
 PAIRS = (SHIFTS + 1) * DATES
 WRAP = 48
@@ -140,33 +141,18 @@
         copies["mask", i] = pltpu.make_async_copy(
             mask.at[pl.ds(block, 8)], mask_in.at[pl.ds(8 * i, 8)], sem.at[8 * count + i]
         )
-    for copy in stack_copies + list(copies.values()):
+    first_copies = [copies["gains"], copies["table"]]
+    last_copies = [copies["mask", i] for i in range(count)]
+    for copy in first_copies + stack_copies + last_copies:
         copy.start()
     lanes = lax.broadcasted_iota(jnp.int32, (8, 128), 1)
-
-    def ahead(block, carry):
-        rows = pl.ds(pl.multiple_of(block * 8, 8), 8)
-
-        def store(q, re, im):
-            spec[0, q, rows] = re
-            spec[1, q, rows] = im
-
-        for c in range(2):
-            pltpu.make_async_copy(
-                stack.at[0, 0, pl.ds(0, 8)], raw.at[c, block], sem.at[c * HERE * count + block]
-            ).wait()
-
-        def load(n):
-            lanes = slice(n * 128, (n + 1) * 128)
-            return (
-                raw[0, block, :, lanes].astype(jnp.float32),
-                raw[1, block, :, lanes].astype(jnp.float32),
-            )
-
-        dft_planes(load, hold, store, -1)
-        return carry
-
-    lax.fori_loop(0, rows_here // 8, ahead, 0)
+    row = lax.broadcasted_iota(jnp.int32, (512, 128), 0)
+    column = lax.broadcasted_iota(jnp.int32, (512, 128), 1)
+    for p in range(4):
+        place[:, 128 * p : 128 * p + 128] = jnp.where(row == 4 * column + p, 1.0, 0.0).astype(
+            jnp.bfloat16
+        )
+
     copies["gains"].wait()
     for n in range(PLANES):
         four = gains_in[:, n * 128 : (n + 1) * 128]
@@ -175,7 +161,6 @@
     for d in range(HERE):
         turned = jnp.transpose(gain[d])
         gain[d] = jnp.concatenate([turned[32 * w : 32 * w + 32] for w in range(4)], axis=1)
-    steps = PLANES // group
     copies["table"].wait()
     for i, target in enumerate((forward, inverse)):
         for half in range(2):
@@ -183,31 +168,54 @@
             high, low = split(table_in[begin : begin + 256])
             for j, part in enumerate((high, high, low)):
                 target[256 * j : 256 * j + 256, 128 * half : 128 * half + 128] = part
-    row = lax.broadcasted_iota(jnp.int32, (512, 128), 0)
-    column = lax.broadcasted_iota(jnp.int32, (512, 128), 1)
-    for p in range(4):
-        place[:, 128 * p : 128 * p + 128] = jnp.where(row == 4 * column + p, 1.0, 0.0).astype(
-            jnp.bfloat16
-        )
-
-    def middle(step, carry):
-        now = jnp.minimum(step, steps - 1) * group
-        past = jnp.maximum(step - 1, 0) * group
+
+    def ahead(block, carry):
+        rows = pl.ds(pl.multiple_of(block * 8, 8), 8)
+
+        def store(q, re, im):
+            spec[0, q, rows] = re
+            spec[1, q, rows] = im
+
+        for c in range(2):
+            pltpu.make_async_copy(
+                stack.at[0, 0, pl.ds(0, 8)], raw.at[c, block], sem.at[c * HERE * count + block]
+            ).wait()
+
+        def load(n):
+            lanes = slice(n * 128, (n + 1) * 128)
+            return (
+                raw[0, block, :, lanes].astype(jnp.float32),
+                raw[1, block, :, lanes].astype(jnp.float32),
+            )
+
+        dft_planes(load, hold, store, -1)
+        return carry
+
+    lax.fori_loop(0, rows_here // 8, ahead, 0)
+    steps = PLANES // group
+
+    def ahead_part(step):
+        now = step * group
         parts = []
         for i in range(group):
             tc = table_in[pl.ds(1024 + now + i, 1), :]
             ts = table_in[pl.ds(1056 + now + i, 1), :]
             re, im = spec[0, now + i], spec[1, now + i]
             parts.append(jnp.concatenate([re * tc + im * ts, im * tc - re * ts], axis=1))
-        back = dot3(held[lax.rem(step + 1, 2)], inverse[...])
         found = dot3(jnp.concatenate(parts, axis=0), forward[...])
+        slot = step % 2 if isinstance(step, int) else lax.rem(step, 2)
         for i in range(group):
             for d in range(HERE):
                 row = gain[d, pl.ds(now + i, 1), :]
                 begin = i * rows_here + d * lines_here
-                held[lax.rem(step, 2), begin : begin + lines_here] = found[
+                held[slot, begin : begin + lines_here] = found[
                     begin : begin + lines_here
                 ] * jnp.concatenate([row, row], axis=1)
+
+    def back_part(step):
+        past = step * group
+        slot = step % 2 if isinstance(step, int) else lax.rem(step, 2)
+        back = dot3(held[slot], inverse[...])
         for i in range(group):
             tc = table_in[pl.ds(1088 + past + i, 1), :]
             ts = table_in[pl.ds(1120 + past + i, 1), :]
@@ -215,9 +223,15 @@
             im = back[i * rows_here : (i + 1) * rows_here, 128:]
             first[0, past + i] = re * tc - im * ts
             first[1, past + i] = im * tc + re * ts
-        return carry
-
-    lax.fori_loop(0, steps + 1, middle, 0)
+
+    def middle(step, carry):
+        back_part(step - 1)
+        ahead_part(step)
+        return carry
+
+    ahead_part(0)
+    lax.fori_loop(1, steps, middle, 0)
+    back_part(steps - 1)
 
     for i in range(count):
         copies["mask", i].wait()
@@ -273,9 +287,7 @@
             jnp.bfloat16
         )
 
-    def one_tile(t):
-        left = jnp.concatenate([gather(4 * t + v) for v in range(4)], axis=1).astype(jnp.bfloat16)
-        found = jnp.dot(left, place[...], preferred_element_type=jnp.float32)
+    def one_tile(t, found):
         for index in range(lines_here):
             line = blocks[index // 8] + index % 8
             value = jnp.concatenate(
@@ -292,8 +304,17 @@
         put_tail(lax.rem(t + TILES - 1, TILES), found)
 
     def tile(step, carry):
-        one_tile(2 * step)
-        one_tile(2 * step + 1)
+        left = [
+            jnp.concatenate([gather(8 * step + 4 * i + v) for v in range(4)], axis=1)
+            for i in range(2)
+        ]
+        found = jnp.dot(
+            jnp.concatenate(left, axis=0).astype(jnp.bfloat16),
+            place[...],
+            preferred_element_type=jnp.float32,
+        )
+        for i in range(2):
+            one_tile(2 * step + i, found[8 * lines_here * i : 8 * lines_here * (i + 1)])
         return carry
 
     lax.fori_loop(0, TILES // 2, tile, 0)
@@ -638,9 +659,9 @@
     def move(tiles):
         return lax.all_to_all(tiles, "dr", split_axis=0, concat_axis=0, tiled=True)
 
-    tiles, kept = filter_lines(stack, range_filter, scatter_mask, FIRST, 4)
+    tiles, kept = filter_lines(stack, range_filter, scatter_mask, FIRST, GROUP_FIRST)
     own = move(tiles)
-    tiles = filter_lines(stack, range_filter, scatter_mask, SECOND, 8, kept)
+    tiles = filter_lines(stack, range_filter, scatter_mask, SECOND, GROUP_SECOND, kept)
     rest = move(tiles)
     count = lax.axis_size("az")
     down = [(i, i + 1) for i in range(count - 1)]

time: 71 us -> 69.9 us (0.985)
  the two profiles are of different devices: /device:TPU:66 before, /device:TPU:2 now
where the time goes in v6:
time: 69.9 us; the launch traced here: 69.6 us
  Pallas kernels  37.1 us (53%)
  waiting for transfers between devices  17.1 us (24%)
  starting transfers between devices  15.1 us (22%)
    all_to_all x2, waiting for transfers between devices, move(): return lax.all_to_all(tiles, 'dr', split_axis=0, concat_axis=0, tiled=True)  17.1 us
    pallas_call x2, Pallas kernels, filter_lines(): pl.pallas_call(kernel, out_shape=(tiles, rest) if blocks == FIRST else ti...  15 us
    pallas_call x1, Pallas kernels, link_windows(): pl.pallas_call(link_kernel, out_shape=jax.ShapeDtypeStruct((2, 6, DATES,...  14.9 us
    all_to_all x2, starting transfers between devices, move(): return lax.all_to_all(tiles, 'dr', split_axis=0, concat_axis=0, tiled=True)  10.7 us
    pallas_call x2, Pallas kernels, own_rows(): pl.pallas_call(kernel, out_shape=jax.ShapeDtypeStruct((count, 2, PAIRS, 1...  7.16 us
    ppermute x1, starting transfers between devices, on_device(): above = lax.ppermute(own[:, 6:13], 'az', down)  3.06 us
  transfers between devices with their start and end apart: 4, of which 2 were waited for; matrix products, arithmetic and copies ran while one was open for 0% of the time, Pallas kernels for 20%

profile of v6, /device:TPU:2, one launch (start us, length us, event | category | flops | bytes accessed | tf_op | source)
XLA Modules:
  0.0 69.6 jit_solution(7110573242725152859)
XLA Ops:
  0.0 8.2 %shard_map.73 = (bf16[8,13,32,128]{3,2,1,0:T(8,128)(2,1)}, bf16[8,4,32,128]{3,2,1,0:T(8,128)(2,1)}) custom-call(bf16[2,4,24,4096]{3,2,1,0:T(8,128)(2,1)} %refs_0_.3, f32[4,4096]{1,0:T(4,128)} %refs_1_.3, s32[24,4096]{1,0:T(8,128)} %refs_2_.3, f32[1152,128]{1,0:T(8,128)} %constant.6.clone.refs_3_), custom_call_target="tpu_custom_call" | custom-call | flops 4000000000 | bytes 2000000 | tf_op jit(solution)/shard_map/pallas_call | solution.py:340
  8.2 5.9 %all-to-all-start = ((bf16[8,13,32,128]{3,2,1,0:T(8,128)(2,1)}), bf16[8,13,32,128]{3,2,1,0:T(8,128)(2,1)S(1)}, u32[]{:S(2)}, u32[]{:S(2)}) async-start(bf16[8,13,32,128]{3,2,1,0:T(8,128)(2,1)} %get-tuple-element.7), calls=%async_computation | async-start | bytes 1703936 | tf_op jit(solution)/shard_map/all_to_all | solution.py:660
  14.1 6.8 %shard_map.74 = bf16[8,13,32,128]{3,2,1,0:T(8,128)(2,1)} custom-call(bf16[2,4,24,4096]{3,2,1,0:T(8,128)(2,1)} %refs_0_.3, f32[4,4096]{1,0:T(4,128)} %refs_1_.3, s32[24,4096]{1,0:T(8,128)} %refs_2_.3, f32[1152,128]{1,0:T(8,128)} %constant.6.clone.refs_3_, bf16[8,4,32,128]{3,2,1,0:T(8,128)(2,1)} %get-tuple-element.8.refs_4_), custom_call_target="tpu_custom_call" | custom-call | flops 2000000000 | bytes 2000000 | tf_op jit(solution)/shard_map/pallas_call | solution.py:340
  20.9 4.9 %all-to-all-done.own = bf16[8,13,32,128]{3,2,1,0:T(8,128)(2,1)S(1)} async-done(((bf16[8,13,32,128]{3,2,1,0:T(8,128)(2,1)}), bf16[8,13,32,128]{3,2,1,0:T(8,128)(2,1)S(1)}, u32[]{:S(2)}, u32[]{:S(2)}) %all-to-all-start) | async-done | bytes 852000 | tf_op jit(solution)/shard_map/all_to_all | solution.py:660
  25.8 4.9 %all-to-all-start.1 = ((bf16[8,13,32,128]{3,2,1,0:T(8,128)(2,1)}), bf16[8,13,32,128]{3,2,1,0:T(8,128)(2,1)S(1)}, u32[]{:S(2)}, u32[]{:S(2)}) async-start(bf16[8,13,32,128]{3,2,1,0:T(8,128)(2,1)} %shard_map.74), calls=%async_computation.1 | async-start | bytes 1703936 | tf_op jit(solution)/shard_map/all_to_all | solution.py:660
  30.7 0.1 fusion
  30.8 1.3 %collective-permute-start.1 = (bf16[8,7,32,128]{3,2,1,0:T(8,128)(2,1)S(1)}, bf16[8,7,32,128]{3,2,1,0:T(8,128)(2,1)S(1)}, u32[]{:S(2)}, u32[]{:S(2)}) collective-permute-start(bf16[8,7,32,128]{3,2,1,0:T(8,128)(2,1)S(1)} %get-tuple-element.9), channel_id=1, source_target_pairs={{8,0},{16,8},{24,16},{32,24},{40,32},{48,40},{56,48},{64,56},{72,6... | collective-permute-start | bytes 1376264 | tf_op jit(solution)/shard_map/ppermute | solution.py:670
  32.1 3.1 %collective-permute-start = (bf16[8,7,32,128]{3,2,1,0:T(8,128)(2,1)S(1)}, bf16[8,7,32,128]{3,2,1,0:T(8,128)(2,1)S(1)}, u32[]{:S(2)}, u32[]{:S(2)}) collective-permute-start(bf16[8,7,32,128]{3,2,1,0:T(8,128)(2,1)S(1)} %get-tuple-element.10), channel_id=1, source_target_pairs={{0,8},{8,16},{16,24},{24,32},{32,40},{40,48},{48,56},{56,64},{64,7... | collective-permute-start | bytes 1376264 | tf_op jit(solution)/shard_map/ppermute | solution.py:669
  35.2 12.2 %all-to-all-done.1.rest = bf16[8,13,32,128]{3,2,1,0:T(8,128)(2,1)S(1)} async-done(((bf16[8,13,32,128]{3,2,1,0:T(8,128)(2,1)}), bf16[8,13,32,128]{3,2,1,0:T(8,128)(2,1)S(1)}, u32[]{:S(2)}, u32[]{:S(2)}) %all-to-all-start.1) | async-done | bytes 852000 | tf_op jit(solution)/shard_map/all_to_all | solution.py:660
  47.4 4.3 %shard_map.76.inner = f32[3,2,576,128]{3,2,1,0:T(8,128)S(1)} custom-call(bf16[8,13,32,128]{3,2,1,0:T(8,128)(2,1)S(1)} %all-to-all-done.1.rest), custom_call_target="tpu_custom_call" | custom-call | flops 8999999488 | bytes 2000000 | tf_op jit(solution)/shard_map/pallas_call | solution.py:470
  51.7 0.0 copy-start
  51.7 0.0 copy-start.1
  51.7 2.9 %shard_map.75.early = f32[2,2,576,128]{3,2,1,0:T(8,128)S(1)} custom-call(bf16[8,13,32,128]{3,2,1,0:T(8,128)(2,1)S(1)} %all-to-all-done.own), custom_call_target="tpu_custom_call" | custom-call | flops 6000000000 | bytes 2000000 | tf_op jit(solution)/shard_map/pallas_call | solution.py:470
  54.6 0.0 collective-permute-done.1.below
  54.6 0.0 collective-permute-done.above
  54.6 0.0 copy-done
  54.6 0.0 copy-done.1
  54.6 14.9 %link_windows.1 = f32[2,6,32,128]{3,2,1,0:T(8,128)} custom-call(bf16[8,13,32,128]{3,2,1,0:T(8,128)(2,1)S(1)} %all-to-all-done.own, bf16[8,13,32,128]{3,2,1,0:T(8,128)(2,1)S(1)} %all-to-all-done.1.rest, bf16[8,7,32,128]{3,2,1,0:T(8,128)(2,1)S(1)} %collective-permute-done.above, bf16[8,7,32,128]{3,2,1,0:T(8,128)(2,1)S(1)} %collective-permute-done.1.below, ...), custom_call_target="tpu_custom_call" | custom-call | flops 20000000000 | bytes 8000000 | tf_op jit(solution)/shard_map/link_windows/pallas_call | solution.py:638
Async XLA Ops:
  8.2 17.6 %all-to-all-start = ((bf16[8,13,32,128]{3,2,1,0:T(8,128)(2,1)}), bf16[8,13,32,128]{3,2,1,0:T(8,128)(2,1)S(1)}, u32[]{:S(2)}, u32[]{:S(2)}) async-start(bf16[8,13,32,128]{3,2,1,0:T(8,128)(2,1)} %get-tuple-element.7), calls=%async_computation | async-start | bytes 1703936 | tf_op jit(solution)/shard_map/all_to_all | solution.py:660
  25.8 21.5 %all-to-all-start.1 = ((bf16[8,13,32,128]{3,2,1,0:T(8,128)(2,1)}), bf16[8,13,32,128]{3,2,1,0:T(8,128)(2,1)S(1)}, u32[]{:S(2)}, u32[]{:S(2)}) async-start(bf16[8,13,32,128]{3,2,1,0:T(8,128)(2,1)} %shard_map.74), calls=%async_computation.1 | async-start | bytes 1703936 | tf_op jit(solution)/shard_map/all_to_all | solution.py:660
  30.8 23.7 %collective-permute-start.1 = (bf16[8,7,32,128]{3,2,1,0:T(8,128)(2,1)S(1)}, bf16[8,7,32,128]{3,2,1,0:T(8,128)(2,1)S(1)}, u32[]{:S(2)}, u32[]{:S(2)}) collective-permute-start(bf16[8,7,32,128]{3,2,1,0:T(8,128)(2,1)S(1)} %get-tuple-element.9), channel_id=1, source_target_pairs={{8,0},{16,8},{24,16},{32,24},{40,32},{48,40},{56,48},{64,56},{72,6... | collective-permute-start | bytes 1376264 | tf_op jit(solution)/shard_map/ppermute | solution.py:670
  32.1 22.5 %collective-permute-start = (bf16[8,7,32,128]{3,2,1,0:T(8,128)(2,1)S(1)}, bf16[8,7,32,128]{3,2,1,0:T(8,128)(2,1)S(1)}, u32[]{:S(2)}, u32[]{:S(2)}) collective-permute-start(bf16[8,7,32,128]{3,2,1,0:T(8,128)(2,1)S(1)} %get-tuple-element.10), channel_id=1, source_target_pairs={{0,8},{8,16},{16,24},{24,32},{32,40},{40,48},{48,56},{56,64},{64,7... | collective-permute-start | bytes 1376264 | tf_op jit(solution)/shard_map/ppermute | solution.py:669
  51.7 2.9 %copy-start = (bf16[256,768]{1,0:T(8,128)(2,1)S(1)}, bf16[256,768]{1,0:T(8,128)(2,1)}, u32[]{:S(2)}) copy-start(bf16[256,768]{1,0:T(8,128)(2,1)} %constant.8.clone.band) | copy-start | bytes 1179652
  51.7 2.9 %copy-start.1 = (bf16[256,128]{1,0:T(8,128)(2,1)S(1)}, bf16[256,128]{1,0:T(8,128)(2,1)}, u32[]{:S(2)}) copy-start(bf16[256,128]{1,0:T(8,128)(2,1)} %constant.7.clone.near) | copy-start | bytes 196612

commit v7 on v6

--- a/solution.py
+++ b/solution.py
@@ -409,14 +409,14 @@
 
         def some(chunk, totals):
             totals = [list(totals[3 * i : 3 * i + 3]) for i in range(WIDTH)]
-            for step in range(unit):
-                plane = base + chunk * unit + step
-                mine = (z_sum[plane, own], z_re[plane, own], z_im[plane, own])
+            for step in range(0, unit, 2):
+                pair = [base + chunk * unit + step + q for q in range(2)]
+                mine = [(z_sum[p, own], z_re[p, own], z_im[p, own]) for p in pair]
                 for i in range(WIDTH):
                     other = pl.ds(begin + 1 + i, 8)
-                    others = (z_re[plane, other], z_sum[plane, other], z_dif[plane, other])
-                    for k in range(3):
-                        totals[i][k] = totals[i][k] + others[k] * mine[k]
+                    for k, ref in enumerate((z_re, z_sum, z_dif)):
+                        terms = [ref[p, other] * part[k] for p, part in zip(pair, mine)]
+                        totals[i][k] = totals[i][k] + (terms[0] + terms[1])
             return tuple(t for total in totals for t in total)
 
         zero = jnp.zeros((8, 128), jnp.float32)
@@ -563,11 +563,11 @@
             put_vec(0, group, weights[group])
 
         def iterate(real, last):
-            found = []
-            for group in range(4):
-                row = 8 * group
-                re_parts, im_parts = [], []
-                for s in range(SHIFTS):
+            sums = [[None, None] for _ in range(4)]
+            for s in range(SHIFTS):
+                for group in range(4):
+                    row = 8 * group
+                    re_parts, im_parts = [], []
                     terms = [(2 * s * DATES + row, DATES + row + s, 1)]
                     if 0 < s < SHIFTS - 1:
                         terms.append((2 * s * DATES + DATES + row - s, DATES + row - s, -1))
@@ -591,7 +591,11 @@
                         re_parts.append(re)
                         if im is not None:
                             im_parts.append(im)
-                found.append((sum_two(re_parts), sum_two(im_parts)))
+                    for k, parts in enumerate((re_parts, im_parts)):
+                        if parts:
+                            part = parts[0] if len(parts) == 1 else parts[0] + parts[1]
+                            sums[group][k] = part if sums[group][k] is None else sums[group][k] + part
+            found = sums
             for group in range(4):
                 u_re = found[group][0] * weights[group]
                 u_im = found[group][1] * weights[group]
@@ -605,18 +609,12 @@
                     put_vec(1, group, x_im * weights[group])
 
         iterate(True, False)
-        lax.fori_loop(0, ITERS - 2, lambda i, carry: (iterate(False, False), carry)[1], 0)
+        for _ in range(ITERS - 2):
+            iterate(False, False)
         iterate(False, True)
         return carry
 
     lax.fori_loop(0, 6, window_row, 0)
-
-
-def sum_two(parts):
-    sums = parts[:2]
-    for i, part in enumerate(parts[2:]):
-        sums[i % 2] = sums[i % 2] + part
-    return sums[0] + sums[1]
 
 
 def tail_band():

time: 69.9 us -> 67.4 us (0.964)
  Pallas kernels: 37.1 us -> 34.7 us
    pallas_call x1, Pallas kernels: 14.9 us -> 13.1 us  [link_windows(): pl.pallas_call(link_kernel, out_shape=jax.ShapeDtypeStruct((2, 6, DATES,...]
where the time goes in v7:
time: 67.4 us; the launch traced here: 67.1 us
  Pallas kernels  34.7 us (51%)
  waiting for transfers between devices  17.1 us (25%)
  starting transfers between devices  15.1 us (22%)
    all_to_all x2, waiting for transfers between devices, move(): return lax.all_to_all(tiles, 'dr', split_axis=0, concat_axis=0, tiled=True)  17.1 us
    pallas_call x2, Pallas kernels, filter_lines(): pl.pallas_call(kernel, out_shape=(tiles, rest) if blocks == FIRST else ti...  15 us
    pallas_call x1, Pallas kernels, link_windows(): pl.pallas_call(link_kernel, out_shape=jax.ShapeDtypeStruct((2, 6, DATES,...  13.1 us
    all_to_all x2, starting transfers between devices, move(): return lax.all_to_all(tiles, 'dr', split_axis=0, concat_axis=0, tiled=True)  10.7 us
    pallas_call x2, Pallas kernels, own_rows(): pl.pallas_call(kernel, out_shape=jax.ShapeDtypeStruct((count, 2, PAIRS, 1...  6.55 us
    ppermute x1, starting transfers between devices, on_device(): above = lax.ppermute(own[:, 6:13], 'az', down)  3.06 us
  transfers between devices with their start and end apart: 4, of which 2 were waited for; matrix products, arithmetic and copies ran while one was open for 0% of the time, Pallas kernels for 20%

profile of v7, /device:TPU:2, one launch (start us, length us, event | category | flops | bytes accessed | tf_op | source)
XLA Modules:
  0.0 67.1 jit_solution(11181080928510498369)
XLA Ops:
  0.0 8.2 %shard_map.73 = (bf16[8,13,32,128]{3,2,1,0:T(8,128)(2,1)}, bf16[8,4,32,128]{3,2,1,0:T(8,128)(2,1)}) custom-call(bf16[2,4,24,4096]{3,2,1,0:T(8,128)(2,1)} %refs_0_.3, f32[4,4096]{1,0:T(4,128)} %refs_1_.3, s32[24,4096]{1,0:T(8,128)} %refs_2_.3, f32[1152,128]{1,0:T(8,128)} %constant.6.clone.refs_3_), custom_call_target="tpu_custom_call" | custom-call | flops 4000000000 | bytes 2000000 | tf_op jit(solution)/shard_map/pallas_call | solution.py:340
  8.2 5.9 %all-to-all-start = ((bf16[8,13,32,128]{3,2,1,0:T(8,128)(2,1)}), bf16[8,13,32,128]{3,2,1,0:T(8,128)(2,1)S(1)}, u32[]{:S(2)}, u32[]{:S(2)}) async-start(bf16[8,13,32,128]{3,2,1,0:T(8,128)(2,1)} %get-tuple-element.7), calls=%async_computation | async-start | bytes 1703936 | tf_op jit(solution)/shard_map/all_to_all | solution.py:658
  14.1 6.8 %shard_map.74 = bf16[8,13,32,128]{3,2,1,0:T(8,128)(2,1)} custom-call(bf16[2,4,24,4096]{3,2,1,0:T(8,128)(2,1)} %refs_0_.3, f32[4,4096]{1,0:T(4,128)} %refs_1_.3, s32[24,4096]{1,0:T(8,128)} %refs_2_.3, f32[1152,128]{1,0:T(8,128)} %constant.6.clone.refs_3_, bf16[8,4,32,128]{3,2,1,0:T(8,128)(2,1)} %get-tuple-element.8.refs_4_), custom_call_target="tpu_custom_call" | custom-call | flops 2000000000 | bytes 2000000 | tf_op jit(solution)/shard_map/pallas_call | solution.py:340
  20.9 4.9 %all-to-all-done.own = bf16[8,13,32,128]{3,2,1,0:T(8,128)(2,1)S(1)} async-done(((bf16[8,13,32,128]{3,2,1,0:T(8,128)(2,1)}), bf16[8,13,32,128]{3,2,1,0:T(8,128)(2,1)S(1)}, u32[]{:S(2)}, u32[]{:S(2)}) %all-to-all-start) | async-done | bytes 852000 | tf_op jit(solution)/shard_map/all_to_all | solution.py:658
  25.8 4.9 %all-to-all-start.1 = ((bf16[8,13,32,128]{3,2,1,0:T(8,128)(2,1)}), bf16[8,13,32,128]{3,2,1,0:T(8,128)(2,1)S(1)}, u32[]{:S(2)}, u32[]{:S(2)}) async-start(bf16[8,13,32,128]{3,2,1,0:T(8,128)(2,1)} %shard_map.74), calls=%async_computation.1 | async-start | bytes 1703936 | tf_op jit(solution)/shard_map/all_to_all | solution.py:658
  30.7 0.1 fusion
  30.8 1.3 %collective-permute-start.1 = (bf16[8,7,32,128]{3,2,1,0:T(8,128)(2,1)S(1)}, bf16[8,7,32,128]{3,2,1,0:T(8,128)(2,1)S(1)}, u32[]{:S(2)}, u32[]{:S(2)}) collective-permute-start(bf16[8,7,32,128]{3,2,1,0:T(8,128)(2,1)S(1)} %get-tuple-element.9), channel_id=1, source_target_pairs={{8,0},{16,8},{24,16},{32,24},{40,32},{48,40},{56,48},{64,56},{72,6... | collective-permute-start | bytes 1376264 | tf_op jit(solution)/shard_map/ppermute | solution.py:668
  32.1 3.1 %collective-permute-start = (bf16[8,7,32,128]{3,2,1,0:T(8,128)(2,1)S(1)}, bf16[8,7,32,128]{3,2,1,0:T(8,128)(2,1)S(1)}, u32[]{:S(2)}, u32[]{:S(2)}) collective-permute-start(bf16[8,7,32,128]{3,2,1,0:T(8,128)(2,1)S(1)} %get-tuple-element.10), channel_id=1, source_target_pairs={{0,8},{8,16},{16,24},{24,32},{32,40},{40,48},{48,56},{56,64},{64,7... | collective-permute-start | bytes 1376264 | tf_op jit(solution)/shard_map/ppermute | solution.py:667
  35.2 12.2 %all-to-all-done.1.rest = bf16[8,13,32,128]{3,2,1,0:T(8,128)(2,1)S(1)} async-done(((bf16[8,13,32,128]{3,2,1,0:T(8,128)(2,1)}), bf16[8,13,32,128]{3,2,1,0:T(8,128)(2,1)S(1)}, u32[]{:S(2)}, u32[]{:S(2)}) %all-to-all-start.1) | async-done | bytes 852000 | tf_op jit(solution)/shard_map/all_to_all | solution.py:658
  47.4 3.9 %shard_map.76.inner = f32[3,2,576,128]{3,2,1,0:T(8,128)S(1)} custom-call(bf16[8,13,32,128]{3,2,1,0:T(8,128)(2,1)S(1)} %all-to-all-done.1.rest), custom_call_target="tpu_custom_call" | custom-call | flops 8999999488 | bytes 2000000 | tf_op jit(solution)/shard_map/pallas_call | solution.py:470
  51.3 0.0 copy-start
  51.3 0.0 copy-start.1
  51.3 2.6 %shard_map.75.early = f32[2,2,576,128]{3,2,1,0:T(8,128)S(1)} custom-call(bf16[8,13,32,128]{3,2,1,0:T(8,128)(2,1)S(1)} %all-to-all-done.own), custom_call_target="tpu_custom_call" | custom-call | flops 6000000000 | bytes 2000000 | tf_op jit(solution)/shard_map/pallas_call | solution.py:470
  54.0 0.0 collective-permute-done.1.below
  54.0 0.0 collective-permute-done.above
  54.0 0.0 copy-done
  54.0 0.0 copy-done.1
  54.0 13.1 %link_windows.1 = f32[2,6,32,128]{3,2,1,0:T(8,128)} custom-call(bf16[8,13,32,128]{3,2,1,0:T(8,128)(2,1)S(1)} %all-to-all-done.own, bf16[8,13,32,128]{3,2,1,0:T(8,128)(2,1)S(1)} %all-to-all-done.1.rest, bf16[8,7,32,128]{3,2,1,0:T(8,128)(2,1)S(1)} %collective-permute-done.above, bf16[8,7,32,128]{3,2,1,0:T(8,128)(2,1)S(1)} %collective-permute-done.1.below, ...), custom_call_target="tpu_custom_call" | custom-call | flops 20000000000 | bytes 8000000 | tf_op jit(solution)/shard_map/link_windows/pallas_call | solution.py:636
Async XLA Ops:
  8.2 17.6 %all-to-all-start = ((bf16[8,13,32,128]{3,2,1,0:T(8,128)(2,1)}), bf16[8,13,32,128]{3,2,1,0:T(8,128)(2,1)S(1)}, u32[]{:S(2)}, u32[]{:S(2)}) async-start(bf16[8,13,32,128]{3,2,1,0:T(8,128)(2,1)} %get-tuple-element.7), calls=%async_computation | async-start | bytes 1703936 | tf_op jit(solution)/shard_map/all_to_all | solution.py:658
  25.8 21.5 %all-to-all-start.1 = ((bf16[8,13,32,128]{3,2,1,0:T(8,128)(2,1)}), bf16[8,13,32,128]{3,2,1,0:T(8,128)(2,1)S(1)}, u32[]{:S(2)}, u32[]{:S(2)}) async-start(bf16[8,13,32,128]{3,2,1,0:T(8,128)(2,1)} %shard_map.74), calls=%async_computation.1 | async-start | bytes 1703936 | tf_op jit(solution)/shard_map/all_to_all | solution.py:658
  30.8 23.1 %collective-permute-start.1 = (bf16[8,7,32,128]{3,2,1,0:T(8,128)(2,1)S(1)}, bf16[8,7,32,128]{3,2,1,0:T(8,128)(2,1)S(1)}, u32[]{:S(2)}, u32[]{:S(2)}) collective-permute-start(bf16[8,7,32,128]{3,2,1,0:T(8,128)(2,1)S(1)} %get-tuple-element.9), channel_id=1, source_target_pairs={{8,0},{16,8},{24,16},{32,24},{40,32},{48,40},{56,48},{64,56},{72,6... | collective-permute-start | bytes 1376264 | tf_op jit(solution)/shard_map/ppermute | solution.py:668
  32.1 21.8 %collective-permute-start = (bf16[8,7,32,128]{3,2,1,0:T(8,128)(2,1)S(1)}, bf16[8,7,32,128]{3,2,1,0:T(8,128)(2,1)S(1)}, u32[]{:S(2)}, u32[]{:S(2)}) collective-permute-start(bf16[8,7,32,128]{3,2,1,0:T(8,128)(2,1)S(1)} %get-tuple-element.10), channel_id=1, source_target_pairs={{0,8},{8,16},{16,24},{24,32},{32,40},{40,48},{48,56},{56,64},{64,7... | collective-permute-start | bytes 1376264 | tf_op jit(solution)/shard_map/ppermute | solution.py:667
  51.3 2.7 %copy-start = (bf16[256,768]{1,0:T(8,128)(2,1)S(1)}, bf16[256,768]{1,0:T(8,128)(2,1)}, u32[]{:S(2)}) copy-start(bf16[256,768]{1,0:T(8,128)(2,1)} %constant.8.clone.band) | copy-start | bytes 1179652
  51.3 2.7 %copy-start.1 = (bf16[256,128]{1,0:T(8,128)(2,1)S(1)}, bf16[256,128]{1,0:T(8,128)(2,1)}, u32[]{:S(2)}) copy-start(bf16[256,128]{1,0:T(8,128)(2,1)} %constant.7.clone.near) | copy-start | bytes 196612

commit v8 on v7

--- a/solution.py
+++ b/solution.py
@@ -465,6 +465,13 @@
     gram_rows(fields, sums, 3, 0, 0)
 
 
+def upper_kernel(own, above, sums, *fields):
+    _, run = unpacker(fields)
+    run(above, 1, 0, 6)
+    run(own, 0, 6, 2)
+    gram_rows(fields, sums, 2, 0, 0)
+
+
 def own_rows(kernel, count, *chunks):
     field = pltpu.VMEM((count * 16, WRAP, 128), jnp.float32)
     return pl.pallas_call(
@@ -479,16 +486,14 @@
 
 
 def link_kernel(
-    own, rest, above, below, early, inner, near, band, out,
+    own, rest, above, below, upper, early, inner, near, band, out,
     z_re, z_im, z_sum, z_dif, sums, tails, extra, cov, vec,
 ):
     fields = (z_re, z_im, z_sum, z_dif)
     lanes = lax.broadcasted_iota(jnp.int32, (8, 128), 1)
     put, run = unpacker(fields)
-    run(above, 1, 0, 6)
-    run(own, 0, 6, 2)
-    run(own, 11, 8, 2)
-    run(below, 0, 10, 6)
+    run(own, 11, 0, 2)
+    run(below, 0, 2, 6)
     for group in range(4):
         pieces = []
         for source in (2 * group, 2 * group + 1):
@@ -511,14 +516,14 @@
                 piece.append(jnp.where(lanes < 108, value, 0.0))
             pieces.append(piece)
         for p in range(4):
-            put(64 + p, group, pieces[0][p], pieces[1][p])
+            put(32 + p, group, pieces[0][p], pieces[1][p])
 
     def store_tail(c, spot, value):
         tails[c, spot] = value
 
-    gram(fields, 64, 4, store_tail)
+    gram(fields, 32, 4, store_tail)
     tails[1, 0:DATES] = jnp.zeros((DATES, 128), jnp.float32)
-    gram_rows(fields, sums, 4, 0, 0)
+    gram_rows(fields, sums, 2, 0, 0)
     for c in range(2):
         high, low = split(tails[c])
         extra[c] = jnp.dot(
@@ -531,10 +536,10 @@
         spot = pl.ds(begin, size)
         twice = pl.multiple_of(step * 2 * size, 2 * size)
         for c in range(2):
-            rowsum = [sums[r, c, spot] for r in (0, 1)]
+            rowsum = [upper[r, c, spot] for r in (0, 1)]
             rowsum += [early[0, c, spot]] + [inner[r, c, spot] for r in range(3)]
             rowsum += [early[1, c, spot]]
-            rowsum += [sums[r, c, spot] for r in (2, 3)]
+            rowsum += [sums[r, c, spot] for r in (0, 1)]
             pairs = [rowsum[r] + rowsum[r + 1] for r in range(8)]
             value = jnp.concatenate([pairs[a] + pairs[a + 2] for a in range(6)], axis=0)
             high, low = split(value)
@@ -631,14 +636,14 @@
     return np.concatenate([near, near], axis=0).astype(jnp.bfloat16), both
 
 
-def link_windows(own, rest, above, below, early, inner):
-    field = pltpu.VMEM((68, WRAP, 128), jnp.float32)
+def link_windows(own, rest, above, below, upper, early, inner):
+    field = pltpu.VMEM((36, WRAP, 128), jnp.float32)
     found = pl.pallas_call(
         link_kernel,
         out_shape=jax.ShapeDtypeStruct((2, 6, DATES, 128), jnp.float32),
         scratch_shapes=[field] * 4
         + [
-            pltpu.VMEM((4, 2, PAIRS, 128), jnp.float32),
+            pltpu.VMEM((2, 2, PAIRS, 128), jnp.float32),
             pltpu.VMEM((2, PAIRS, 128), jnp.float32),
             pltpu.VMEM((2, PAIRS, 6 * 128), jnp.float32),
             pltpu.VMEM((6, 2, 2 * PAIRS, 128), jnp.float32),
@@ -649,7 +654,7 @@
             flops=20_000_000_000, bytes_accessed=8_000_000, transcendentals=0
         ),
         name="link_windows",
-    )(own, rest, above, below, early, inner, *tail_band())
+    )(own, rest, above, below, upper, early, inner, *tail_band())
     return jnp.transpose(found, (0, 2, 1, 3))
 
 
@@ -668,7 +673,8 @@
     below = lax.ppermute(own[:, 0:7], "az", up)
     early = own_rows(early_kernel, 2, own)
     inner = own_rows(inner_kernel, 3, rest)
-    return link_windows(own, rest, above, below, early, inner)
+    upper = own_rows(upper_kernel, 2, own, above)
+    return link_windows(own, rest, above, below, upper, early, inner)
 
 
 def solution(mesh):

time: 67.4 us -> 67.4 us (level)
    pallas_call x1, Pallas kernels: 13.1 us -> 10.4 us  [link_windows(): pl.pallas_call(link_kernel, out_shape=jax.ShapeDtypeStruct((2, 6, DATES,...]
    pallas_call x2 -> x3, Pallas kernels: 6.55 us -> 9.17 us  [own_rows(): pl.pallas_call(kernel, out_shape=jax.ShapeDtypeStruct((count, 2, PAIRS, 1...]
  transfers between devices with their start and end apart: 4 -> 4, of which waited for: 2 -> 2; matrix products, arithmetic and copies ran while one was open for 0% -> 0% of each run, Pallas kernels for 20% -> 24%
where the time goes in v8:
time: 67.4 us; the launch traced here: 67.1 us
  Pallas kernels  34.6 us (51%)
  waiting for transfers between devices  17.1 us (25%)
  starting transfers between devices  15.1 us (22%)
    all_to_all x2, waiting for transfers between devices, move(): return lax.all_to_all(tiles, 'dr', split_axis=0, concat_axis=0, tiled=True)  17.1 us
    pallas_call x2, Pallas kernels, filter_lines(): pl.pallas_call(kernel, out_shape=(tiles, rest) if blocks == FIRST else ti...  15 us
    all_to_all x2, starting transfers between devices, move(): return lax.all_to_all(tiles, 'dr', split_axis=0, concat_axis=0, tiled=True)  10.7 us
    pallas_call x1, Pallas kernels, link_windows(): pl.pallas_call(link_kernel, out_shape=jax.ShapeDtypeStruct((2, 6, DATES,...  10.4 us
    pallas_call x3, Pallas kernels, own_rows(): pl.pallas_call(kernel, out_shape=jax.ShapeDtypeStruct((count, 2, PAIRS, 1...  9.17 us
    ppermute x1, starting transfers between devices, on_device(): above = lax.ppermute(own[:, 6:13], 'az', down)  3.06 us
  transfers between devices with their start and end apart: 4, of which 2 were waited for; matrix products, arithmetic and copies ran while one was open for 0% of the time, Pallas kernels for 24%

profile of v8, /device:TPU:2, one launch (start us, length us, event | category | flops | bytes accessed | tf_op | source)
XLA Modules:
  0.0 67.1 jit_solution(2349343752213746927)
XLA Ops:
  0.0 8.2 %shard_map.73 = (bf16[8,13,32,128]{3,2,1,0:T(8,128)(2,1)}, bf16[8,4,32,128]{3,2,1,0:T(8,128)(2,1)}) custom-call(bf16[2,4,24,4096]{3,2,1,0:T(8,128)(2,1)} %refs_0_.3, f32[4,4096]{1,0:T(4,128)} %refs_1_.3, s32[24,4096]{1,0:T(8,128)} %refs_2_.3, f32[1152,128]{1,0:T(8,128)} %constant.6.clone.refs_3_), custom_call_target="tpu_custom_call" | custom-call | flops 4000000000 | bytes 2000000 | tf_op jit(solution)/shard_map/pallas_call | solution.py:340
  8.2 5.9 %all-to-all-start = ((bf16[8,13,32,128]{3,2,1,0:T(8,128)(2,1)}), bf16[8,13,32,128]{3,2,1,0:T(8,128)(2,1)S(1)}, u32[]{:S(2)}, u32[]{:S(2)}) async-start(bf16[8,13,32,128]{3,2,1,0:T(8,128)(2,1)} %get-tuple-element.7), calls=%async_computation | async-start | bytes 1703936 | tf_op jit(solution)/shard_map/all_to_all | solution.py:663
  14.1 6.8 %shard_map.74 = bf16[8,13,32,128]{3,2,1,0:T(8,128)(2,1)} custom-call(bf16[2,4,24,4096]{3,2,1,0:T(8,128)(2,1)} %refs_0_.3, f32[4,4096]{1,0:T(4,128)} %refs_1_.3, s32[24,4096]{1,0:T(8,128)} %refs_2_.3, f32[1152,128]{1,0:T(8,128)} %constant.6.clone.refs_3_, bf16[8,4,32,128]{3,2,1,0:T(8,128)(2,1)} %get-tuple-element.8.refs_4_), custom_call_target="tpu_custom_call" | custom-call | flops 2000000000 | bytes 2000000 | tf_op jit(solution)/shard_map/pallas_call | solution.py:340
  20.9 4.9 %all-to-all-done.own = bf16[8,13,32,128]{3,2,1,0:T(8,128)(2,1)S(1)} async-done(((bf16[8,13,32,128]{3,2,1,0:T(8,128)(2,1)}), bf16[8,13,32,128]{3,2,1,0:T(8,128)(2,1)S(1)}, u32[]{:S(2)}, u32[]{:S(2)}) %all-to-all-start) | async-done | bytes 852000 | tf_op jit(solution)/shard_map/all_to_all | solution.py:663
  25.8 4.9 %all-to-all-start.1 = ((bf16[8,13,32,128]{3,2,1,0:T(8,128)(2,1)}), bf16[8,13,32,128]{3,2,1,0:T(8,128)(2,1)S(1)}, u32[]{:S(2)}, u32[]{:S(2)}) async-start(bf16[8,13,32,128]{3,2,1,0:T(8,128)(2,1)} %shard_map.74), calls=%async_computation.1 | async-start | bytes 1703936 | tf_op jit(solution)/shard_map/all_to_all | solution.py:663
  30.7 0.1 fusion
  30.8 1.3 %collective-permute-start.1 = (bf16[8,7,32,128]{3,2,1,0:T(8,128)(2,1)S(1)}, bf16[8,7,32,128]{3,2,1,0:T(8,128)(2,1)S(1)}, u32[]{:S(2)}, u32[]{:S(2)}) collective-permute-start(bf16[8,7,32,128]{3,2,1,0:T(8,128)(2,1)S(1)} %get-tuple-element.9), channel_id=1, source_target_pairs={{8,0},{16,8},{24,16},{32,24},{40,32},{48,40},{56,48},{64,56},{72,6... | collective-permute-start | bytes 1376264 | tf_op jit(solution)/shard_map/ppermute | solution.py:673
  32.1 3.1 %collective-permute-start = (bf16[8,7,32,128]{3,2,1,0:T(8,128)(2,1)S(1)}, bf16[8,7,32,128]{3,2,1,0:T(8,128)(2,1)S(1)}, u32[]{:S(2)}, u32[]{:S(2)}) collective-permute-start(bf16[8,7,32,128]{3,2,1,0:T(8,128)(2,1)S(1)} %get-tuple-element.10), channel_id=1, source_target_pairs={{0,8},{8,16},{16,24},{24,32},{32,40},{40,48},{48,56},{56,64},{64,7... | collective-permute-start | bytes 1376264 | tf_op jit(solution)/shard_map/ppermute | solution.py:672
  35.2 12.2 %all-to-all-done.1.rest = bf16[8,13,32,128]{3,2,1,0:T(8,128)(2,1)S(1)} async-done(((bf16[8,13,32,128]{3,2,1,0:T(8,128)(2,1)}), bf16[8,13,32,128]{3,2,1,0:T(8,128)(2,1)S(1)}, u32[]{:S(2)}, u32[]{:S(2)}) %all-to-all-start.1) | async-done | bytes 852000 | tf_op jit(solution)/shard_map/all_to_all | solution.py:663
  47.4 3.9 %shard_map.77.inner = f32[3,2,576,128]{3,2,1,0:T(8,128)S(1)} custom-call(bf16[8,13,32,128]{3,2,1,0:T(8,128)(2,1)S(1)} %all-to-all-done.1.rest), custom_call_target="tpu_custom_call" | custom-call | flops 8999999488 | bytes 2000000 | tf_op jit(solution)/shard_map/pallas_call | solution.py:477
  51.3 2.6 %shard_map.76.early = f32[2,2,576,128]{3,2,1,0:T(8,128)S(1)} custom-call(bf16[8,13,32,128]{3,2,1,0:T(8,128)(2,1)S(1)} %all-to-all-done.own), custom_call_target="tpu_custom_call" | custom-call | flops 6000000000 | bytes 2000000 | tf_op jit(solution)/shard_map/pallas_call | solution.py:477
  53.9 0.0 copy-start
  53.9 0.0 copy-start.1
  54.0 0.0 collective-permute-done.above
  54.0 2.6 %shard_map.75.upper = f32[2,2,576,128]{3,2,1,0:T(8,128)S(1)} custom-call(bf16[8,13,32,128]{3,2,1,0:T(8,128)(2,1)S(1)} %all-to-all-done.own, bf16[8,7,32,128]{3,2,1,0:T(8,128)(2,1)S(1)} %collective-permute-done.above), custom_call_target="tpu_custom_call" | custom-call | flops 6000000000 | bytes 2000000 | tf_op jit(solution)/shard_map/pallas_call | solution.py:477
  56.6 0.0 collective-permute-done.1.below
  56.6 0.0 copy-done
  56.6 0.0 copy-done.1
  56.6 10.4 %link_windows.1 = f32[2,6,32,128]{3,2,1,0:T(8,128)} custom-call(bf16[8,13,32,128]{3,2,1,0:T(8,128)(2,1)S(1)} %all-to-all-done.own, bf16[8,13,32,128]{3,2,1,0:T(8,128)(2,1)S(1)} %all-to-all-done.1.rest, bf16[8,7,32,128]{3,2,1,0:T(8,128)(2,1)S(1)} %collective-permute-done.above, bf16[8,7,32,128]{3,2,1,0:T(8,128)(2,1)S(1)} %collective-permute-done.1.below, ...), custom_call_target="tpu_custom_call" | custom-call | flops 20000000000 | bytes 8000000 | tf_op jit(solution)/shard_map/link_windows/pallas_call | solution.py:641
Async XLA Ops:
  8.2 17.6 %all-to-all-start = ((bf16[8,13,32,128]{3,2,1,0:T(8,128)(2,1)}), bf16[8,13,32,128]{3,2,1,0:T(8,128)(2,1)S(1)}, u32[]{:S(2)}, u32[]{:S(2)}) async-start(bf16[8,13,32,128]{3,2,1,0:T(8,128)(2,1)} %get-tuple-element.7), calls=%async_computation | async-start | bytes 1703936 | tf_op jit(solution)/shard_map/all_to_all | solution.py:663
  25.8 21.5 %all-to-all-start.1 = ((bf16[8,13,32,128]{3,2,1,0:T(8,128)(2,1)}), bf16[8,13,32,128]{3,2,1,0:T(8,128)(2,1)S(1)}, u32[]{:S(2)}, u32[]{:S(2)}) async-start(bf16[8,13,32,128]{3,2,1,0:T(8,128)(2,1)} %shard_map.74), calls=%async_computation.1 | async-start | bytes 1703936 | tf_op jit(solution)/shard_map/all_to_all | solution.py:663
  30.8 25.8 %collective-permute-start.1 = (bf16[8,7,32,128]{3,2,1,0:T(8,128)(2,1)S(1)}, bf16[8,7,32,128]{3,2,1,0:T(8,128)(2,1)S(1)}, u32[]{:S(2)}, u32[]{:S(2)}) collective-permute-start(bf16[8,7,32,128]{3,2,1,0:T(8,128)(2,1)S(1)} %get-tuple-element.9), channel_id=1, source_target_pairs={{8,0},{16,8},{24,16},{32,24},{40,32},{48,40},{56,48},{64,56},{72,6... | collective-permute-start | bytes 1376264 | tf_op jit(solution)/shard_map/ppermute | solution.py:673
  32.1 21.8 %collective-permute-start = (bf16[8,7,32,128]{3,2,1,0:T(8,128)(2,1)S(1)}, bf16[8,7,32,128]{3,2,1,0:T(8,128)(2,1)S(1)}, u32[]{:S(2)}, u32[]{:S(2)}) collective-permute-start(bf16[8,7,32,128]{3,2,1,0:T(8,128)(2,1)S(1)} %get-tuple-element.10), channel_id=1, source_target_pairs={{0,8},{8,16},{16,24},{24,32},{32,40},{40,48},{48,56},{56,64},{64,7... | collective-permute-start | bytes 1376264 | tf_op jit(solution)/shard_map/ppermute | solution.py:672
  53.9 2.7 %copy-start = (bf16[256,768]{1,0:T(8,128)(2,1)S(1)}, bf16[256,768]{1,0:T(8,128)(2,1)}, u32[]{:S(2)}) copy-start(bf16[256,768]{1,0:T(8,128)(2,1)} %constant.8.clone.band) | copy-start | bytes 1179652
  53.9 2.7 %copy-start.1 = (bf16[256,128]{1,0:T(8,128)(2,1)S(1)}, bf16[256,128]{1,0:T(8,128)(2,1)}, u32[]{:S(2)}) copy-start(bf16[256,128]{1,0:T(8,128)(2,1)} %constant.7.clone.near) | copy-start | bytes 196612

commit v9 on v8

--- a/solution.py
+++ b/solution.py
@@ -542,9 +542,8 @@
             rowsum += [sums[r, c, spot] for r in (0, 1)]
             pairs = [rowsum[r] + rowsum[r + 1] for r in range(8)]
             value = jnp.concatenate([pairs[a] + pairs[a + 2] for a in range(6)], axis=0)
-            high, low = split(value)
             found = jnp.dot(
-                jnp.concatenate([high, low], axis=1), near[...], preferred_element_type=jnp.float32
+                value.astype(jnp.bfloat16), near[...], preferred_element_type=jnp.float32
             )
             for a in range(6):
                 full = found[a * size : (a + 1) * size] + extra[c, spot, a * 128 : a * 128 + 128]
@@ -633,7 +632,7 @@
                 band[row, line * 3 + block, 125 + block :] = 1.0
     both = np.concatenate(list(band), axis=1)
     both = np.concatenate([both, both], axis=0).astype(jnp.bfloat16)
-    return np.concatenate([near, near], axis=0).astype(jnp.bfloat16), both
+    return near.astype(jnp.bfloat16), both
 
 
 def link_windows(own, rest, above, below, upper, early, inner):

time: 67.4 us -> 66.7 us (0.990)
  no operation moved by 1% of the time
where the time goes in v9:
time: 66.7 us; the launch traced here: 66.4 us
  Pallas kernels  34 us (51%)
  waiting for transfers between devices  17.1 us (26%)
  starting transfers between devices  15.1 us (23%)
    all_to_all x2, waiting for transfers between devices, move(): return lax.all_to_all(tiles, 'dr', split_axis=0, concat_axis=0, tiled=True)  17.1 us
    pallas_call x2, Pallas kernels, filter_lines(): pl.pallas_call(kernel, out_shape=(tiles, rest) if blocks == FIRST else ti...  15 us
    all_to_all x2, starting transfers between devices, move(): return lax.all_to_all(tiles, 'dr', split_axis=0, concat_axis=0, tiled=True)  10.7 us
    pallas_call x1, Pallas kernels, link_windows(): pl.pallas_call(link_kernel, out_shape=jax.ShapeDtypeStruct((2, 6, DATES,...  9.79 us
    pallas_call x3, Pallas kernels, own_rows(): pl.pallas_call(kernel, out_shape=jax.ShapeDtypeStruct((count, 2, PAIRS, 1...  9.17 us
    ppermute x1, starting transfers between devices, on_device(): above = lax.ppermute(own[:, 6:13], 'az', down)  3.06 us
  transfers between devices with their start and end apart: 4, of which 2 were waited for; matrix products, arithmetic and copies ran while one was open for 0% of the time, Pallas kernels for 24%

profile of v9, /device:TPU:2, one launch (start us, length us, event | category | flops | bytes accessed | tf_op | source)
XLA Modules:
  0.0 66.4 jit_solution(13813090475135732687)
XLA Ops:
  0.0 8.2 %shard_map.73 = (bf16[8,13,32,128]{3,2,1,0:T(8,128)(2,1)}, bf16[8,4,32,128]{3,2,1,0:T(8,128)(2,1)}) custom-call(bf16[2,4,24,4096]{3,2,1,0:T(8,128)(2,1)} %refs_0_.3, f32[4,4096]{1,0:T(4,128)} %refs_1_.3, s32[24,4096]{1,0:T(8,128)} %refs_2_.3, f32[1152,128]{1,0:T(8,128)} %constant.6.clone.refs_3_), custom_call_target="tpu_custom_call" | custom-call | flops 4000000000 | bytes 2000000 | tf_op jit(solution)/shard_map/pallas_call | solution.py:340
  8.2 5.9 %all-to-all-start = ((bf16[8,13,32,128]{3,2,1,0:T(8,128)(2,1)}), bf16[8,13,32,128]{3,2,1,0:T(8,128)(2,1)S(1)}, u32[]{:S(2)}, u32[]{:S(2)}) async-start(bf16[8,13,32,128]{3,2,1,0:T(8,128)(2,1)} %get-tuple-element.7), calls=%async_computation | async-start | bytes 1703936 | tf_op jit(solution)/shard_map/all_to_all | solution.py:662
  14.1 6.8 %shard_map.74 = bf16[8,13,32,128]{3,2,1,0:T(8,128)(2,1)} custom-call(bf16[2,4,24,4096]{3,2,1,0:T(8,128)(2,1)} %refs_0_.3, f32[4,4096]{1,0:T(4,128)} %refs_1_.3, s32[24,4096]{1,0:T(8,128)} %refs_2_.3, f32[1152,128]{1,0:T(8,128)} %constant.6.clone.refs_3_, bf16[8,4,32,128]{3,2,1,0:T(8,128)(2,1)} %get-tuple-element.8.refs_4_), custom_call_target="tpu_custom_call" | custom-call | flops 2000000000 | bytes 2000000 | tf_op jit(solution)/shard_map/pallas_call | solution.py:340
  20.9 4.9 %all-to-all-done.own = bf16[8,13,32,128]{3,2,1,0:T(8,128)(2,1)S(1)} async-done(((bf16[8,13,32,128]{3,2,1,0:T(8,128)(2,1)}), bf16[8,13,32,128]{3,2,1,0:T(8,128)(2,1)S(1)}, u32[]{:S(2)}, u32[]{:S(2)}) %all-to-all-start) | async-done | bytes 852000 | tf_op jit(solution)/shard_map/all_to_all | solution.py:662
  25.8 4.9 %all-to-all-start.1 = ((bf16[8,13,32,128]{3,2,1,0:T(8,128)(2,1)}), bf16[8,13,32,128]{3,2,1,0:T(8,128)(2,1)S(1)}, u32[]{:S(2)}, u32[]{:S(2)}) async-start(bf16[8,13,32,128]{3,2,1,0:T(8,128)(2,1)} %shard_map.74), calls=%async_computation.1 | async-start | bytes 1703936 | tf_op jit(solution)/shard_map/all_to_all | solution.py:662
  30.7 0.1 fusion
  30.8 1.3 %collective-permute-start.1 = (bf16[8,7,32,128]{3,2,1,0:T(8,128)(2,1)S(1)}, bf16[8,7,32,128]{3,2,1,0:T(8,128)(2,1)S(1)}, u32[]{:S(2)}, u32[]{:S(2)}) collective-permute-start(bf16[8,7,32,128]{3,2,1,0:T(8,128)(2,1)S(1)} %get-tuple-element.9), channel_id=1, source_target_pairs={{8,0},{16,8},{24,16},{32,24},{40,32},{48,40},{56,48},{64,56},{72,6... | collective-permute-start | bytes 1376264 | tf_op jit(solution)/shard_map/ppermute | solution.py:672
  32.1 3.1 %collective-permute-start = (bf16[8,7,32,128]{3,2,1,0:T(8,128)(2,1)S(1)}, bf16[8,7,32,128]{3,2,1,0:T(8,128)(2,1)S(1)}, u32[]{:S(2)}, u32[]{:S(2)}) collective-permute-start(bf16[8,7,32,128]{3,2,1,0:T(8,128)(2,1)S(1)} %get-tuple-element.10), channel_id=1, source_target_pairs={{0,8},{8,16},{16,24},{24,32},{32,40},{40,48},{48,56},{56,64},{64,7... | collective-permute-start | bytes 1376264 | tf_op jit(solution)/shard_map/ppermute | solution.py:671
  35.2 12.2 %all-to-all-done.1.rest = bf16[8,13,32,128]{3,2,1,0:T(8,128)(2,1)S(1)} async-done(((bf16[8,13,32,128]{3,2,1,0:T(8,128)(2,1)}), bf16[8,13,32,128]{3,2,1,0:T(8,128)(2,1)S(1)}, u32[]{:S(2)}, u32[]{:S(2)}) %all-to-all-start.1) | async-done | bytes 852000 | tf_op jit(solution)/shard_map/all_to_all | solution.py:662
  47.4 3.9 %shard_map.77.inner = f32[3,2,576,128]{3,2,1,0:T(8,128)S(1)} custom-call(bf16[8,13,32,128]{3,2,1,0:T(8,128)(2,1)S(1)} %all-to-all-done.1.rest), custom_call_target="tpu_custom_call" | custom-call | flops 8999999488 | bytes 2000000 | tf_op jit(solution)/shard_map/pallas_call | solution.py:477
  51.3 2.6 %shard_map.76.early = f32[2,2,576,128]{3,2,1,0:T(8,128)S(1)} custom-call(bf16[8,13,32,128]{3,2,1,0:T(8,128)(2,1)S(1)} %all-to-all-done.own), custom_call_target="tpu_custom_call" | custom-call | flops 6000000000 | bytes 2000000 | tf_op jit(solution)/shard_map/pallas_call | solution.py:477
  53.9 0.0 copy-start
  53.9 0.0 copy-start.1
  54.0 0.0 collective-permute-done.above
  54.0 2.6 %shard_map.75.upper = f32[2,2,576,128]{3,2,1,0:T(8,128)S(1)} custom-call(bf16[8,13,32,128]{3,2,1,0:T(8,128)(2,1)S(1)} %all-to-all-done.own, bf16[8,7,32,128]{3,2,1,0:T(8,128)(2,1)S(1)} %collective-permute-done.above), custom_call_target="tpu_custom_call" | custom-call | flops 6000000000 | bytes 2000000 | tf_op jit(solution)/shard_map/pallas_call | solution.py:477
  56.6 0.0 collective-permute-done.1.below
  56.6 0.0 copy-done
  56.6 0.0 copy-done.1
  56.6 9.8 %link_windows.1 = f32[2,6,32,128]{3,2,1,0:T(8,128)} custom-call(bf16[8,13,32,128]{3,2,1,0:T(8,128)(2,1)S(1)} %all-to-all-done.own, bf16[8,13,32,128]{3,2,1,0:T(8,128)(2,1)S(1)} %all-to-all-done.1.rest, bf16[8,7,32,128]{3,2,1,0:T(8,128)(2,1)S(1)} %collective-permute-done.above, bf16[8,7,32,128]{3,2,1,0:T(8,128)(2,1)S(1)} %collective-permute-done.1.below, ...), custom_call_target="tpu_custom_call" | custom-call | flops 20000000000 | bytes 8000000 | tf_op jit(solution)/shard_map/link_windows/pallas_call | solution.py:640
Async XLA Ops:
  8.2 17.6 %all-to-all-start = ((bf16[8,13,32,128]{3,2,1,0:T(8,128)(2,1)}), bf16[8,13,32,128]{3,2,1,0:T(8,128)(2,1)S(1)}, u32[]{:S(2)}, u32[]{:S(2)}) async-start(bf16[8,13,32,128]{3,2,1,0:T(8,128)(2,1)} %get-tuple-element.7), calls=%async_computation | async-start | bytes 1703936 | tf_op jit(solution)/shard_map/all_to_all | solution.py:662
  25.8 21.5 %all-to-all-start.1 = ((bf16[8,13,32,128]{3,2,1,0:T(8,128)(2,1)}), bf16[8,13,32,128]{3,2,1,0:T(8,128)(2,1)S(1)}, u32[]{:S(2)}, u32[]{:S(2)}) async-start(bf16[8,13,32,128]{3,2,1,0:T(8,128)(2,1)} %shard_map.74), calls=%async_computation.1 | async-start | bytes 1703936 | tf_op jit(solution)/shard_map/all_to_all | solution.py:662
  30.8 25.8 %collective-permute-start.1 = (bf16[8,7,32,128]{3,2,1,0:T(8,128)(2,1)S(1)}, bf16[8,7,32,128]{3,2,1,0:T(8,128)(2,1)S(1)}, u32[]{:S(2)}, u32[]{:S(2)}) collective-permute-start(bf16[8,7,32,128]{3,2,1,0:T(8,128)(2,1)S(1)} %get-tuple-element.9), channel_id=1, source_target_pairs={{8,0},{16,8},{24,16},{32,24},{40,32},{48,40},{56,48},{64,56},{72,6... | collective-permute-start | bytes 1376264 | tf_op jit(solution)/shard_map/ppermute | solution.py:672
  32.1 21.8 %collective-permute-start = (bf16[8,7,32,128]{3,2,1,0:T(8,128)(2,1)S(1)}, bf16[8,7,32,128]{3,2,1,0:T(8,128)(2,1)S(1)}, u32[]{:S(2)}, u32[]{:S(2)}) collective-permute-start(bf16[8,7,32,128]{3,2,1,0:T(8,128)(2,1)S(1)} %get-tuple-element.10), channel_id=1, source_target_pairs={{0,8},{8,16},{16,24},{24,32},{32,40},{40,48},{48,56},{56,64},{64,7... | collective-permute-start | bytes 1376264 | tf_op jit(solution)/shard_map/ppermute | solution.py:671
  53.9 2.7 %copy-start = (bf16[256,768]{1,0:T(8,128)(2,1)S(1)}, bf16[256,768]{1,0:T(8,128)(2,1)}, u32[]{:S(2)}) copy-start(bf16[256,768]{1,0:T(8,128)(2,1)} %constant.8.clone.band) | copy-start | bytes 1179652
  53.9 2.7 %copy-start.1 = (bf16[128,128]{1,0:T(8,128)(2,1)S(1)}, bf16[128,128]{1,0:T(8,128)(2,1)}, u32[]{:S(2)}) copy-start(bf16[128,128]{1,0:T(8,128)(2,1)} %constant.7.clone.near) | copy-start | bytes 98308
